TPU v7x, 32 devices: a whole 2x2x4 slice. The times are simulated.
32 devices in a mesh: state: 8 (over z, y), tile: 4 (over x, core).
Axes of the slice: x: 2, y: 2, z: 4, core: 2. Of those that a mesh axis runs over, the one named last changes fastest.
Arguments:
- pair_tiles: bfloat16 [8, 4, 64, 64, 128], P('state', 'tile'), may hold values from -60 to 60
- targets: int32 [8, 4, 16, 2, 128], P('state', 'tile'), may hold values from 0 to 63, as said below
- offsets: int32 [8], replicated, may hold values from 0 to 128, as said below
- ln_gain: float32 [128], replicated, may hold values from 0.5 to 1.5
- ln_bias: float32 [128], replicated, may hold values from -3 to 3
- w_query: bfloat16 [128, 128], replicated, may hold values from -0.5 to 0.5
- w_key: bfloat16 [128, 128], replicated, may hold values from -0.5 to 0.5
- w_value: bfloat16 [128, 128], replicated, may hold values from -0.5 to 0.5
- w_pairbias: float32 [128, 4], replicated, may hold values from -25 to 25
- w_gate: bfloat16 [128, 128], replicated, may hold values from -0.5 to 0.5
- gate_bias: float32 [128], replicated, may hold values from -4 to 4
- w_output: bfloat16 [128, 128], replicated, may hold values from -0.5 to 0.5
- out_bias: float32 [128], replicated, may hold values from -3 to 3
- w_distogram: float32 [128, 64], replicated, may hold values from -4 to 4
- dist_bias: float32 [64], replicated, may hold values from -4 to 4
Outputs:
- shared_grad: float32 [4, 4, 16, 2, 128, 128], P(None, 'tile', None, None, 'state')
Inputs may be any that keep to these rules, and one draw needn't show every extreme that they name: `targets`: symmetric: the bin of crop pair (x, y) equals that of (y, x) in every state. `offsets`: each is a multiple of 64; some state starts at 0 and some state at 128.
All inputs are finite; a program needn't handle non-finite values.
Results may differ from a plain program's by a relative error of at most 0.015.
Values may be sent and summed in bfloat16 or wider, within the bound.
No kernel may reach another device: no remote copies, remote signals or barrier semaphores. Data moves between devices by JAX's collectives and lax.ppermute only.
A program may use at most 64 MiB of HBM per device.

v0:
```python
import math

import jax
import jax.numpy as jnp
from jax import lax
from jax.sharding import PartitionSpec as P

C = 128
H = 4
HD = 32
NB = 64
L = 128


def layer_norm(pair_field, ln_gain, ln_bias):
    center = pair_field - jnp.mean(pair_field, axis=-1, keepdims=True)
    inverse = lax.rsqrt(jnp.mean(center * center, axis=-1, keepdims=True) + 1e-05)
    normed = center * inverse
    return (normed * ln_gain + ln_bias, normed, inverse)


def probabilities(queries, key_proj, bias_full):
    scores = jnp.einsum("rjhd,rkhd->rhjk", queries, key_proj, preferred_element_type=jnp.float32)
    scores = scores * (1.0 / math.sqrt(HD)) + bias_full[None]
    row_max = jnp.max(scores, axis=-1, keepdims=True)
    exp_scores = jnp.exp(scores - row_max)
    return exp_scores / jnp.sum(exp_scores, axis=-1, keepdims=True)


def on_device(
    pair_tiles,
    targets,
    offsets,
    ln_gain,
    ln_bias,
    w_query,
    w_key,
    w_value,
    w_pairbias,
    w_gate,
    gate_bias,
    w_output,
    out_bias,
    w_distogram,
    dist_bias,
):
    tile_count = lax.axis_size("tile")
    state_count = lax.axis_size("state")
    tile_side = pair_tiles.shape[2]
    tile_grid = L // tile_side
    row_share = tile_side // tile_count
    rows_here = row_share * tile_grid
    hidden_width = H * HD
    inv_root = 1.0 / math.sqrt(HD)
    block_rows = 2
    groups = rows_here // block_rows

    def split_rows(values_in):
        return values_in.reshape((groups, block_rows) + values_in.shape[1:])

    blocked = pair_tiles[0, 0].reshape(tile_count, row_share, tile_side, C)
    regrouped = lax.all_to_all(blocked, "tile", split_axis=0, concat_axis=2, tiled=True)
    pair_field = regrouped.reshape(rows_here, L, C).astype(jnp.float32)
    normed_out, normed, inverse = layer_norm(pair_field, ln_gain, ln_bias)
    flat_b = normed_out.astype(jnp.bfloat16).reshape(rows_here * L, C)

    def project(weight):
        return (
            jnp.dot(flat_b, weight, preferred_element_type=jnp.float32)
            .astype(jnp.bfloat16)
            .reshape(rows_here, L, H, HD)
        )

    queries = project(w_query)
    key_proj = project(w_key)
    value_proj = project(w_value)
    gate_act = jax.nn.sigmoid(
        jnp.dot(flat_b, w_gate, preferred_element_type=jnp.float32) + gate_bias
    ).reshape(rows_here, L, hidden_width)
    bias_rows = jnp.einsum("rlc,ch->hrl", normed_out, w_pairbias, precision=lax.Precision.HIGHEST)
    gathered = lax.all_gather(bias_rows, "tile", axis=1, tiled=True)
    bias_full = (
        gathered.reshape(H, tile_count, row_share, tile_grid, L)
        .transpose(0, 3, 1, 2, 4)
        .reshape(H, L, L)
    )

    def forward_block(block_args):
        query_blk, key_blk, value_blk = block_args
        weights_b = probabilities(query_blk, key_blk, bias_full).astype(jnp.bfloat16)
        return jnp.einsum(
            "rhjk,rkhd->rjhd", weights_b, value_blk, preferred_element_type=jnp.float32
        )

    attended = lax.map(
        forward_block, (split_rows(queries), split_rows(key_proj), split_rows(value_proj))
    ).reshape(rows_here, L, hidden_width)
    gated_out = (gate_act * attended).astype(jnp.bfloat16)
    updated = (
        pair_field
        + jnp.dot(
            gated_out.reshape(rows_here * L, hidden_width),
            w_output,
            preferred_element_type=jnp.float32,
        ).reshape(rows_here, L, C)
        + out_bias
    )
    outgoing = updated.reshape(row_share, tile_grid, tile_grid, tile_count, row_share * C)
    incoming = lax.all_to_all(
        outgoing.astype(jnp.bfloat16), "tile", split_axis=3, concat_axis=3, tiled=True
    ).astype(outgoing.dtype)
    mirrored = (
        incoming.reshape(row_share, tile_grid, tile_grid, tile_count, row_share, C)
        .transpose(4, 2, 1, 3, 0, 5)
        .reshape(rows_here, L, C)
    )
    logits = (
        jnp.einsum("rlc,cb->rlb", updated + mirrored, w_distogram, precision=lax.Precision.HIGHEST)
        + dist_bias
    )
    row_max = jnp.max(logits, axis=-1, keepdims=True)
    exp_logits = jnp.exp(logits - row_max)
    bin_prob = exp_logits / jnp.sum(exp_logits, axis=-1, keepdims=True)
    target_here = targets.reshape(rows_here, L)
    onehot = (target_here[:, :, None] == jnp.arange(NB, dtype=jnp.int32)[None, None, :]).astype(
        jnp.float32
    )
    logit_grad = 2.0 * (bin_prob - onehot)
    pair_grad = jnp.einsum("rlb,cb->rlc", logit_grad, w_distogram, precision=lax.Precision.HIGHEST)
    out_grad = jnp.einsum(
        "rlc,wc->rlw", pair_grad.astype(jnp.bfloat16), w_output, preferred_element_type=jnp.float32
    )
    att_grad_b = (out_grad * gate_act).astype(jnp.bfloat16).reshape(rows_here, L, H, HD)
    gate_grad = out_grad * attended * gate_act * (1.0 - gate_act)

    def backward_block(bias_sum, block_args):
        query_blk, key_blk, value_blk, grad_blk = block_args
        attn_prob = probabilities(query_blk, key_blk, bias_full)
        weights_b = attn_prob.astype(jnp.bfloat16)
        value_grad = jnp.einsum(
            "rhjk,rjhd->rkhd", weights_b, grad_blk, preferred_element_type=jnp.float32
        )
        weight_grad = jnp.einsum(
            "rjhd,rkhd->rhjk", grad_blk, value_blk, preferred_element_type=jnp.float32
        )
        score_grad = attn_prob * (
            weight_grad - jnp.sum(attn_prob * weight_grad, axis=-1, keepdims=True)
        )
        score_b = score_grad.astype(jnp.bfloat16)
        query_grad = (
            jnp.einsum("rhjk,rkhd->rjhd", score_b, key_blk, preferred_element_type=jnp.float32)
            * inv_root
        )
        key_grad = (
            jnp.einsum("rhjk,rjhd->rkhd", score_b, query_blk, preferred_element_type=jnp.float32)
            * inv_root
        )
        return (bias_sum + jnp.sum(score_grad, axis=0), (query_grad, key_grad, value_grad))

    bias_grad, grad_parts = lax.scan(
        backward_block,
        jnp.zeros((H, L, L), jnp.float32),
        (split_rows(queries), split_rows(key_proj), split_rows(value_proj), split_rows(att_grad_b)),
    )
    query_grad, key_grad, value_grad = grad_parts
    owner_order = (
        bias_grad.reshape(H, tile_grid, tile_count, row_share, L)
        .transpose(0, 2, 3, 1, 4)
        .reshape(H, L, L)
    )
    bias_share = lax.psum_scatter(
        owner_order.astype(jnp.bfloat16), "tile", scatter_dimension=1, tiled=True
    ).astype(jnp.float32)

    def back_project(grad_part, weight):
        return jnp.einsum(
            "rlw,cw->rlc",
            grad_part.reshape(rows_here, L, hidden_width).astype(jnp.bfloat16),
            weight,
            preferred_element_type=jnp.float32,
        )

    normed_grad = (
        back_project(query_grad, w_query)
        + back_project(key_grad, w_key)
        + back_project(value_grad, w_value)
        + back_project(gate_grad, w_gate)
    )
    normed_grad = normed_grad + jnp.einsum(
        "hrl,ch->rlc", bias_share, w_pairbias, precision=lax.Precision.HIGHEST
    )
    scaled = normed_grad * ln_gain
    ln_back = inverse * (
        scaled
        - jnp.mean(scaled, axis=-1, keepdims=True)
        - normed * jnp.mean(scaled * normed, axis=-1, keepdims=True)
    )
    total_grad = (pair_grad + ln_back).astype(jnp.bfloat16)
    state_here = lax.axis_index("state")
    piece_cols = L // state_count
    shifted = jnp.roll(total_grad, offsets[state_here], axis=1)
    outgoing_rows = shifted.reshape(rows_here, state_count, piece_cols, C)
    received = lax.all_to_all(outgoing_rows, "state", split_axis=1, concat_axis=1, tiled=True)
    placed = (
        received.astype(jnp.float32)
        .reshape(row_share, tile_grid, state_count, piece_cols, C)
        .transpose(2, 1, 0, 3, 4)
    )
    columns = state_here * piece_cols + jnp.arange(piece_cols, dtype=jnp.int32)
    full_blocks = 2 * tile_grid

    def place(source, accum):
        offset = offsets[source]
        high_half = (columns < offset).astype(jnp.float32)[:, None]
        incoming_blk = lax.dynamic_index_in_dim(placed, source, 0, keepdims=False)
        contrib = jnp.stack([incoming_blk * (1.0 - high_half), incoming_blk * high_half], axis=2)
        row_start = offset // tile_side
        zero_index = jnp.zeros((), jnp.int32)
        corner = (row_start, zero_index, zero_index, zero_index, zero_index)
        window = lax.dynamic_slice(accum, corner, contrib.shape)
        return lax.dynamic_update_slice(accum, window + contrib, corner)

    accum = lax.fori_loop(
        0, state_count, place, jnp.zeros((full_blocks, row_share, 2, piece_cols, C), jnp.float32)
    )
    return accum.reshape(full_blocks, 1, row_share, 2, piece_cols, C)


def solution(mesh):
    in_specs = (
        P("state", "tile", None, None, None),
        P("state", "tile", None, None, None),
        P(),
        P(),
        P(),
        P(),
        P(),
        P(),
        P(),
        P(),
        P(),
        P(),
        P(),
        P(),
        P(),
    )
    out_specs = P(None, "tile", None, None, "state", None)
    return jax.shard_map(
        on_device, mesh=mesh, in_specs=in_specs, out_specs=out_specs, check_vma=False
    )
```

profile of v0, /device:TPU:0, one launch (start us, length us, event | category | flops | bytes accessed | tf_op | source)
XLA Modules:
  0.0 457.8 jit_solution(5351371893127979779)
XLA Ops:
  6.5 4.4 all-to-all-start
  10.9 14.4 %all-to-all-done = bf16[4,16,64,128]{3,2,1,0:T(8,128)(2,1)S(1)} async-done(((bf16[4,16,64,128]{3,2,1,0:T(8,128)(2,1)}), bf16[4,16,64,128]{3,2,1,0:T(8,128)(2,1)S(1)}, u32[]{:S(2)}, u32[]{:S(2)}) %all-to-all-start) | async-done | bytes 1048608 | tf_op jit(solution)/shard_map/all_to_all | solution.py:62
  28.0 3.2 fusion.100
  31.2 5.8 %all_gather.3 = f32[4,128,128]{2,0,1:T(4,128)S(1)} all-gather(f32[4,32,128]{2,0,1:T(4,128)S(1)} %fusion.100), channel_id=1, replica_groups=mesh['state'=8,'tile'=4] {'tile'}, dimensions={1}, use_global_device_ids=true | all-gather | bytes 327680 | tf_op jit(solution)/shard_map/all_gather | solution.py:81
  41.0 2.7 reshape_reshape.15
  43.7 2.6 copy.165
  47.7 2.3 copy.162
  50.0 2.6 reshape_reshape.16
  52.6 2.7 copy.166
  59.6 2.6 copy.167
  62.2 68.6 %while.46 = (s32[]{:T(128)}, f32[16,2,128,4,32]{2,4,3,1,0:T(8,128)}, bf16[16,2,128,4,32]{2,4,3,1,0:T(8,128)(2,1)}, bf16[16,2,128,4,32]{2,4,3,1,0:T(8,128)(2,1)},...) while((s32[]{:T(128)}, f32[16,2,128,4,32]{2,4,3,1,0:T(8,128)}, ...), condition=%wide.region_5.6_spmd.clone, body=%wide.region_2.5_spmd.sunk.clone | while | flops 26346752 | bytes 3091525 | solution.py:95
  130.8 4.5 copy.168
  135.3 3.9 reshape.172
  139.3 3.0 copy.169
  142.3 3.7 multiply_convert_fusion.2
  148.9 2.8 copy.170
  151.7 3.5 all-to-all-start.1
  161.9 2.9 copy.173
  164.8 4.8 %all-to-all-done.1 = bf16[16,2,2,4,2048]{4,0,2,1,3:T(8,128)(2,1)S(1)} async-done(((bf16[16,2,2,4,2048]{4,0,2,1,3:T(8,128)(2,1)}), bf16[16,2,2,4,2048]{4,0,2,1,3:T(8,128)(2,1)S(1)}, u32[]{:S(2)}, u32[]{:S(2)}) %all-to-all-start.1) | async-done | bytes 1048608 | tf_op jit(solution)/shard_map/all_to_all | solution.py:109
  171.8 2.4 fusion.97
  175.7 3.5 fusion.108
  179.2 2.3 multiply_convert_fusion.1
  181.5 155.2 %while.48 = (s32[]{:T(128)}, f32[4,128,128]{1,2,0:T(8,128)}, bf16[16,2,128,4,32]{2,4,3,1,0:T(8,128)(2,1)}, bf16[16,2,128,4,32]{2,4,3,1,0:T(8,128)(2,1)}, bf16[16...) while((s32[]{:T(128)}, f32[4,128,128]{1,2,0:T(8,128)}, ...), condition=%wide.region_13.14_spmd.clone.clone, body=%wide.region_8.13_spmd.clone.sunk.clone | while | flops 52691200 | bytes 6518895 | solution.py:160
  188.3 2.0 fusion.244
  198.1 2.0 fusion.244
  207.8 2.0 fusion.244
  217.6 2.0 fusion.244
  227.3 2.0 fusion.244
  237.1 2.0 fusion.244
  246.8 2.0 fusion.244
  256.6 2.0 fusion.244
  266.4 2.0 fusion.244
  276.1 2.0 fusion.244
  285.9 2.0 fusion.244
  295.6 2.0 fusion.244
  305.4 2.0 fusion.244
  315.2 2.1 fusion.244
  324.9 2.0 fusion.244
  334.7 2.0 fusion.244
  336.7 3.1 fusion.122
  339.9 1.8 fusion.124
  342.8 4.8 %fusion.103 = f32[32,128,128]{2,1,0:T(8,128)} fusion(f32[32,128,128]{1,2,0:T(8,128)} %copy.173, f32[32,128,128]{1,2,0:T(8,128)} %get-tuple-element.441, f32[32,128,128]{1,2,0:T(8,128)} %bitcast.299, bf16[128,128]{1,0:T(8,128)(2,1)S(1)} %copy-done.19), kind=kOutput, calls=%fused_computation.110 | convolution fusion | flops 136839168 | bytes 8421376 | tf_op jit(solution)/shard_map/rlw,cw->rlc/dot_general | solution.py:176
  349.3 26.4 %all-reduce.3.cloned.1.call-done = bf16[4,128,128]{2,0,1:T(4,128)(2,1)} async-done(((bf16[4,128,128]{2,0,1:T(4,128)(2,1)}), bf16[4,128,128]{2,0,1:T(4,128)(2,1)}) %all-reduce.3.cloned.1.call-update) | async-done | bytes 131088
  375.7 5.9 %fusion.137 = (f32[32,128]{1,0:T(8,128)S(1)}, f32[32,128]{1,0:T(8,128)S(1)}, f32[32,128,128]{2,1,0:T(8,128)S(1)}) fusion(f32[32,128]{1,0:T(8,128)S(1)} %rsqrt.17, f32[32,128,128]{2,1,0:T(8,128)S(1)} %bitcast.290, f32[32,128]{1,0:T(8,128)S(1)} %div.57, f32[128]{0:T(128)S(1)} %copy-done.21, f32[128,4]{0,1:T(4,128)S(1)} %copy-done.20, ...), kind=kOutput, calls=%fused_computation.151 | convolution fusion | flops 30400512 | bytes 12683780 | tf_op jit(solution)/shard_map/hrl,ch->rlc/dot_general | solution.py:189
  381.6 2.5 add_convert_fusion
  386.0 5.5 %all-to-all-start.2 = ((bf16[32,8,16,128]{3,2,0,1:T(8,128)(2,1)}), bf16[32,8,16,128]{3,2,0,1:T(8,128)(2,1)S(1)}, u32[]{:S(2)}, u32[]{:S(2)}) async-start(bf16[32,8,16,128]{3,2,0,1:T(8,128)(2,1)} %copy.191), calls=%async_computation.2 | async-start | bytes 2097152 | tf_op jit(solution)/shard_map/all_to_all | solution.py:203
  391.6 24.9 %all-to-all-done.2 = bf16[32,8,16,128]{3,2,0,1:T(8,128)(2,1)S(1)} async-done(((bf16[32,8,16,128]{3,2,0,1:T(8,128)(2,1)}), bf16[32,8,16,128]{3,2,0,1:T(8,128)(2,1)S(1)}, u32[]{:S(2)}, u32[]{:S(2)}) %all-to-all-start.2) | async-done | bytes 1048608 | tf_op jit(solution)/shard_map/all_to_all | solution.py:203
  417.2 32.8 %while.47 = (s32[]{:T(128)}, f32[4,16,2,16,128]{4,3,2,1,0:T(8,128)S(1)}, s32[8]{0:T(128)S(1)}, f32[8,2,16,16,128]{4,3,0,1,2:T(8,128)S(1)}, s32[]{:T(128)}) while((s32[]{:T(128)}, f32[4,16,2,16,128]{4,3,2,1,0:T(8,128)S(1)}, s32[8]{0:T(128)S(1)}, f32[8,2,16,16,128]{4,3,0,1,2:T(8,128)S(1)}, s32[]{:T(128)}) %tuple.139), condition=%wide.region_18.19_spmd.clone.clone, body=%wide.region_17.18_spmd.clone.sunk.clone | while | flops 393300 | bytes 2360721 | solution.py:223
  (308 shorter events, 231.7 us)
Async XLA Ops:
  6.5 139.5 %copy-start = (bf16[128,128]{1,0:T(8,128)(2,1)S(1)}, bf16[128,128]{1,0:T(8,128)(2,1)}, u32[]{:S(2)}) copy-start(bf16[128,128]{1,0:T(8,128)(2,1)} %param.32) | copy-start | bytes 98308
  6.5 18.8 %all-to-all-start = ((bf16[4,16,64,128]{3,2,1,0:T(8,128)(2,1)}), bf16[4,16,64,128]{3,2,1,0:T(8,128)(2,1)S(1)}, u32[]{:S(2)}, u32[]{:S(2)}) async-start(bf16[4,16,64,128]{3,2,1,0:T(8,128)(2,1)} %bitcast.308), calls=%async_computation | async-start | bytes 2097152 | tf_op jit(solution)/shard_map/all_to_all | solution.py:62
  26.1 1.9 copy-start.20
  26.1 1.9 copy-start.21
  26.1 1.9 copy-start.22
  28.0 11.3 %copy-start.14 = (bf16[128,128]{1,0:T(8,128)(2,1)S(1)}, bf16[128,128]{1,0:T(8,128)(2,1)}, u32[]{:S(2)}) copy-start(bf16[128,128]{1,0:T(8,128)(2,1)} %param.28) | copy-start | bytes 98308
  38.3 1.0 copy-start.5
  41.0 5.3 %copy-start.6 = (bf16[4096,128]{1,0:T(8,128)(2,1)S(1)}, bf16[4096,128]{1,0:T(8,128)(2,1)}, u32[]{:S(2)}) copy-start(bf16[4096,128]{1,0:T(8,128)(2,1)} %copy-done.5) | copy-start | bytes 3145732
  41.0 5.3 %copy-start.16 = (bf16[128,128]{1,0:T(8,128)(2,1)S(1)}, bf16[128,128]{1,0:T(8,128)(2,1)}, u32[]{:S(2)}) copy-start(bf16[128,128]{1,0:T(8,128)(2,1)} %param.26) | copy-start | bytes 98308
  50.0 5.2 %copy-start.15 = (bf16[128,128]{1,0:T(8,128)(2,1)S(1)}, bf16[128,128]{1,0:T(8,128)(2,1)}, u32[]{:S(2)}) copy-start(bf16[128,128]{1,0:T(8,128)(2,1)} %param.27) | copy-start | bytes 98308
  139.3 3.0 copy-start.7
  139.3 3.0 copy-start.26
  142.3 3.7 copy-start.23
  151.7 17.9 %all-to-all-start.1 = ((bf16[16,2,2,4,2048]{4,0,2,1,3:T(8,128)(2,1)}), bf16[16,2,2,4,2048]{4,0,2,1,3:T(8,128)(2,1)S(1)}, u32[]{:S(2)}, u32[]{:S(2)}) async-start(bf16[16,2,2,4,2048]{4,0,2,1,3:T(8,128)(2,1)} %copy.170), calls=%async_computation.1 | async-start | bytes 2097152 | tf_op jit(solution)/shard_map/all_to_all | solution.py:109
  155.2 220.5 %all-reduce.3.cloned.1.call-start = ((), (), s32[]{:S(2)}) async-start(), calls=%async_computation.3 | async-start | bytes 262144
  155.7 1.3 copy-start.3
  155.7 2.4 copy-start.27
  155.7 4.9 %copy-start.28 = (u32[32]{0:T(128)S(1)}, u32[32]{0:T(128)}, u32[]{:S(2)}) copy-start(u32[32]{0:T(128)} %constant.184) | copy-start | bytes 388
  170.2 1.6 copy-start.12
  170.2 1.6 copy-start.18
  170.3 1.6 copy-start.24
  174.2 1.5 copy-start.25
  175.7 3.5 copy-start.2
  179.2 2.3 copy-start.10
  336.7 3.1 copy-start.13
  339.9 1.8 copy-start.9
  339.9 2.9 copy-start.19
  342.7 4.8 %copy-start.4 = (bf16[16,2,128,4,32]{2,4,3,1,0:T(8,128)(2,1)S(1)}, bf16[16,2,128,4,32]{2,4,3,1,0:T(8,128)(2,1)}, u32[]{:S(2)}) copy-start(bf16[16,2,128,4,32]{2,4,3,1,0:T(8,128)(2,1)} %get-tuple-element.226) | copy-start | bytes 3145732
  342.7 4.8 %copy-start.17 = (bf16[128,128]{1,0:T(8,128)(2,1)S(1)}, bf16[128,128]{1,0:T(8,128)(2,1)}, u32[]{:S(2)}) copy-start(bf16[128,128]{1,0:T(8,128)(2,1)} %param.26) | copy-start | bytes 98308
  375.7 5.9 %copy-start.11 = (f32[32,128,128]{2,1,0:T(8,128)S(1)}, f32[32,128,128]{2,1,0:T(8,128)}, u32[]{:S(2)}) copy-start(f32[32,128,128]{2,1,0:T(8,128)} %copy-done.10) | copy-start | bytes 6291460
  386.0 30.4 %all-to-all-start.2 = ((bf16[32,8,16,128]{3,2,0,1:T(8,128)(2,1)}), bf16[32,8,16,128]{3,2,0,1:T(8,128)(2,1)S(1)}, u32[]{:S(2)}, u32[]{:S(2)}) async-start(bf16[32,8,16,128]{3,2,0,1:T(8,128)(2,1)} %copy.191), calls=%async_computation.2 | async-start | bytes 2097152 | tf_op jit(solution)/shard_map/all_to_all | solution.py:203
  450.0 1.0 copy-start.8
  450.0 1.0 copy-start.1
Sparse Core Ops, SparseCore 0:
  342.8 32.8 all-reduce.2
where the time goes:
time: 466 us; the launch traced here: 458 us
  matrix products  229 us (49%)
  waiting for transfers between devices  70.6 us (15%)
  local copies, waits for them, and re-layouts  57.3 us (12%)
  other arithmetic  43.7 us (9%)
  loops' own time  21.7 us (5%)
  between operations  16.4 us (4%)
  starting transfers between devices  13.6 us (3%)
  blocking collectives  5.78 us (1%)
    sub x32, matrix products, probabilities(): exp_scores = jnp.exp(scores - row_max)  40.1 us
    dot_general x16, matrix products, backward_block(): jnp.einsum('rhjk,rjhd->rkhd', weights_b, grad_blk, preferred_element_type...  32.6 us
    dot_general x16, matrix products, forward_block(): jnp.einsum('rhjk,rkhd->rjhd', weights_b, value_blk, preferred_element_typ...  27.8 us
    dot_general x16, matrix products, backward_block(): jnp.einsum('rhjk,rjhd->rkhd', score_b, query_blk, preferred_element_type=...  27.3 us
    unnamed x2, waiting for transfers between devices  26.4 us
    dot_general x16, matrix products, backward_block(): jnp.einsum('rhjk,rkhd->rjhd', score_b, key_blk, preferred_element_type=jn...  26.4 us
    add x16, other arithmetic, backward_block(): bias_sum + jnp.sum(score_grad, axis=0)  25.9 us
    all_to_all x1, waiting for transfers between devices, on_device(): lax.all_to_all(outgoing_rows, 'state', split_axis=1, concat_axis=1, tiled...  24.9 us
  transfers between devices with their start and end apart: 4, of which 4 were waited for; matrix products, arithmetic and copies ran while one was open for 3% of the time, Pallas kernels for 0%

commit v1 on v0

v1 whole, which is shorter than its diff:
```python
import functools
import math

import jax
import jax.numpy as jnp
from jax import lax
from jax.experimental import pallas as pl
from jax.experimental.pallas import tpu as pltpu
from jax.sharding import PartitionSpec as P

H = 4
HD = 32
NB = 64
EPS = 1e-5
LOG2E = 1.0 / math.log(2.0)
BF = jnp.bfloat16
F32 = jnp.float32
HIGHEST = lax.Precision.HIGHEST


def nn(left, right, **kw):
    return lax.dot_general(left, right, (((1,), (0,)), ((), ())), preferred_element_type=F32, **kw)


def nt(left, right, **kw):
    return lax.dot_general(left, right, (((1,), (1,)), ((), ())), preferred_element_type=F32, **kw)


def split(value):
    high = value.astype(BF)
    low = (value - high.astype(F32)).astype(BF)
    return high, low


def transposed(value):
    return value.astype(F32).T.astype(value.dtype)


def column(row, lanes):
    return jnp.broadcast_to(row, (lanes, row.shape[1])).T


def eye(size):
    rows = lax.broadcasted_iota(jnp.int32, (size, size), 0)
    cols = lax.broadcasted_iota(jnp.int32, (size, size), 1)
    return jnp.where(rows == cols, 1.0, 0.0).astype(BF)


def rows_norm(pair_rows):
    mean = jnp.mean(pair_rows, axis=-1, keepdims=True)
    center = pair_rows - mean
    inverse = lax.rsqrt(jnp.mean(center * center, axis=-1, keepdims=True) + EPS)
    return center * inverse


def full(shape):
    return pl.BlockSpec(shape, lambda *_: (0,) * len(shape))


def prep_kernel(wq, wk, wv, wg, wo, gb, ob, wd, db, wpb, lng, w4t, w3, wod, wdt, wd3, wqg, wkv, gbc, lgc, cst, wgc):
    wide = gbc.shape[1]
    w4t[...] = jnp.concatenate([transposed(w[...]) for w in (wq, wk, wv, wg)], axis=0)
    w3[...] = jnp.concatenate([wq[...], wk[...], wv[...]], axis=1)
    wqg[...] = jnp.concatenate([wq[...], wg[...]], axis=1)
    wkv[...] = jnp.concatenate([wk[...], wv[...]], axis=1)
    dist = wd[...]
    dist_hi, dist_lo = split(dist)
    wd3[...] = jnp.concatenate([dist_hi, dist_hi, dist_lo], axis=1)
    dist_t = dist.T
    wdt[...] = jnp.concatenate(split(dist_t), axis=0)
    both = nn(wo[...].astype(F32), dist, precision=HIGHEST)
    wod[...] = jnp.concatenate(split(both.T), axis=0)
    gbc[...] = column(gb[...], wide)
    lgc[...] = column(lng[...], wide)
    shift = 2.0 * jnp.sum(dist_t * ob[...], axis=1, keepdims=True)
    cst[...] = column(db[...], wide) + shift
    gain = column(lng[...], wide)
    proj = wpb[...]
    for h in range(H):
        wgc[h] = jnp.broadcast_to(proj[:, h : h + 1], gain.shape) * gain


def bias_kernel(tile, targets, lng, lnb, wpb, out, *, per_head):
    step = pl.program_id(0)
    fold, lines, side, chans = tile.shape
    pieces = [tile[f, q] for q in range(lines) for f in range(fold)]
    normed = rows_norm(jnp.concatenate(pieces, axis=0).astype(F32)) * lng[...] + lnb[...]
    proj = jnp.concatenate([wpb[...].T, jnp.zeros((8 - H, chans), F32)], axis=0)
    bias = nt(proj, normed, precision=HIGHEST)
    width = fold * side
    for q in range(lines):
        for h in range(H):
            out[pl.ds(h * per_head + step * lines + q, 1), :] = bias[
                h : h + 1, q * width : (q + 1) * width
            ]

    @pl.when(step == 0)
    def _():
        count = targets.shape[0]
        out[pl.ds(H * per_head, count), :] = targets[...].astype(F32)


def project_kernel(*refs, parts):
    here = lax.axis_index("tile")
    part_refs = refs[:parts]
    lng, lnb, w4t, w3, gbc, zr, qt, kt, vt, qn, kn, vn, gt = refs[parts:]
    own = lax.rem(here, parts)
    rows, side, _ = part_refs[0].shape
    width = H * HD
    for row in range(rows):
        for k in range(parts):
            block = lax.rem(own + parts - k, parts)
            zr[row, pl.ds(pl.multiple_of(block * side, side), side), :] = part_refs[k][row]
    for row in range(rows):
        flat = (rows_norm(zr[row].astype(F32)) * lng[...] + lnb[...]).astype(BF)
        up = nt(w4t[...], flat)
        qt[row] = up[:width].astype(BF)
        kt[row] = up[width : 2 * width].astype(BF)
        vt[row] = up[2 * width : 3 * width].astype(BF)
        gt[row] = jax.nn.sigmoid(up[3 * width :] + gbc[...])
        flatp = nn(flat, w3[...])
        qn[row] = flatp[:, :width].astype(BF)
        kn[row] = flatp[:, width : 2 * width].astype(BF)
        vn[row] = flatp[:, 2 * width :].astype(BF)


def head_blocks(packed):
    rows, lanes = packed.shape
    blocks = []
    for h in range(H):
        pieces = []
        if h:
            pieces.append(jnp.zeros((h * HD, lanes), packed.dtype))
        pieces.append(packed[h * HD : (h + 1) * HD])
        if h < H - 1:
            pieces.append(jnp.zeros((rows - (h + 1) * HD, lanes), packed.dtype))
        blocks.append(jnp.concatenate(pieces, axis=0))
    return jnp.concatenate(blocks, axis=1)


def head_rows(packed):
    lane = lax.broadcasted_iota(jnp.int32, packed.shape, 1) // HD
    zero = jnp.zeros_like(packed)
    return jnp.concatenate([jnp.where(lane == h, packed, zero) for h in range(H)], axis=0)


def forward_kernel(gath, kn, qt, vt, gt, zr, wod, wdt, at, ot, ut, snd, bias_t, stage, *, grid_side, groups, group_rows):
    step = pl.program_id(0)
    rows = kn.shape[0]
    wide = kn.shape[1]
    side = wide // grid_side
    per_head = side * side // wide
    count = snd.shape[2]
    share = snd.shape[1]

    @pl.when(step == 0)
    def _():
        lane = lax.broadcasted_iota(jnp.int32, (per_head, wide), 1) // side
        for h in range(H):
            pieces = []
            for i in range(grid_side):
                for f in range(grid_side):
                    total = None
                    for j in range(grid_side):
                        part = gath[i * grid_side + j, h * per_head : (h + 1) * per_head, :]
                        turn = ((j - f) * side) % wide
                        if turn:
                            part = pltpu.roll(part, turn, 1)
                        total = part if total is None else jnp.where(lane == j, part, total)
                    pieces.append(total)
            bias_t[h] = jnp.concatenate(pieces, axis=0).T * LOG2E

    scale = LOG2E / math.sqrt(HD)
    for row in range(rows):
        scores = nn(kn[row], head_blocks(qt[row]))
        outs = []
        for h in range(H):
            part = scores[:, h * wide : (h + 1) * wide] * scale + bias_t[h]
            part = jnp.exp2(part - jnp.max(part, axis=0, keepdims=True))
            part = part * (1.0 / jnp.sum(part, axis=0, keepdims=True))
            part_b = part.astype(BF)
            at[row, :, h * wide : (h + 1) * wide] = part_b
            outs.append(nn(vt[row, h * HD : (h + 1) * HD, :], part_b))
        attended = jnp.concatenate(outs, axis=0)
        ot[row] = attended
        gated = (gt[row] * attended).astype(BF)
        both = nn(wod[...], gated) + nt(wdt[...], zr[row])
        mine = both[:NB] + both[NB:]
        ut[row] = mine
        high = mine.astype(BF).astype(F32)
        packed = jnp.concatenate([high, mine - high], axis=0).T
        here = step * rows + row
        for i in range(grid_side):
            for p in range(groups):
                for j in range(grid_side):
                    source = ((i * groups + p) * grid_side + j) * group_rows
                    target = ((i * grid_side + j) * share + p * group_rows) * count
                    stage[pl.ds(target + here, group_rows, stride=count), :] = packed[
                        source : source + group_rows
                    ]

    @pl.when(step == pl.num_programs(0) - 1)
    def _():
        for e in range(snd.shape[0]):
            for r in range(share):
                snd[e, r] = stage[(e * share + r) * count : (e * share + r + 1) * count, :].astype(BF)


def backward_kernel(
    gath, rcv, at, ot, ut, gt, vn, kt, qn, zr, wo, wd3, wqg, wkv, lgc, cst, dzm, dbo, acc,
    *, grid_side, groups, group_rows, owner_rows, bias_rows
):
    step = pl.program_id(0)
    rows = vn.shape[0]
    wide = vn.shape[1]
    here = lax.axis_index("tile")
    tile_i = here // grid_side
    tile_j = lax.rem(here, grid_side)
    group_span = wide // grid_side // groups
    inv_root = 1.0 / math.sqrt(HD)
    ident = eye(wide)
    adder = jnp.concatenate([ident[:NB, :NB], ident[:NB, :NB]], axis=1)
    bins = lax.broadcasted_iota(jnp.int32, (NB, wide), 0).astype(F32)

    @pl.when(step == 0)
    def _():
        acc[...] = jnp.zeros_like(acc)

    db_parts = [None] * H
    for row in range(rows):
        local = step * rows + row
        within = (local // group_rows) * group_span + tile_j * group_rows + lax.rem(local, group_rows)
        target = gath[
            within // owner_rows,
            pl.ds(bias_rows + lax.rem(within, owner_rows) * grid_side + tile_i, 1),
            :,
        ]
        mirror = [rcv[e, row].astype(F32) for e in range(rcv.shape[0])]
        pieces = []
        for i in range(grid_side):
            for p in range(groups):
                for j in range(grid_side):
                    pieces.append(
                        mirror[i * grid_side + j][p * group_rows : (p + 1) * group_rows]
                    )
        other = nt(adder, jnp.concatenate(pieces, axis=0).astype(BF))
        logits = ut[row] + other + cst[...]
        probs = jnp.exp(logits - jnp.max(logits, axis=0, keepdims=True))
        probs = probs * (1.0 / jnp.sum(probs, axis=0, keepdims=True))
        resid = 2.0 * (probs - jnp.where(bins == target, 1.0, 0.0))
        res_hi, res_lo = split(resid)
        pair_grad = nn(wd3[...], jnp.concatenate([res_hi, res_lo, res_hi], axis=0))
        out_grad = nn(wo[...], pair_grad.astype(BF))
        gate = gt[row]
        gated = out_grad * gate
        gate_grad = (gated * ot[row] * (1.0 - gate)).astype(BF)
        grad_t = gated.astype(BF)
        grad_n = gated.T.astype(BF)
        weight_grad = nn(vn[row], head_blocks(grad_t))
        score_parts = []
        query_parts = []
        for h in range(H):
            prob = at[row, :, h * wide : (h + 1) * wide].astype(F32)
            prod = weight_grad[:, h * wide : (h + 1) * wide]
            prod = prob * (prod - jnp.sum(prob * prod, axis=0, keepdims=True))
            db_parts[h] = prod if db_parts[h] is None else db_parts[h] + prod
            prod_b = prod.astype(BF)
            score_parts.append(prod_b)
            query_parts.append(nn(kt[row, h * HD : (h + 1) * HD, :], prod_b))
        query_grad = (jnp.concatenate(query_parts, axis=0) * inv_root).astype(BF)
        key_grad = nn(jnp.concatenate(score_parts, axis=1), head_rows(qn[row])) * inv_root
        value_grad = nn(at[row], head_rows(grad_n))
        normed_grad = nn(wqg[...], jnp.concatenate([query_grad, gate_grad], axis=0)) + nt(
            wkv[...], jnp.concatenate([key_grad.astype(BF), value_grad.astype(BF)], axis=1)
        )
        pair_t = nt(ident, zr[row])
        center = pair_t - jnp.mean(pair_t, axis=0, keepdims=True)
        inverse = lax.rsqrt(jnp.mean(center * center, axis=0, keepdims=True) + EPS)
        normed = center * inverse
        scaled = normed_grad * lgc[...]
        back = (
            scaled
            - jnp.mean(scaled, axis=0, keepdims=True)
            - normed * jnp.mean(scaled * normed, axis=0, keepdims=True)
        )
        dzm[row] = pair_grad + inverse * back
    for h in range(H):
        acc[h] += db_parts[h]

    @pl.when(step == pl.num_programs(0) - 1)
    def _():
        for h in range(H):
            grad = acc[h].T
            for i in range(grid_side):
                for j in range(grid_side):
                    pieces = []
                    for p in range(groups):
                        source = ((i * groups + p) * grid_side + j) * group_rows
                        pieces.append(grad[source : source + group_rows])
                    dbo[i * grid_side + j, h] = jnp.concatenate(pieces, axis=0).astype(BF)


def finish_kernel(offsets, rdb, dzm, zr, wgc, out, sums):
    step = pl.program_id(0)
    rows, chans, wide = dzm.shape
    states, _, piece, _ = out.shape
    total_rows = rdb.shape[2]
    turn = offsets[lax.axis_index("state")] // piece

    @pl.when(step == 0)
    def _():
        for h in range(H):
            total = rdb[0, h].astype(F32)
            for e in range(1, rdb.shape[0]):
                total = total + rdb[e, h].astype(F32)
            sums[pl.ds(h * total_rows, total_rows), :] = total

    ident = eye(chans)
    for row in range(rows):
        local = step * rows + row
        scaled = None
        for h in range(H):
            term = wgc[h] * sums[pl.ds(h * total_rows + local, 1), :]
            scaled = term if scaled is None else scaled + term
        pair_t = nt(ident, zr[row])
        center = pair_t - jnp.mean(pair_t, axis=0, keepdims=True)
        inverse = lax.rsqrt(jnp.mean(center * center, axis=0, keepdims=True) + EPS)
        normed = center * inverse
        back = (
            scaled
            - jnp.mean(scaled, axis=0, keepdims=True)
            - normed * jnp.mean(scaled * normed, axis=0, keepdims=True)
        )
        total = (dzm[row] + inverse * back).T.astype(BF)
        for c in range(wide // piece):
            out[lax.rem(turn + c, states), row] = total[c * piece : (c + 1) * piece]


def place_kernel(offsets, rcv, out, *, side):
    states, grid_side, rows, piece, chans = rcv.shape
    start = lax.axis_index("state") * piece
    out[...] = jnp.zeros_like(out)
    for s in range(states):
        offset = offsets[s]
        half = (start < offset).astype(jnp.int32)
        base = offset // side
        for i in range(grid_side):
            out[base + i, :, half] += rcv[s, i].astype(F32)


def on_device(
    pair_tiles,
    targets,
    offsets,
    ln_gain,
    ln_bias,
    w_query,
    w_key,
    w_value,
    w_pairbias,
    w_gate,
    gate_bias,
    w_output,
    out_bias,
    w_distogram,
    dist_bias,
):
    tiles = lax.axis_size("tile")
    states = lax.axis_size("state")
    side, chans = pair_tiles.shape[3], pair_tiles.shape[4]
    wide = targets.shape[4]
    grid_side = wide // side
    owner_rows = side // tiles
    width = H * HD
    here = lax.axis_index("tile")
    tile_i = here // grid_side
    tile_j = lax.rem(here, grid_side)
    even = owner_rows % grid_side == 0
    groups = tiles if even else 1
    group_rows = side // groups // grid_side
    share = groups * group_rows
    per_head = side * side // wide
    piece = wide // states

    def shapes(*pairs):
        return [jax.ShapeDtypeStruct(s, t) for s, t in pairs]

    tile = pair_tiles.reshape(groups, grid_side, group_rows, side, chans)

    def rows_of(j):
        return lax.dynamic_index_in_dim(tile, j, 1, keepdims=False).reshape(share, side, chans)

    parts = [rows_of(tile_j)]
    for k in range(1, grid_side):
        perm = [
            (i * grid_side + j, i * grid_side + (j + k) % grid_side)
            for i in range(grid_side)
            for j in range(grid_side)
        ]
        parts.append(lax.ppermute(rows_of(lax.rem(tile_j + k, grid_side)), "tile", perm))

    gain_row = ln_gain.reshape(1, chans)
    shift_row = ln_bias.reshape(1, chans)
    prep_shapes = shapes(
        ((4 * width, chans), BF),
        ((chans, 3 * width), BF),
        ((2 * NB, width), BF),
        ((2 * NB, chans), BF),
        ((chans, 3 * NB), BF),
        ((chans, 2 * width), BF),
        ((chans, 2 * width), BF),
        ((width, wide), F32),
        ((chans, wide), F32),
        ((NB, wide), F32),
        ((H, chans, wide), F32),
    )
    w4t, w3, wod, wdt, wd3, wqg, wkv, gbc, lgc, cst, wgc = pl.pallas_call(
        prep_kernel, out_shape=prep_shapes, name="prep"
    )(
        w_query,
        w_key,
        w_value,
        w_gate,
        w_output,
        gate_bias.reshape(1, width),
        out_bias.reshape(1, chans),
        w_distogram,
        dist_bias.reshape(1, NB),
        w_pairbias,
        gain_row,
    )

    lines = 8
    bias_rows = H * per_head
    target_rows = owner_rows * grid_side
    bias_mine = pl.pallas_call(
        functools.partial(bias_kernel, per_head=per_head),
        grid=(per_head // lines,),
        in_specs=[
            pl.BlockSpec((grid_side, lines, side, chans), lambda g: (0, g, 0, 0)),
            full((target_rows, wide)),
            full((1, chans)),
            full((1, chans)),
            full((chans, H)),
        ],
        out_specs=full((bias_rows + target_rows, wide)),
        out_shape=jax.ShapeDtypeStruct((bias_rows + target_rows, wide), F32),
        name="bias",
    )(
        pair_tiles.reshape(grid_side, per_head, side, chans),
        targets.reshape(target_rows, wide),
        gain_row,
        shift_row,
        w_pairbias,
    )
    gathered = lax.all_gather(bias_mine, "tile", axis=0, tiled=False)

    block = 4 if share % 4 == 0 else 1

    def by_row(*shape, rows=block):
        return pl.BlockSpec((rows,) + shape, lambda g: (g,) + (0,) * len(shape))

    square_b = ((share, wide, width), BF)
    zr, qt, kt, vt, qn, kn, vn, gt = pl.pallas_call(
        functools.partial(project_kernel, parts=grid_side),
        grid=(share // block,),
        in_specs=[by_row(side, chans)] * grid_side
        + [full((1, chans)), full((1, chans)), full(w4t.shape), full(w3.shape), full(gbc.shape)],
        out_specs=[by_row(wide, width)] * 8,
        out_shape=shapes(*([square_b] * 7), ((share, width, wide), F32)),
        name="project",
    )(*parts, gain_row, shift_row, w4t, w3, gbc)

    block = 2
    layout = dict(grid_side=grid_side, groups=groups, group_rows=group_rows)
    at, ot, ut, snd = pl.pallas_call(
        functools.partial(forward_kernel, **layout),
        grid=(share // block,),
        in_specs=[full(gathered.shape)]
        + [by_row(wide, width, rows=block)] * 5
        + [full(wod.shape), full(wdt.shape)],
        out_specs=[
            by_row(wide, H * wide, rows=block),
            by_row(width, wide, rows=block),
            by_row(NB, wide, rows=block),
            full((tiles, share, share, 2 * NB)),
        ],
        out_shape=shapes(
            ((share, wide, H * wide), BF),
            ((share, width, wide), F32),
            ((share, NB, wide), F32),
            ((tiles, share, share, 2 * NB), BF),
        ),
        scratch_shapes=[
            pltpu.VMEM((H, wide, wide), F32),
            pltpu.VMEM((tiles * share * share, 2 * NB), F32),
        ],
        name="forward",
    )(gathered, kn, qt, vt, gt, zr, wod, wdt)

    mirrored = lax.all_to_all(snd, "tile", split_axis=0, concat_axis=0, tiled=True)

    dzm, dbo = pl.pallas_call(
        functools.partial(
            backward_kernel, owner_rows=owner_rows, bias_rows=bias_rows, **layout
        ),
        grid=(share // block,),
        in_specs=[
            full(gathered.shape),
            pl.BlockSpec((tiles, block, share, 2 * NB), lambda g: (0, g, 0, 0)),
            by_row(wide, H * wide, rows=block),
            by_row(width, wide, rows=block),
            by_row(NB, wide, rows=block),
        ]
        + [by_row(wide, width, rows=block)] * 5
        + [full(w.shape) for w in (w_output, wd3, wqg, wkv, lgc, cst)],
        out_specs=[by_row(chans, wide, rows=block), full((tiles, H, share, wide))],
        out_shape=shapes(((share, chans, wide), F32), ((tiles, H, share, wide), BF)),
        scratch_shapes=[pltpu.VMEM((H, wide, wide), F32)],
        name="backward",
    )(gathered, mirrored, at, ot, ut, gt, vn, kt, qn, zr, w_output, wd3, wqg, wkv, lgc, cst)

    rdb = lax.all_to_all(dbo, "tile", split_axis=0, concat_axis=0, tiled=True)

    block = 4 if share % 4 == 0 else 1
    outgoing = pl.pallas_call(
        finish_kernel,
        grid_spec=pltpu.PrefetchScalarGridSpec(
            num_scalar_prefetch=1,
            grid=(share // block,),
            in_specs=[
                full(rdb.shape),
                pl.BlockSpec((block, chans, wide), lambda g, _: (g, 0, 0)),
                pl.BlockSpec((block, wide, chans), lambda g, _: (g, 0, 0)),
                full(wgc.shape),
            ],
            out_specs=pl.BlockSpec((states, block, piece, chans), lambda g, _: (0, g, 0, 0)),
            scratch_shapes=[pltpu.VMEM((H * share, wide), F32)],
        ),
        out_shape=jax.ShapeDtypeStruct((states, share, piece, chans), BF),
        name="finish",
    )(offsets, rdb, dzm, zr, wgc)

    if even:
        slots = outgoing.reshape(states * tiles, group_rows, piece, chans)
    else:
        slots = lax.dynamic_update_slice(
            jnp.zeros((states, tiles, owner_rows, piece, chans), BF),
            outgoing.reshape(states, grid_side, owner_rows, piece, chans),
            (0, tile_j * grid_side, 0, 0, 0),
        ).reshape(states * tiles, owner_rows, piece, chans)
    received = lax.all_to_all(slots, ("state", "tile"), split_axis=0, concat_axis=0, tiled=True)
    if even:
        received = received.reshape(states, grid_side, owner_rows, piece, chans)
    else:
        received = lax.dynamic_index_in_dim(
            received.reshape(states, grid_side, grid_side, owner_rows, piece, chans),
            tile_i,
            2,
            keepdims=False,
        )

    block = 4 if owner_rows % 4 == 0 else 1
    out_shape = (2 * grid_side, owner_rows, 2, piece, chans)
    placed = pl.pallas_call(
        functools.partial(place_kernel, side=side),
        grid_spec=pltpu.PrefetchScalarGridSpec(
            num_scalar_prefetch=1,
            grid=(owner_rows // block,),
            in_specs=[
                pl.BlockSpec(
                    (states, grid_side, block, piece, chans), lambda g, _: (0, 0, g, 0, 0)
                )
            ],
            out_specs=pl.BlockSpec(
                (2 * grid_side, block, 2, piece, chans), lambda g, _: (0, g, 0, 0, 0)
            ),
        ),
        out_shape=jax.ShapeDtypeStruct(out_shape, F32),
        name="place",
    )(offsets, received)
    return placed.reshape(2 * grid_side, 1, owner_rows, 2, piece, chans)


def solution(mesh):
    in_specs = (
        P("state", "tile", None, None, None),
        P("state", "tile", None, None, None),
    ) + (P(),) * 13
    out_specs = P(None, "tile", None, None, "state", None)
    return jax.shard_map(
        on_device, mesh=mesh, in_specs=in_specs, out_specs=out_specs, check_vma=False
    )
```

time: 466 us -> 159 us (0.34); the launches traced: 458 us -> 158 us
  matrix products: 229 us -> 0 us
  Pallas kernels: 0 us -> 84.9 us
  waiting for transfers between devices: 70.6 us -> 0.01 us
  blocking collectives: 5.78 us -> 67.9 us
  local copies, waits for them, and re-layouts: 57.3 us -> 4.35 us
  other arithmetic: 43.7 us -> 0 us
  loops' own time: 21.7 us -> 0 us
  between operations: 16.4 us -> 0.02 us
  starting transfers between devices: 13.6 us -> 0.49 us
    dot_general x110 -> x0, matrix products: 189 us -> none  [the longest x16 32.6 us: backward_block(): jnp.einsum('rhjk,rjhd->rkhd', weights_b, grad_blk, preferred_element_type...]
    pallas_call x0 -> x7, Pallas kernels: none -> 84.9 us  [the longest x1 37.1 us: on_device(): pl.pallas_call(functools.partial(backward_kernel, owner_rows=owner_rows,...]
    all_to_all x0 -> x3, blocking collectives: none -> 58.6 us  [the longest x1 31.2 us: on_device(): lax.all_to_all(slots, ('state', 'tile'), split_axis=0, concat_axis=0, til...]
    all_to_all x3 -> x0, waiting for transfers between devices: 44.2 us -> none  [the longest x1 24.9 us: on_device(): lax.all_to_all(outgoing_rows, 'state', split_axis=1, concat_axis=1, tiled...]
    sub x32 -> x0, matrix products: 40.1 us -> none  [probabilities(): exp_scores = jnp.exp(scores - row_max)]
    unnamed x2 -> x0, waiting for transfers between devices: 26.4 us -> none
    add x16 -> x0, other arithmetic: 25.9 us -> none  [backward_block(): bias_sum + jnp.sum(score_grad, axis=0)]
    another operation x3 -> x0, loops' own time: 21.7 us -> none  [the longest x1 21.1 us: on_device(): lax.fori_loop(0, state_count, place, jnp.zeros((full_blocks, row_share, 2...]
  transfers between devices with their start and end apart: 4 -> 1, of which waited for: 4 -> 0; matrix products, arithmetic and copies ran while one was open for 3% -> 1% of each run, Pallas kernels for 0% -> 4%
where the time goes in v1:
time: 159 us; the launch traced here: 158 us
  Pallas kernels  84.9 us (53%)
  blocking collectives  67.9 us (43%)
  local copies, waits for them, and re-layouts  4.35 us (3%)
    pallas_call x1, Pallas kernels, on_device(): pl.pallas_call(functools.partial(backward_kernel, owner_rows=owner_rows,...  37.1 us
    all_to_all x1, blocking collectives, on_device(): lax.all_to_all(slots, ('state', 'tile'), split_axis=0, concat_axis=0, til...  31.2 us
    pallas_call x1, Pallas kernels, on_device(): pl.pallas_call(functools.partial(forward_kernel, **layout), grid=(share /...  19.6 us
    all_to_all x1, blocking collectives, on_device(): lax.all_to_all(snd, 'tile', split_axis=0, concat_axis=0, tiled=True)  18.8 us
    all_gather x1, blocking collectives, on_device(): gathered = lax.all_gather(bias_mine, 'tile', axis=0, tiled=False)  9.26 us
    pallas_call x1, Pallas kernels, on_device(): pl.pallas_call(functools.partial(project_kernel, parts=grid_side), grid=(...  8.79 us
    all_to_all x1, blocking collectives, on_device(): rdb = lax.all_to_all(dbo, 'tile', split_axis=0, concat_axis=0, tiled=True)  8.63 us
    pallas_call x1, Pallas kernels, on_device(): pl.pallas_call(finish_kernel, grid_spec=pltpu.PrefetchScalarGridSpec(num_...  8.2 us
  transfers between devices with their start and end apart: 1, of which 0 were waited for; matrix products, arithmetic and copies ran while one was open for 1% of the time, Pallas kernels for 4%

profile of v1, /device:TPU:0, one launch (start us, length us, event | category | flops | bytes accessed | tf_op | source)
XLA Modules:
  0.0 157.6 jit_solution(14278102081727300746)
XLA Ops:
  0.0 0.0 copy-start.2
  0.0 0.0 copy-start.1
  0.0 2.1 %constant_dynamic-slice_fusion = (bf16[4,1,8,64,128]{4,3,2,1,0:T(8,128)(2,1)S(1)}, bf16[4,1,8,64,128]{4,3,2,1,0:T(8,128)(2,1)}) fusion(bf16[4,2,8,64,128]{4,3,2,1,0:T(8,128)(2,1)} %bitcast.22, s32[]{:T(128)S(6)} %select_n.8, s32[]{:T(128)S(6)} %select_n.7), kind=kLoop, calls=%fused_computation | loop fusion | bytes 2097160 | tf_op jit(solution)/shard_map/jit(dynamic_index_in_dim)/dynamic_slice | solution.py:391
  2.1 0.5 collective-permute-start
  2.6 0.0 copy-done.2
  2.6 0.7 copy.16.wpb
  3.3 0.0 copy-done.1
  3.4 0.7 copy.19.wd
  4.1 4.8 %bias.1 = f32[160,128]{1,0:T(8,128)} custom-call(bf16[2,32,64,128]{3,2,1,0:T(8,128)(2,1)} %bitcast.23, s32[32,128]{1,0:T(8,128)} %bitcast.28, f32[1,128]{1,0:T(1,128)} %bitcast.29, f32[1,128]{1,0:T(1,128)} %bitcast.32, f32[128,4]{1,0:T(8,128)} %copy.16.wpb), custom_call_target="tpu_custom_call" | custom-call | tf_op jit(solution)/shard_map/bias/pallas_call | solution.py:436
  8.9 2.2 %prep.1 = (bf16[512,128]{1,0:T(8,128)(2,1)}, bf16[128,384]{1,0:T(8,128)(2,1)}, bf16[128,128]{1,0:T(8,128)(2,1)}, bf16[128,128]{1,0:T(8,128)(2,1)}, bf16[128,192]...) custom-call(bf16[128,128]{1,0:T(8,128)(2,1)} %wq.1, ...), custom_call_target="tpu_custom_call" | custom-call | tf_op jit(solution)/shard_map/prep/pallas_call | solution.py:417
  11.1 9.3 %all-gather = f32[640,128]{1,0:T(8,128)} all-gather(f32[160,128]{1,0:T(8,128)} %bias.1), channel_id=2, replica_groups=mesh['state'=8,'tile'=4] {'tile'}, dimensions={0}, use_global_device_ids=true | all-gather | bytes 409600 | tf_op jit(solution)/shard_map/all_gather | solution.py:456
  20.4 0.0 collective-permute-done.refs_1_
  20.4 0.0 copy-start
  20.4 0.8 copy-done
  21.1 8.8 %project.1 = (bf16[32,128,128]{2,1,0:T(8,128)(2,1)}, bf16[32,128,128]{2,1,0:T(8,128)(2,1)}, bf16[32,128,128]{2,1,0:T(8,128)(2,1)}, bf16[32,128,128]{2,1,0:T(8,12...) custom-call(bf16[32,64,128]{2,1,0:T(8,128)(2,1)} %bitcast.26, ...), custom_call_target="tpu_custom_call" | custom-call | tf_op jit(solution)/shard_map/project/pallas_call | solution.py:464
  29.9 19.6 %forward.1 = (bf16[32,128,512]{2,1,0:T(8,128)(2,1)}, f32[32,128,128]{2,1,0:T(8,128)}, f32[32,64,128]{2,1,0:T(8,128)}, bf16[4,32,32,128]{3,2,1,0:T(8,128)(2,1)}) custom-call(f32[4,160,128]{2,1,0:T(8,128)} %bitcast.24, bf16[32,128,128]{2,1,0:T(8,128)(2,1)} %get-tuple-element.33.kn, bf16[32,128,128]{2,1,0:T(8,128)(2,1)} %get-tuple-element.34.qt, ...), custom_call_target="tpu_custom_call" | custom-call | tf_op jit(solution)/shard_map/forward/pallas_call | solution.py:476
  49.5 18.8 %all_to_all.15.rcv = bf16[4,32,32,128]{3,2,1,0:T(8,128)(2,1)} all-to-all(bf16[4,32,32,128]{3,2,1,0:T(8,128)(2,1)} %get-tuple-element.40), channel_id=1, replica_groups=mesh['state'=8,'tile'=4] {'tile'}, dimensions={0} | all-to-all | bytes 2097152 | tf_op jit(solution)/shard_map/all_to_all | solution.py:501
  68.3 37.1 %backward.1 = (f32[32,128,128]{2,1,0:T(8,128)}, bf16[4,4,32,128]{3,2,1,0:T(8,128)(2,1)}) custom-call(f32[4,160,128]{2,1,0:T(8,128)} %bitcast.25, bf16[4,32,32,128]{3,2,1,0:T(8,128)(2,1)} %all_to_all.15.rcv, bf16[32,128,512]{2,1,0:T(8,128)(2,1)} %get-tuple-element.41.at, f32[32,128,128]{2,1,0:T(8,128)} %get-tuple-element.42.ot, ...), custom_call_target="tpu_custom_call" | custom-call | tf_op jit(solution)/shard_map/backward/pallas_call | solution.py:503
  105.4 8.6 %all_to_all.16.rdb = bf16[4,4,32,128]{3,2,1,0:T(8,128)(2,1)} all-to-all(bf16[4,4,32,128]{3,2,1,0:T(8,128)(2,1)} %get-tuple-element.52), channel_id=1, replica_groups=mesh['state'=8,'tile'=4] {'tile'}, dimensions={0} | all-to-all | bytes 262144 | tf_op jit(solution)/shard_map/all_to_all | solution.py:523
  114.0 8.2 %finish.1 = bf16[8,32,16,128]{3,2,1,0:T(8,128)(2,1)} custom-call(s32[8]{0:T(128)} %offsets.3, bf16[4,4,32,128]{3,2,1,0:T(8,128)(2,1)} %all_to_all.16.rdb, f32[32,128,128]{2,1,0:T(8,128)} %get-tuple-element.53.dzm, bf16[32,128,128]{2,1,0:T(8,128)(2,1)} %get-tuple-element.37.zr, f32[4,128,128]{2,1,0:T(8,128)} %get-tuple-element.54.wgc), custom_call_target="tpu_custom_call" | custom-call | tf_op jit(solution)/shard_map/finish/pallas_call | solution.py:526
  122.2 31.2 %all_to_all.17 = bf16[32,8,16,128]{3,2,1,0:T(8,128)(2,1)} all-to-all(bf16[32,8,16,128]{3,2,1,0:T(8,128)(2,1)} %bitcast.20), channel_id=1, replica_groups=mesh['state'=8,'tile'=4] {'state','tile'}, dimensions={0} | all-to-all | bytes 2097152 | tf_op jit(solution)/shard_map/all_to_all | solution.py:552
  153.5 4.2 %place.1 = f32[4,16,2,16,128]{4,3,2,1,0:T(8,128)} custom-call(s32[8]{0:T(128)} %offsets.3, bf16[8,2,16,16,128]{4,3,2,1,0:T(8,128)(2,1)} %bitcast.21), custom_call_target="tpu_custom_call" | custom-call | tf_op jit(solution)/shard_map/place/pallas_call | solution.py:565
Async XLA Ops:
  0.0 2.6 %copy-start.2 = (f32[128,4]{0,1:T(4,128)S(1)}, f32[128,4]{0,1:T(4,128)}, u32[]{:S(2)}) copy-start(f32[128,4]{0,1:T(4,128)} %param.23) | copy-start | bytes 6148
  0.0 3.3 %copy-start.1 = (f32[128,64]{0,1:T(8,128)S(1)}, f32[128,64]{0,1:T(8,128)}, u32[]{:S(2)}) copy-start(f32[128,64]{0,1:T(8,128)} %param.28) | copy-start | bytes 98308
  2.1 18.2 %collective-permute-start = (bf16[32,64,128]{2,1,0:T(8,128)(2,1)S(1)}, bf16[32,64,128]{2,1,0:T(8,128)(2,1)S(1)}, u32[]{:S(2)}, u32[]{:S(2)}) collective-permute-start(bf16[32,64,128]{2,1,0:T(8,128)(2,1)S(1)} %bitcast.27), channel_id=1, source_target_pairs={{0,1},{1,0},{2,3},{3,2},{4,5},{5,4},{6,7},{7,6},{8,9},{9,8},{10,11... | collective-permute-start | bytes 1572872 | tf_op jit(solution)/shard_map/ppermute | solution.py:400
  20.4 0.8 copy-start

commit v2 on v1

--- a/solution.py
+++ b/solution.py
@@ -11,6 +11,14 @@
 H = 4
 HD = 32
 NB = 64
+FWD_ROWS = 8
+BWD_ROWS = 8
+FWD_PACE = (8, 1, 0)
+BWD_PACE = (8, 0, 0)
+PROJ_PACE = (2, 0, 3)
+FIN_PACE = (8, 0, 0)
+PROJ_ROWS = 8
+FIN_ROWS = 8
 EPS = 1e-5
 LOG2E = 1.0 / math.log(2.0)
 BF = jnp.bfloat16
@@ -51,6 +59,20 @@
     center = pair_rows - mean
     inverse = lax.rsqrt(jnp.mean(center * center, axis=-1, keepdims=True) + EPS)
     return center * inverse
+
+
+def interleave(rows, pace):
+    size, inner, outer = pace
+    begin = {row: (r % size) * inner + (r // size) * outer for r, row in enumerate(rows)}
+    tick = 0
+    while begin:
+        for row in list(begin):
+            if begin[row] <= tick:
+                try:
+                    next(row)
+                except StopIteration:
+                    del begin[row]
+        tick += 1
 
 
 def full(shape):
@@ -111,17 +133,25 @@
         for k in range(parts):
             block = lax.rem(own + parts - k, parts)
             zr[row, pl.ds(pl.multiple_of(block * side, side), side), :] = part_refs[k][row]
-    for row in range(rows):
-        flat = (rows_norm(zr[row].astype(F32)) * lng[...] + lnb[...]).astype(BF)
-        up = nt(w4t[...], flat)
-        qt[row] = up[:width].astype(BF)
-        kt[row] = up[width : 2 * width].astype(BF)
-        vt[row] = up[2 * width : 3 * width].astype(BF)
-        gt[row] = jax.nn.sigmoid(up[3 * width :] + gbc[...])
-        flatp = nn(flat, w3[...])
-        qn[row] = flatp[:, :width].astype(BF)
-        kn[row] = flatp[:, width : 2 * width].astype(BF)
-        vn[row] = flatp[:, 2 * width :].astype(BF)
+
+    def one_row(row):
+        pair_row = zr[row].astype(F32)
+        center = pair_row - jnp.mean(pair_row, axis=-1, keepdims=True)
+        yield
+        inverse = lax.rsqrt(jnp.mean(center * center, axis=-1, keepdims=True) + EPS)
+        yield
+        flat = (center * inverse * lng[...] + lnb[...]).astype(BF)
+        yield
+        for k, out in enumerate((qt, kt, vt)):
+            out[row] = nt(w4t[k * width : (k + 1) * width], flat).astype(BF)
+            yield
+        gt[row] = jax.nn.sigmoid(nt(w4t[3 * width :], flat) + gbc[...])
+        yield
+        for k, out in enumerate((qn, kn, vn)):
+            out[row] = nn(flat, w3[:, k * width : (k + 1) * width]).astype(BF)
+            yield
+
+    interleave([one_row(row) for row in range(rows)], PROJ_PACE)
 
 
 def head_blocks(packed):
@@ -171,25 +201,37 @@
             bias_t[h] = jnp.concatenate(pieces, axis=0).T * LOG2E
 
     scale = LOG2E / math.sqrt(HD)
-    for row in range(rows):
-        scores = nn(kn[row], head_blocks(qt[row]))
+
+    def one_row(row):
+        blocks = head_blocks(qt[row])
         outs = []
-        for h in range(H):
-            part = scores[:, h * wide : (h + 1) * wide] * scale + bias_t[h]
-            part = jnp.exp2(part - jnp.max(part, axis=0, keepdims=True))
-            part = part * (1.0 / jnp.sum(part, axis=0, keepdims=True))
-            part_b = part.astype(BF)
-            at[row, :, h * wide : (h + 1) * wide] = part_b
-            outs.append(nn(vt[row, h * HD : (h + 1) * HD, :], part_b))
-        attended = jnp.concatenate(outs, axis=0)
-        ot[row] = attended
-        gated = (gt[row] * attended).astype(BF)
+        for pair in range(0, H, 2):
+            scores = nn(kn[row], blocks[:, pair * wide : (pair + 2) * wide])
+            yield
+            for h in range(pair, pair + 2):
+                part = scores[:, (h - pair) * wide : (h - pair + 1) * wide] * scale + bias_t[h]
+                peak = jnp.max(part, axis=0, keepdims=True)
+                yield
+                part = jnp.exp2(part - peak)
+                total = jnp.sum(part, axis=0, keepdims=True)
+                yield
+                part_b = (part * (1.0 / total)).astype(BF)
+                at[row, :, h * wide : (h + 1) * wide] = part_b
+                yield
+                outs.append(nn(vt[row, h * HD : (h + 1) * HD, :], part_b))
+                ot[row, h * HD : (h + 1) * HD, :] = outs[-1]
+                yield
+        gated = (gt[row] * ot[row]).astype(BF)
+        yield
         both = nn(wod[...], gated) + nt(wdt[...], zr[row])
+        yield
         mine = both[:NB] + both[NB:]
         ut[row] = mine
         high = mine.astype(BF).astype(F32)
+        yield
         packed = jnp.concatenate([high, mine - high], axis=0).T
         here = step * rows + row
+        yield
         for i in range(grid_side):
             for p in range(groups):
                 for j in range(grid_side):
@@ -198,6 +240,9 @@
                     stage[pl.ds(target + here, group_rows, stride=count), :] = packed[
                         source : source + group_rows
                     ]
+                yield
+
+    interleave([one_row(row) for row in range(rows)], FWD_PACE)
 
     @pl.when(step == pl.num_programs(0) - 1)
     def _():
@@ -207,7 +252,7 @@
 
 
 def backward_kernel(
-    gath, rcv, at, ot, ut, gt, vn, kt, qn, zr, wo, wd3, wqg, wkv, lgc, cst, dzm, dbo, acc,
+    gath, rcv, at, ot, ut, gt, vn, kt, qn, zr, wo, wd3, wqg, wkv, lgc, cst, dzm, dbo, acc, grad_s, gate_s, value_s, score_s, query_s,
     *, grid_side, groups, group_rows, owner_rows, bias_rows
 ):
     step = pl.program_id(0)
@@ -226,8 +271,7 @@
     def _():
         acc[...] = jnp.zeros_like(acc)
 
-    db_parts = [None] * H
-    for row in range(rows):
+    def one_row(row):
         local = step * rows + row
         within = (local // group_rows) * group_span + tile_j * group_rows + lax.rem(local, group_rows)
         target = gath[
@@ -244,48 +288,70 @@
                         mirror[i * grid_side + j][p * group_rows : (p + 1) * group_rows]
                     )
         other = nt(adder, jnp.concatenate(pieces, axis=0).astype(BF))
+        yield
         logits = ut[row] + other + cst[...]
-        probs = jnp.exp(logits - jnp.max(logits, axis=0, keepdims=True))
-        probs = probs * (1.0 / jnp.sum(probs, axis=0, keepdims=True))
-        resid = 2.0 * (probs - jnp.where(bins == target, 1.0, 0.0))
+        peak = jnp.max(logits, axis=0, keepdims=True)
+        yield
+        probs = jnp.exp(logits - peak)
+        total = jnp.sum(probs, axis=0, keepdims=True)
+        yield
+        resid = 2.0 * (probs * (1.0 / total) - jnp.where(bins == target, 1.0, 0.0))
         res_hi, res_lo = split(resid)
+        yield
         pair_grad = nn(wd3[...], jnp.concatenate([res_hi, res_lo, res_hi], axis=0))
+        dzm[row] = pair_grad
+        yield
         out_grad = nn(wo[...], pair_grad.astype(BF))
+        yield
         gate = gt[row]
         gated = out_grad * gate
-        gate_grad = (gated * ot[row] * (1.0 - gate)).astype(BF)
-        grad_t = gated.astype(BF)
+        grad_s[row] = gated.astype(BF)
+        yield
+        gate_s[row] = (gated * ot[row] * (1.0 - gate)).astype(BF)
+        yield
         grad_n = gated.T.astype(BF)
-        weight_grad = nn(vn[row], head_blocks(grad_t))
-        score_parts = []
-        query_parts = []
-        for h in range(H):
-            prob = at[row, :, h * wide : (h + 1) * wide].astype(F32)
-            prod = weight_grad[:, h * wide : (h + 1) * wide]
-            prod = prob * (prod - jnp.sum(prob * prod, axis=0, keepdims=True))
-            db_parts[h] = prod if db_parts[h] is None else db_parts[h] + prod
-            prod_b = prod.astype(BF)
-            score_parts.append(prod_b)
-            query_parts.append(nn(kt[row, h * HD : (h + 1) * HD, :], prod_b))
-        query_grad = (jnp.concatenate(query_parts, axis=0) * inv_root).astype(BF)
-        key_grad = nn(jnp.concatenate(score_parts, axis=1), head_rows(qn[row])) * inv_root
-        value_grad = nn(at[row], head_rows(grad_n))
-        normed_grad = nn(wqg[...], jnp.concatenate([query_grad, gate_grad], axis=0)) + nt(
-            wkv[...], jnp.concatenate([key_grad.astype(BF), value_grad.astype(BF)], axis=1)
+        yield
+        value_s[row] = nn(at[row], head_rows(grad_n)).astype(BF)
+        yield
+        blocks = head_blocks(grad_s[row])
+        yield
+        for pair in range(0, H, 2):
+            weight_grad = nn(vn[row], blocks[:, pair * wide : (pair + 2) * wide])
+            yield
+            for h in range(pair, pair + 2):
+                prob = at[row, :, h * wide : (h + 1) * wide].astype(F32)
+                prod = prob * weight_grad[:, (h - pair) * wide : (h - pair + 1) * wide]
+                total = jnp.sum(prod, axis=0, keepdims=True)
+                yield
+                prod = prod - prob * total
+                score_s[row, :, h * wide : (h + 1) * wide] = prod.astype(BF)
+                acc[h] += prod
+                yield
+                query_s[row, h * HD : (h + 1) * HD, :] = (
+                    nn(kt[row, h * HD : (h + 1) * HD, :], score_s[row, :, h * wide : (h + 1) * wide])
+                    * inv_root
+                ).astype(BF)
+                yield
+        key_grad = nn(score_s[row], head_rows(qn[row])) * inv_root
+        yield
+        normed_grad = nn(wqg[...], jnp.concatenate([query_s[row], gate_s[row]], axis=0)) + nt(
+            wkv[...], jnp.concatenate([key_grad.astype(BF), value_s[row]], axis=1)
         )
+        yield
         pair_t = nt(ident, zr[row])
         center = pair_t - jnp.mean(pair_t, axis=0, keepdims=True)
+        yield
         inverse = lax.rsqrt(jnp.mean(center * center, axis=0, keepdims=True) + EPS)
         normed = center * inverse
+        yield
         scaled = normed_grad * lgc[...]
-        back = (
-            scaled
-            - jnp.mean(scaled, axis=0, keepdims=True)
-            - normed * jnp.mean(scaled * normed, axis=0, keepdims=True)
-        )
-        dzm[row] = pair_grad + inverse * back
-    for h in range(H):
-        acc[h] += db_parts[h]
+        mean_a = jnp.mean(scaled, axis=0, keepdims=True)
+        mean_b = jnp.mean(scaled * normed, axis=0, keepdims=True)
+        yield
+        dzm[row] = dzm[row] + inverse * (scaled - mean_a - normed * mean_b)
+        yield
+
+    interleave([one_row(row) for row in range(rows)], BWD_PACE)
 
     @pl.when(step == pl.num_programs(0) - 1)
     def _():
@@ -316,24 +382,32 @@
             sums[pl.ds(h * total_rows, total_rows), :] = total
 
     ident = eye(chans)
-    for row in range(rows):
+
+    def one_row(row):
         local = step * rows + row
+        pair_t = nt(ident, zr[row])
+        yield
+        center = pair_t - jnp.mean(pair_t, axis=0, keepdims=True)
+        yield
+        inverse = lax.rsqrt(jnp.mean(center * center, axis=0, keepdims=True) + EPS)
+        normed = center * inverse
+        yield
         scaled = None
         for h in range(H):
             term = wgc[h] * sums[pl.ds(h * total_rows + local, 1), :]
             scaled = term if scaled is None else scaled + term
-        pair_t = nt(ident, zr[row])
-        center = pair_t - jnp.mean(pair_t, axis=0, keepdims=True)
-        inverse = lax.rsqrt(jnp.mean(center * center, axis=0, keepdims=True) + EPS)
-        normed = center * inverse
-        back = (
-            scaled
-            - jnp.mean(scaled, axis=0, keepdims=True)
-            - normed * jnp.mean(scaled * normed, axis=0, keepdims=True)
-        )
-        total = (dzm[row] + inverse * back).T.astype(BF)
+        yield
+        mean_a = jnp.mean(scaled, axis=0, keepdims=True)
+        mean_b = jnp.mean(scaled * normed, axis=0, keepdims=True)
+        yield
+        total = dzm[row] + inverse * (scaled - mean_a - normed * mean_b)
+        yield
+        total = total.T.astype(BF)
         for c in range(wide // piece):
             out[lax.rem(turn + c, states), row] = total[c * piece : (c + 1) * piece]
+        yield
+
+    interleave([one_row(row) for row in range(rows)], FIN_PACE)
 
 
 def place_kernel(offsets, rcv, out, *, side):
@@ -455,7 +529,7 @@
     )
     gathered = lax.all_gather(bias_mine, "tile", axis=0, tiled=False)
 
-    block = 4 if share % 4 == 0 else 1
+    block = PROJ_ROWS if share % PROJ_ROWS == 0 else 1
 
     def by_row(*shape, rows=block):
         return pl.BlockSpec((rows,) + shape, lambda g: (g,) + (0,) * len(shape))
@@ -471,7 +545,7 @@
         name="project",
     )(*parts, gain_row, shift_row, w4t, w3, gbc)
 
-    block = 2
+    block = FWD_ROWS if share % FWD_ROWS == 0 else 1
     layout = dict(grid_side=grid_side, groups=groups, group_rows=group_rows)
     at, ot, ut, snd = pl.pallas_call(
         functools.partial(forward_kernel, **layout),
@@ -500,6 +574,7 @@
 
     mirrored = lax.all_to_all(snd, "tile", split_axis=0, concat_axis=0, tiled=True)
 
+    block = BWD_ROWS if share % BWD_ROWS == 0 else 1
     dzm, dbo = pl.pallas_call(
         functools.partial(
             backward_kernel, owner_rows=owner_rows, bias_rows=bias_rows, **layout
@@ -516,13 +591,17 @@
         + [full(w.shape) for w in (w_output, wd3, wqg, wkv, lgc, cst)],
         out_specs=[by_row(chans, wide, rows=block), full((tiles, H, share, wide))],
         out_shape=shapes(((share, chans, wide), F32), ((tiles, H, share, wide), BF)),
-        scratch_shapes=[pltpu.VMEM((H, wide, wide), F32)],
+        scratch_shapes=[pltpu.VMEM((H, wide, wide), F32)]
+        + [
+            pltpu.VMEM((block,) + shape, BF)
+            for shape in ((width, wide), (width, wide), (wide, width), (wide, H * wide), (width, wide))
+        ],
         name="backward",
     )(gathered, mirrored, at, ot, ut, gt, vn, kt, qn, zr, w_output, wd3, wqg, wkv, lgc, cst)
 
     rdb = lax.all_to_all(dbo, "tile", split_axis=0, concat_axis=0, tiled=True)
 
-    block = 4 if share % 4 == 0 else 1
+    block = FIN_ROWS if share % FIN_ROWS == 0 else 1
     outgoing = pl.pallas_call(
         finish_kernel,
         grid_spec=pltpu.PrefetchScalarGridSpec(

time: 159 us -> 126 us (0.79)
  Pallas kernels: 84.9 us -> 52.1 us
    pallas_call x1, Pallas kernels: 37.1 us -> 16 us  [on_device(): pl.pallas_call(functools.partial(backward_kernel, owner_rows=owner_rows,...]
    pallas_call x1, Pallas kernels: 19.6 us -> 11 us  [on_device(): pl.pallas_call(functools.partial(forward_kernel, **layout), grid=(share /...]
    pallas_call x1, Pallas kernels: 8.2 us -> 6.09 us  [on_device(): pl.pallas_call(finish_kernel, grid_spec=pltpu.PrefetchScalarGridSpec(num_...]
  transfers between devices with their start and end apart: 1 -> 1, of which waited for: 0 -> 0; matrix products, arithmetic and copies ran while one was open for 1% -> 1% of each run, Pallas kernels for 4% -> 6%
where the time goes in v2:
time: 126 us; the launch traced here: 125 us
  blocking collectives  67.9 us (54%)
  Pallas kernels  52.1 us (41%)
  local copies, waits for them, and re-layouts  4.35 us (3%)
    all_to_all x1, blocking collectives, on_device(): lax.all_to_all(slots, ('state', 'tile'), split_axis=0, concat_axis=0, til...  31.2 us
    all_to_all x1, blocking collectives, on_device(): lax.all_to_all(snd, 'tile', split_axis=0, concat_axis=0, tiled=True)  18.8 us
    pallas_call x1, Pallas kernels, on_device(): pl.pallas_call(functools.partial(backward_kernel, owner_rows=owner_rows,...  16 us
    pallas_call x1, Pallas kernels, on_device(): pl.pallas_call(functools.partial(forward_kernel, **layout), grid=(share /...  11 us
    all_gather x1, blocking collectives, on_device(): gathered = lax.all_gather(bias_mine, 'tile', axis=0, tiled=False)  9.26 us
    all_to_all x1, blocking collectives, on_device(): rdb = lax.all_to_all(dbo, 'tile', split_axis=0, concat_axis=0, tiled=True)  8.63 us
    pallas_call x1, Pallas kernels, on_device(): pl.pallas_call(functools.partial(project_kernel, parts=grid_side), grid=(...  7.83 us
    pallas_call x1, Pallas kernels, on_device(): pl.pallas_call(finish_kernel, grid_spec=pltpu.PrefetchScalarGridSpec(num_...  6.09 us
  transfers between devices with their start and end apart: 1, of which 0 were waited for; matrix products, arithmetic and copies ran while one was open for 1% of the time, Pallas kernels for 6%

profile of v2, /device:TPU:0, one launch (start us, length us, event | category | flops | bytes accessed | tf_op | source)
XLA Modules:
  0.0 124.9 jit_solution(5987621903735549757)
XLA Ops:
  0.0 0.0 copy-start.2
  0.0 0.0 copy-start.1
  0.0 2.1 %constant_dynamic-slice_fusion = (bf16[4,1,8,64,128]{4,3,2,1,0:T(8,128)(2,1)S(1)}, bf16[4,1,8,64,128]{4,3,2,1,0:T(8,128)(2,1)}) fusion(bf16[4,2,8,64,128]{4,3,2,1,0:T(8,128)(2,1)} %bitcast.22, s32[]{:T(128)S(6)} %select_n.8, s32[]{:T(128)S(6)} %select_n.7), kind=kLoop, calls=%fused_computation | loop fusion | bytes 2097160 | tf_op jit(solution)/shard_map/jit(dynamic_index_in_dim)/dynamic_slice | solution.py:465
  2.1 0.5 collective-permute-start
  2.6 0.0 copy-done.2
  2.6 0.7 copy.16.wpb
  3.3 0.0 copy-done.1
  3.4 0.7 copy.19.wd
  4.1 4.8 %bias.1 = f32[160,128]{1,0:T(8,128)} custom-call(bf16[2,32,64,128]{3,2,1,0:T(8,128)(2,1)} %bitcast.23, s32[32,128]{1,0:T(8,128)} %bitcast.28, f32[1,128]{1,0:T(1,128)} %bitcast.29, f32[1,128]{1,0:T(1,128)} %bitcast.32, f32[128,4]{1,0:T(8,128)} %copy.16.wpb), custom_call_target="tpu_custom_call" | custom-call | tf_op jit(solution)/shard_map/bias/pallas_call | solution.py:510
  8.9 2.2 %prep.1 = (bf16[512,128]{1,0:T(8,128)(2,1)}, bf16[128,384]{1,0:T(8,128)(2,1)}, bf16[128,128]{1,0:T(8,128)(2,1)}, bf16[128,128]{1,0:T(8,128)(2,1)}, bf16[128,192]...) custom-call(bf16[128,128]{1,0:T(8,128)(2,1)} %wq.1, ...), custom_call_target="tpu_custom_call" | custom-call | tf_op jit(solution)/shard_map/prep/pallas_call | solution.py:491
  11.1 9.3 %all-gather = f32[640,128]{1,0:T(8,128)} all-gather(f32[160,128]{1,0:T(8,128)} %bias.1), channel_id=2, replica_groups=mesh['state'=8,'tile'=4] {'tile'}, dimensions={0}, use_global_device_ids=true | all-gather | bytes 409600 | tf_op jit(solution)/shard_map/all_gather | solution.py:530
  20.4 0.0 collective-permute-done.refs_1_
  20.4 0.0 copy-start
  20.4 0.8 copy-done
  21.1 7.8 %project.1 = (bf16[32,128,128]{2,1,0:T(8,128)(2,1)}, bf16[32,128,128]{2,1,0:T(8,128)(2,1)}, bf16[32,128,128]{2,1,0:T(8,128)(2,1)}, bf16[32,128,128]{2,1,0:T(8,12...) custom-call(bf16[32,64,128]{2,1,0:T(8,128)(2,1)} %bitcast.26, ...), custom_call_target="tpu_custom_call" | custom-call | tf_op jit(solution)/shard_map/project/pallas_call | solution.py:538
  29.0 11.0 %forward.1 = (bf16[32,128,512]{2,1,0:T(8,128)(2,1)}, f32[32,128,128]{2,1,0:T(8,128)}, f32[32,64,128]{2,1,0:T(8,128)}, bf16[4,32,32,128]{3,2,1,0:T(8,128)(2,1)}) custom-call(f32[4,160,128]{2,1,0:T(8,128)} %bitcast.24, bf16[32,128,128]{2,1,0:T(8,128)(2,1)} %get-tuple-element.33.kn, bf16[32,128,128]{2,1,0:T(8,128)(2,1)} %get-tuple-element.34.qt, ...), custom_call_target="tpu_custom_call" | custom-call | tf_op jit(solution)/shard_map/forward/pallas_call | solution.py:550
  40.0 18.8 %all_to_all.15.rcv = bf16[4,32,32,128]{3,2,1,0:T(8,128)(2,1)} all-to-all(bf16[4,32,32,128]{3,2,1,0:T(8,128)(2,1)} %get-tuple-element.40), channel_id=1, replica_groups=mesh['state'=8,'tile'=4] {'tile'}, dimensions={0} | all-to-all | bytes 2097152 | tf_op jit(solution)/shard_map/all_to_all | solution.py:575
  58.8 16.0 %backward.1 = (f32[32,128,128]{2,1,0:T(8,128)}, bf16[4,4,32,128]{3,2,1,0:T(8,128)(2,1)}) custom-call(f32[4,160,128]{2,1,0:T(8,128)} %bitcast.25, bf16[4,32,32,128]{3,2,1,0:T(8,128)(2,1)} %all_to_all.15.rcv, bf16[32,128,512]{2,1,0:T(8,128)(2,1)} %get-tuple-element.41.at, f32[32,128,128]{2,1,0:T(8,128)} %get-tuple-element.42.ot, ...), custom_call_target="tpu_custom_call" | custom-call | tf_op jit(solution)/shard_map/backward/pallas_call | solution.py:578
  74.8 8.6 %all_to_all.16.rdb = bf16[4,4,32,128]{3,2,1,0:T(8,128)(2,1)} all-to-all(bf16[4,4,32,128]{3,2,1,0:T(8,128)(2,1)} %get-tuple-element.52), channel_id=1, replica_groups=mesh['state'=8,'tile'=4] {'tile'}, dimensions={0} | all-to-all | bytes 262144 | tf_op jit(solution)/shard_map/all_to_all | solution.py:602
  83.4 6.1 %finish.1 = bf16[8,32,16,128]{3,2,1,0:T(8,128)(2,1)} custom-call(s32[8]{0:T(128)} %offsets.3, bf16[4,4,32,128]{3,2,1,0:T(8,128)(2,1)} %all_to_all.16.rdb, f32[32,128,128]{2,1,0:T(8,128)} %get-tuple-element.53.dzm, bf16[32,128,128]{2,1,0:T(8,128)(2,1)} %get-tuple-element.37.zr, f32[4,128,128]{2,1,0:T(8,128)} %get-tuple-element.54.wgc), custom_call_target="tpu_custom_call" | custom-call | tf_op jit(solution)/shard_map/finish/pallas_call | solution.py:605
  89.5 31.2 %all_to_all.17 = bf16[32,8,16,128]{3,2,1,0:T(8,128)(2,1)} all-to-all(bf16[32,8,16,128]{3,2,1,0:T(8,128)(2,1)} %bitcast.20), channel_id=1, replica_groups=mesh['state'=8,'tile'=4] {'state','tile'}, dimensions={0} | all-to-all | bytes 2097152 | tf_op jit(solution)/shard_map/all_to_all | solution.py:631
  120.7 4.2 %place.1 = f32[4,16,2,16,128]{4,3,2,1,0:T(8,128)} custom-call(s32[8]{0:T(128)} %offsets.3, bf16[8,2,16,16,128]{4,3,2,1,0:T(8,128)(2,1)} %bitcast.21), custom_call_target="tpu_custom_call" | custom-call | tf_op jit(solution)/shard_map/place/pallas_call | solution.py:644
Async XLA Ops:
  0.0 2.6 %copy-start.2 = (f32[128,4]{0,1:T(4,128)S(1)}, f32[128,4]{0,1:T(4,128)}, u32[]{:S(2)}) copy-start(f32[128,4]{0,1:T(4,128)} %param.23) | copy-start | bytes 6148
  0.0 3.3 %copy-start.1 = (f32[128,64]{0,1:T(8,128)S(1)}, f32[128,64]{0,1:T(8,128)}, u32[]{:S(2)}) copy-start(f32[128,64]{0,1:T(8,128)} %param.28) | copy-start | bytes 98308
  2.1 18.2 %collective-permute-start = (bf16[32,64,128]{2,1,0:T(8,128)(2,1)S(1)}, bf16[32,64,128]{2,1,0:T(8,128)(2,1)S(1)}, u32[]{:S(2)}, u32[]{:S(2)}) collective-permute-start(bf16[32,64,128]{2,1,0:T(8,128)(2,1)S(1)} %bitcast.27), channel_id=1, source_target_pairs={{0,1},{1,0},{2,3},{3,2},{4,5},{5,4},{6,7},{7,6},{8,9},{9,8},{10,11... | collective-permute-start | bytes 1572872 | tf_op jit(solution)/shard_map/ppermute | solution.py:474
  20.4 0.8 copy-start

commit v3 on v2

--- a/solution.py
+++ b/solution.py
@@ -85,10 +85,10 @@
     w3[...] = jnp.concatenate([wq[...], wk[...], wv[...]], axis=1)
     wqg[...] = jnp.concatenate([wq[...], wg[...]], axis=1)
     wkv[...] = jnp.concatenate([wk[...], wv[...]], axis=1)
-    dist = wd[...]
+    dist_t = wd[...]
+    dist = dist_t.T
     dist_hi, dist_lo = split(dist)
     wd3[...] = jnp.concatenate([dist_hi, dist_hi, dist_lo], axis=1)
-    dist_t = dist.T
     wdt[...] = jnp.concatenate(split(dist_t), axis=0)
     both = nn(wo[...].astype(F32), dist, precision=HIGHEST)
     wod[...] = jnp.concatenate(split(both.T), axis=0)
@@ -97,9 +97,8 @@
     shift = 2.0 * jnp.sum(dist_t * ob[...], axis=1, keepdims=True)
     cst[...] = column(db[...], wide) + shift
     gain = column(lng[...], wide)
-    proj = wpb[...]
     for h in range(H):
-        wgc[h] = jnp.broadcast_to(proj[:, h : h + 1], gain.shape) * gain
+        wgc[h] = column(wpb[h : h + 1], wide) * gain
 
 
 def bias_kernel(tile, targets, lng, lnb, wpb, out, *, per_head):
@@ -107,7 +106,7 @@
     fold, lines, side, chans = tile.shape
     pieces = [tile[f, q] for q in range(lines) for f in range(fold)]
     normed = rows_norm(jnp.concatenate(pieces, axis=0).astype(F32)) * lng[...] + lnb[...]
-    proj = jnp.concatenate([wpb[...].T, jnp.zeros((8 - H, chans), F32)], axis=0)
+    proj = jnp.concatenate([wpb[...], jnp.zeros((8 - H, chans), F32)], axis=0)
     bias = nt(proj, normed, precision=HIGHEST)
     width = fold * side
     for q in range(lines):
@@ -122,11 +121,10 @@
         out[pl.ds(H * per_head, count), :] = targets[...].astype(F32)
 
 
-def project_kernel(*refs, parts):
-    here = lax.axis_index("tile")
+def project_kernel(own_ref, *refs, parts):
+    own = own_ref[0]
     part_refs = refs[:parts]
     lng, lnb, w4t, w3, gbc, zr, qt, kt, vt, qn, kn, vn, gt = refs[parts:]
-    own = lax.rem(here, parts)
     rows, side, _ = part_refs[0].shape
     width = H * HD
     for row in range(rows):
@@ -174,17 +172,29 @@
     return jnp.concatenate([jnp.where(lane == h, packed, zero) for h in range(H)], axis=0)
 
 
-def forward_kernel(gath, kn, qt, vt, gt, zr, wod, wdt, at, ot, ut, snd, bias_t, stage, *, grid_side, groups, group_rows):
+def forward_kernel(
+    *refs, tiles, base, count, bias_rows, owner_rows, extra, grid_side, groups, group_rows
+):
+    gath = refs[:tiles]
+    kn, qt, vt, gt, zr, wod, wdt = refs[tiles : tiles + 7]
+    at, ot, ut, tgt, bias_t = refs[tiles + 7 + extra : tiles + 12 + extra]
+    sends = refs[tiles + 12 + extra : 2 * tiles + 12 + extra]
+    order, stage = refs[2 * tiles + 12 + extra :]
     step = pl.program_id(0)
+    mine = lax.axis_index("tile")
+    tile_i = mine // grid_side
+    tile_j = lax.rem(mine, grid_side)
     rows = kn.shape[0]
     wide = kn.shape[1]
     side = wide // grid_side
     per_head = side * side // wide
-    count = snd.shape[2]
-    share = snd.shape[1]
+    share = groups * group_rows
+    span = side // groups
 
     @pl.when(step == 0)
     def _():
+        for k in range(tiles):
+            order[mine ^ k] = gath[k][...]
         lane = lax.broadcasted_iota(jnp.int32, (per_head, wide), 1) // side
         for h in range(H):
             pieces = []
@@ -192,13 +202,21 @@
                 for f in range(grid_side):
                     total = None
                     for j in range(grid_side):
-                        part = gath[i * grid_side + j, h * per_head : (h + 1) * per_head, :]
+                        part = order[i * grid_side + j, h * per_head : (h + 1) * per_head, :]
                         turn = ((j - f) * side) % wide
                         if turn:
                             part = pltpu.roll(part, turn, 1)
                         total = part if total is None else jnp.where(lane == j, part, total)
                     pieces.append(total)
             bias_t[h] = jnp.concatenate(pieces, axis=0).T * LOG2E
+
+    for row in range(rows):
+        within = (base + step) * span + tile_j * group_rows + row
+        tgt[row : row + 1, :] = order[
+            within // owner_rows,
+            pl.ds(bias_rows + lax.rem(within, owner_rows) * grid_side + tile_i, 1),
+            :,
+        ]
 
     scale = LOG2E / math.sqrt(HD)
 
@@ -225,11 +243,11 @@
         yield
         both = nn(wod[...], gated) + nt(wdt[...], zr[row])
         yield
-        mine = both[:NB] + both[NB:]
-        ut[row] = mine
-        high = mine.astype(BF).astype(F32)
-        yield
-        packed = jnp.concatenate([high, mine - high], axis=0).T
+        logit = both[:NB] + both[NB:]
+        ut[row] = logit
+        high = logit.astype(BF).astype(F32)
+        yield
+        packed = jnp.concatenate([high, logit - high], axis=0).T
         here = step * rows + row
         yield
         for i in range(grid_side):
@@ -246,22 +264,29 @@
 
     @pl.when(step == pl.num_programs(0) - 1)
     def _():
-        for e in range(snd.shape[0]):
+        for k in range(tiles):
+            start = (mine ^ k) * (share * count)
             for r in range(share):
-                snd[e, r] = stage[(e * share + r) * count : (e * share + r + 1) * count, :].astype(BF)
-
-
-def backward_kernel(
-    gath, rcv, at, ot, ut, gt, vn, kt, qn, zr, wo, wd3, wqg, wkv, lgc, cst, dzm, dbo, acc, grad_s, gate_s, value_s, score_s, query_s,
-    *, grid_side, groups, group_rows, owner_rows, bias_rows
-):
+                sends[k][r] = stage[
+                    pl.ds(pl.multiple_of(start + r * count, 8), count), :
+                ].astype(BF)
+
+
+def backward_kernel(*refs, tiles, chunks, grid_side, groups, group_rows):
+    rcv = refs[: tiles * chunks]
+    tgt, at, ot, ut, gt, vn, kt, qn, zr, wo, wd3, wqg, wkv, lgc, cst, dzm = refs[
+        tiles * chunks : tiles * chunks + 16
+    ]
+    sends = refs[tiles * chunks + 16 : tiles * chunks + 16 + tiles]
+    acc, grad_s, gate_s, value_s, score_s, query_s, mirror_s, order = refs[
+        tiles * chunks + 16 + tiles :
+    ]
     step = pl.program_id(0)
+    mine = lax.axis_index("tile")
     rows = vn.shape[0]
     wide = vn.shape[1]
-    here = lax.axis_index("tile")
-    tile_i = here // grid_side
-    tile_j = lax.rem(here, grid_side)
-    group_span = wide // grid_side // groups
+    chunk_groups = groups // chunks
+    share = groups * group_rows
     inv_root = 1.0 / math.sqrt(HD)
     ident = eye(wide)
     adder = jnp.concatenate([ident[:NB, :NB], ident[:NB, :NB]], axis=1)
@@ -272,22 +297,17 @@
         acc[...] = jnp.zeros_like(acc)
 
     def one_row(row):
-        local = step * rows + row
-        within = (local // group_rows) * group_span + tile_j * group_rows + lax.rem(local, group_rows)
-        target = gath[
-            within // owner_rows,
-            pl.ds(bias_rows + lax.rem(within, owner_rows) * grid_side + tile_i, 1),
-            :,
-        ]
-        mirror = [rcv[e, row].astype(F32) for e in range(rcv.shape[0])]
-        pieces = []
-        for i in range(grid_side):
+        for k in range(tiles):
+            source_i = (mine ^ k) // grid_side
+            source_j = lax.rem(mine ^ k, grid_side)
             for p in range(groups):
-                for j in range(grid_side):
-                    pieces.append(
-                        mirror[i * grid_side + j][p * group_rows : (p + 1) * group_rows]
-                    )
-        other = nt(adder, jnp.concatenate(pieces, axis=0).astype(BF))
+                start = ((source_i * groups + p) * grid_side + source_j) * group_rows
+                local = (p % chunk_groups) * group_rows
+                mirror_s[row, pl.ds(pl.multiple_of(start, group_rows), group_rows), :] = rcv[
+                    (p // chunk_groups) * tiles + k
+                ][row, local : local + group_rows].astype(F32)
+        yield
+        other = nt(adder, mirror_s[row].astype(BF))
         yield
         logits = ut[row] + other + cst[...]
         peak = jnp.max(logits, axis=0, keepdims=True)
@@ -295,7 +315,7 @@
         probs = jnp.exp(logits - peak)
         total = jnp.sum(probs, axis=0, keepdims=True)
         yield
-        resid = 2.0 * (probs * (1.0 / total) - jnp.where(bins == target, 1.0, 0.0))
+        resid = 2.0 * (probs * (1.0 / total) - jnp.where(bins == tgt[row : row + 1, :], 1.0, 0.0))
         res_hi, res_lo = split(resid)
         yield
         pair_grad = nn(wd3[...], jnp.concatenate([res_hi, res_lo, res_hi], axis=0))
@@ -363,22 +383,28 @@
                     for p in range(groups):
                         source = ((i * groups + p) * grid_side + j) * group_rows
                         pieces.append(grad[source : source + group_rows])
-                    dbo[i * grid_side + j, h] = jnp.concatenate(pieces, axis=0).astype(BF)
-
-
-def finish_kernel(offsets, rdb, dzm, zr, wgc, out, sums):
+                    order[i * grid_side + j, h * share : (h + 1) * share, :] = jnp.concatenate(
+                        pieces, axis=0
+                    )
+        for k in range(tiles):
+            sends[k][...] = order[mine ^ k].reshape(H, share, wide).astype(BF)
+
+
+def finish_kernel(offsets, *refs, tiles):
+    rdb = refs[:tiles]
+    dzm, zr, wgc, out, sums = refs[tiles:]
     step = pl.program_id(0)
     rows, chans, wide = dzm.shape
     states, _, piece, _ = out.shape
-    total_rows = rdb.shape[2]
+    total_rows = rdb[0].shape[1]
     turn = offsets[lax.axis_index("state")] // piece
 
     @pl.when(step == 0)
     def _():
         for h in range(H):
-            total = rdb[0, h].astype(F32)
-            for e in range(1, rdb.shape[0]):
-                total = total + rdb[e, h].astype(F32)
+            total = rdb[0][h].astype(F32)
+            for part in rdb[1:]:
+                total = total + part[h].astype(F32)
             sums[pl.ds(h * total_rows, total_rows), :] = total
 
     ident = eye(chans)
@@ -464,7 +490,7 @@
     def rows_of(j):
         return lax.dynamic_index_in_dim(tile, j, 1, keepdims=False).reshape(share, side, chans)
 
-    parts = [rows_of(tile_j)]
+    parts = [tile]
     for k in range(1, grid_side):
         perm = [
             (i * grid_side + j, i * grid_side + (j + k) % grid_side)
@@ -498,9 +524,9 @@
         w_output,
         gate_bias.reshape(1, width),
         out_bias.reshape(1, chans),
-        w_distogram,
+        w_distogram.T,
         dist_bias.reshape(1, NB),
-        w_pairbias,
+        w_pairbias.T,
         gain_row,
     )
 
@@ -515,7 +541,7 @@
             full((target_rows, wide)),
             full((1, chans)),
             full((1, chans)),
-            full((chans, H)),
+            full((H, chans)),
         ],
         out_specs=full((bias_rows + target_rows, wide)),
         out_shape=jax.ShapeDtypeStruct((bias_rows + target_rows, wide), F32),
@@ -525,90 +551,135 @@
         targets.reshape(target_rows, wide),
         gain_row,
         shift_row,
-        w_pairbias,
+        w_pairbias.T,
     )
-    gathered = lax.all_gather(bias_mine, "tile", axis=0, tiled=False)
-
-    block = PROJ_ROWS if share % PROJ_ROWS == 0 else 1
-
-    def by_row(*shape, rows=block):
-        return pl.BlockSpec((rows,) + shape, lambda g: (g,) + (0,) * len(shape))
-
+
+    def to_partner(value, k):
+        return lax.ppermute(value, "tile", [(t, t ^ k) for t in range(tiles)]) if k else value
+
+    gathered = [to_partner(bias_mine, k) for k in range(tiles)]
+
+    def by_row(*shape, rows, base=0):
+        return pl.BlockSpec((rows,) + shape, lambda g, *_: (g + base,) + (0,) * len(shape))
+
+    def cost(flops, moved):
+        return pl.CostEstimate(flops=flops, bytes_accessed=moved, transcendentals=0)
+
+    cell = wide * width * wide
     square_b = ((share, wide, width), BF)
     zr, qt, kt, vt, qn, kn, vn, gt = pl.pallas_call(
         functools.partial(project_kernel, parts=grid_side),
+        grid_spec=pltpu.PrefetchScalarGridSpec(
+            num_scalar_prefetch=1,
+            grid=(groups,),
+            in_specs=[
+                pl.BlockSpec(
+                    (None, None, group_rows, side, chans), lambda g, own: (g, own[0], 0, 0, 0)
+                )
+            ]
+            + [by_row(side, chans, rows=group_rows)] * (grid_side - 1)
+            + [full((1, chans)), full((1, chans)), full(w4t.shape), full(w3.shape), full(gbc.shape)],
+            out_specs=[by_row(wide, width, rows=group_rows)] * 8,
+        ),
+        out_shape=shapes(*([square_b] * 7), ((share, width, wide), F32)),
+        cost_estimate=cost(80 * share * cell, 12 * share * wide * width * 2),
+        name="project",
+    )(tile_j.reshape(1), *parts, gain_row, shift_row, w4t, w3, gbc)
+
+    chunks = 2 if groups % 2 == 0 else 1
+    chunk_groups = groups // chunks
+    count = share // chunks
+    block = group_rows
+    layout = dict(grid_side=grid_side, groups=groups, group_rows=group_rows)
+    saved_shapes = shapes(
+        ((share, wide, H * wide), BF),
+        ((share, width, wide), F32),
+        ((share, NB, wide), F32),
+        ((share, wide), F32),
+        ((H, wide, wide), F32),
+    )
+    packed_shape = (share, count, 2 * NB)
+    saved = []
+    mirrored = []
+    for c in range(chunks):
+        base = c * chunk_groups
+        inputs = [*gathered, kn, qt, vt, gt, zr, wod, wdt]
+        first = len(inputs)
+        call = pl.pallas_call(
+            functools.partial(
+                forward_kernel,
+                tiles=tiles,
+                base=base,
+                count=count,
+                bias_rows=bias_rows,
+                owner_rows=owner_rows,
+                extra=len(saved),
+                **layout,
+            ),
+            grid=(count // block,),
+            in_specs=[full(gathered[0].shape)] * tiles
+            + [by_row(wide, width, rows=block, base=base)] * 5
+            + [full(wod.shape), full(wdt.shape)]
+            + [pl.BlockSpec(memory_space=pl.ANY)] * len(saved),
+            out_specs=[
+                by_row(wide, H * wide, rows=block, base=base),
+                by_row(width, wide, rows=block, base=base),
+                by_row(NB, wide, rows=block, base=base),
+                by_row(wide, rows=block, base=base),
+                full((H, wide, wide)),
+            ]
+            + [full(packed_shape)] * tiles,
+            out_shape=saved_shapes + shapes(*([(packed_shape, BF)] * tiles)),
+            scratch_shapes=[
+                pltpu.VMEM((tiles,) + gathered[0].shape, F32),
+                pltpu.VMEM((tiles * share * count, 2 * NB), F32),
+            ],
+            input_output_aliases={first + n: n for n in range(len(saved))},
+            cost_estimate=cost(150 * count * cell, 14 * count * wide * width * 2),
+            name="forward",
+        )
+        results = call(*inputs, *saved)
+        saved = list(results[:4])
+        mirrored.append([to_partner(results[5 + k], k) for k in range(tiles)])
+    at, ot, ut, tgt = saved
+
+    results = pl.pallas_call(
+        functools.partial(backward_kernel, tiles=tiles, chunks=chunks, **layout),
         grid=(share // block,),
-        in_specs=[by_row(side, chans)] * grid_side
-        + [full((1, chans)), full((1, chans)), full(w4t.shape), full(w3.shape), full(gbc.shape)],
-        out_specs=[by_row(wide, width)] * 8,
-        out_shape=shapes(*([square_b] * 7), ((share, width, wide), F32)),
-        name="project",
-    )(*parts, gain_row, shift_row, w4t, w3, gbc)
-
-    block = FWD_ROWS if share % FWD_ROWS == 0 else 1
-    layout = dict(grid_side=grid_side, groups=groups, group_rows=group_rows)
-    at, ot, ut, snd = pl.pallas_call(
-        functools.partial(forward_kernel, **layout),
-        grid=(share // block,),
-        in_specs=[full(gathered.shape)]
-        + [by_row(wide, width, rows=block)] * 5
-        + [full(wod.shape), full(wdt.shape)],
-        out_specs=[
-            by_row(wide, H * wide, rows=block),
-            by_row(width, wide, rows=block),
-            by_row(NB, wide, rows=block),
-            full((tiles, share, share, 2 * NB)),
-        ],
-        out_shape=shapes(
-            ((share, wide, H * wide), BF),
-            ((share, width, wide), F32),
-            ((share, NB, wide), F32),
-            ((tiles, share, share, 2 * NB), BF),
-        ),
-        scratch_shapes=[
-            pltpu.VMEM((H, wide, wide), F32),
-            pltpu.VMEM((tiles * share * share, 2 * NB), F32),
-        ],
-        name="forward",
-    )(gathered, kn, qt, vt, gt, zr, wod, wdt)
-
-    mirrored = lax.all_to_all(snd, "tile", split_axis=0, concat_axis=0, tiled=True)
-
-    block = BWD_ROWS if share % BWD_ROWS == 0 else 1
-    dzm, dbo = pl.pallas_call(
-        functools.partial(
-            backward_kernel, owner_rows=owner_rows, bias_rows=bias_rows, **layout
-        ),
-        grid=(share // block,),
-        in_specs=[
-            full(gathered.shape),
-            pl.BlockSpec((tiles, block, share, 2 * NB), lambda g: (0, g, 0, 0)),
+        in_specs=[by_row(count, 2 * NB, rows=block)] * (tiles * chunks)
+        + [
+            by_row(wide, rows=block),
             by_row(wide, H * wide, rows=block),
             by_row(width, wide, rows=block),
             by_row(NB, wide, rows=block),
         ]
         + [by_row(wide, width, rows=block)] * 5
         + [full(w.shape) for w in (w_output, wd3, wqg, wkv, lgc, cst)],
-        out_specs=[by_row(chans, wide, rows=block), full((tiles, H, share, wide))],
-        out_shape=shapes(((share, chans, wide), F32), ((tiles, H, share, wide), BF)),
+        out_specs=[by_row(chans, wide, rows=block)] + [full((H, share, wide))] * tiles,
+        out_shape=shapes(((share, chans, wide), F32), *([((H, share, wide), BF)] * tiles)),
         scratch_shapes=[pltpu.VMEM((H, wide, wide), F32)]
         + [
             pltpu.VMEM((block,) + shape, BF)
             for shape in ((width, wide), (width, wide), (wide, width), (wide, H * wide), (width, wide))
-        ],
+        ]
+        + [pltpu.VMEM((block, wide, 2 * NB), F32), pltpu.VMEM((tiles, H * share, wide), F32)],
+        cost_estimate=cost(500 * share * cell, 20 * share * wide * width * 2),
         name="backward",
-    )(gathered, mirrored, at, ot, ut, gt, vn, kt, qn, zr, w_output, wd3, wqg, wkv, lgc, cst)
-
-    rdb = lax.all_to_all(dbo, "tile", split_axis=0, concat_axis=0, tiled=True)
+    )(
+        *[part for parts_c in mirrored for part in parts_c],
+        tgt, at, ot, ut, gt, vn, kt, qn, zr, w_output, wd3, wqg, wkv, lgc, cst,
+    )
+    dzm = results[0]
+    rdb = [to_partner(results[1 + k], k) for k in range(tiles)]
 
     block = FIN_ROWS if share % FIN_ROWS == 0 else 1
     outgoing = pl.pallas_call(
-        finish_kernel,
+        functools.partial(finish_kernel, tiles=tiles),
         grid_spec=pltpu.PrefetchScalarGridSpec(
             num_scalar_prefetch=1,
             grid=(share // block,),
             in_specs=[
-                full(rdb.shape),
+                *([full(rdb[0].shape)] * tiles),
                 pl.BlockSpec((block, chans, wide), lambda g, _: (g, 0, 0)),
                 pl.BlockSpec((block, wide, chans), lambda g, _: (g, 0, 0)),
                 full(wgc.shape),
@@ -618,7 +689,7 @@
         ),
         out_shape=jax.ShapeDtypeStruct((states, share, piece, chans), BF),
         name="finish",
-    )(offsets, rdb, dzm, zr, wgc)
+    )(offsets, *rdb, dzm, zr, wgc)
 
     if even:
         slots = outgoing.reshape(states * tiles, group_rows, piece, chans)

time: 126 us -> 111 us (0.88)
  blocking collectives: 67.9 us -> 31.2 us
  waiting for transfers between devices: 0.01 us -> 10 us
  starting transfers between devices: 0.49 us -> 10.1 us
  Pallas kernels: 52.1 us -> 54.7 us
    all_to_all x2 -> x0, blocking collectives: 27.4 us -> none  [the longest x1 18.8 us: on_device(): lax.all_to_all(snd, 'tile', split_axis=0, concat_axis=0, tiled=True)]
    ppermute x0 -> x12, waiting for transfers between devices: none -> 10 us  [to_partner(): lax.ppermute(value, 'tile', [(t, t ^ k) for t in range(tiles)])]
    ppermute x0 -> x12, starting transfers between devices: none -> 9.56 us  [to_partner(): lax.ppermute(value, 'tile', [(t, t ^ k) for t in range(tiles)])]
    all_gather x1 -> x0, blocking collectives: 9.26 us -> none  [on_device(): gathered = lax.all_gather(bias_mine, 'tile', axis=0, tiled=False)]
    pallas_call x4 -> x5, Pallas kernels: 41 us -> 43.6 us  [the longest x1 16.2 us: on_device(): pl.pallas_call(functools.partial(backward_kernel, tiles=tiles, chunks=chu...]
    unnamed x8 -> x26, local copies, waits for them, and re-layouts: 2.23 us -> 2.79 us
  transfers between devices with their start and end apart: 1 -> 13, of which waited for: 0 -> 4; matrix products, arithmetic and copies ran while one was open for 1% -> 0% of each run, Pallas kernels for 6% -> 19%
where the time goes in v3:
time: 111 us; the launch traced here: 110 us
  Pallas kernels  54.7 us (49%)
  blocking collectives  31.2 us (28%)
  starting transfers between devices  10.1 us (9%)
  waiting for transfers between devices  10 us (9%)
  local copies, waits for them, and re-layouts  3.86 us (3%)
    all_to_all x1, blocking collectives, on_device(): lax.all_to_all(slots, ('state', 'tile'), split_axis=0, concat_axis=0, til...  31.2 us
    pallas_call x1, Pallas kernels, on_device(): pl.pallas_call(functools.partial(backward_kernel, tiles=tiles, chunks=chu...  16.2 us
    pallas_call x2, Pallas kernels, on_device(): results = call(*inputs, *saved)  13.4 us
    ppermute x12, waiting for transfers between devices, to_partner(): lax.ppermute(value, 'tile', [(t, t ^ k) for t in range(tiles)])  10 us
    ppermute x12, starting transfers between devices, to_partner(): lax.ppermute(value, 'tile', [(t, t ^ k) for t in range(tiles)])  9.56 us
    pallas_call x1, Pallas kernels, on_device(): pl.pallas_call(functools.partial(project_kernel, parts=grid_side), grid_s...  7.76 us
    pallas_call x1, Pallas kernels, on_device(): pl.pallas_call(functools.partial(finish_kernel, tiles=tiles), grid_spec=p...  6.14 us
    pallas_call x1, Pallas kernels, on_device(): pl.pallas_call(functools.partial(bias_kernel, per_head=per_head), grid=(p...  4.86 us
  transfers between devices with their start and end apart: 13, of which 4 were waited for; matrix products, arithmetic and copies ran while one was open for 0% of the time, Pallas kernels for 19%

profile of v3, /device:TPU:0, one launch (start us, length us, event | category | flops | bytes accessed | tf_op | source)
XLA Modules:
  0.0 110.1 jit_solution(1490424200389726005)
XLA Ops:
  0.0 1.1 constant_dynamic-slice_fusion
  1.1 0.6 collective-permute-start.3
  1.6 4.9 %bias.1.refs_0_ = f32[160,128]{1,0:T(8,128)} custom-call(bf16[2,32,64,128]{3,2,1,0:T(8,128)(2,1)} %bitcast.20, s32[32,128]{1,0:T(8,128)} %bitcast.24, f32[1,128]{1,0:T(1,128)} %bitcast.27, f32[1,128]{1,0:T(1,128)} %bitcast.33, f32[4,128]{1,0:T(4,128)} %bitcast.25), custom_call_target="tpu_custom_call" | custom-call | tf_op jit(solution)/shard_map/bias/pallas_call | solution.py:536
  6.5 2.6 %collective-permute-start.2 = (f32[160,128]{1,0:T(8,128)}, f32[160,128]{1,0:T(8,128)S(1)}, u32[]{:S(2)}, u32[]{:S(2)}) collective-permute-start(f32[160,128]{1,0:T(8,128)} %bias.1.refs_0_), channel_id=1, source_target_pairs={{0,3},{1,2},{2,1},{3,0},{4,7},{5,6},{6,5},{7,4},{8,11},{9,10},{10,... | collective-permute-start | bytes 245768 | tf_op jit(solution)/shard_map/ppermute | solution.py:558
  9.1 0.0 collective-permute-start.1
  9.1 0.1 collective-permute-start
  9.2 2.1 %prep.1 = (bf16[512,128]{1,0:T(8,128)(2,1)}, bf16[128,384]{1,0:T(8,128)(2,1)}, bf16[128,128]{1,0:T(8,128)(2,1)}, bf16[128,128]{1,0:T(8,128)(2,1)}, bf16[128,192]...) custom-call(bf16[128,128]{1,0:T(8,128)(2,1)} %wq.1, ...), custom_call_target="tpu_custom_call" | custom-call | tf_op jit(solution)/shard_map/prep/pallas_call | solution.py:517
  11.3 0.0 collective-permute-done.3.refs_1_
  11.3 0.0 copy-start.3
  11.3 0.9 copy-done.3
  12.2 7.8 %project.1 = (bf16[32,128,128]{2,1,0:T(8,128)(2,1)}, bf16[32,128,128]{2,1,0:T(8,128)(2,1)}, bf16[32,128,128]{2,1,0:T(8,128)(2,1)}, bf16[32,128,128]{2,1,0:T(8,12...) custom-call(s32[1]{0:T(128)} %bitcast.5.own_ref, ...), custom_call_target="tpu_custom_call" | custom-call | flops 5368709120 | bytes 12582912 | tf_op jit(solution)/shard_map/project/pallas_call | solution.py:570
  20.0 0.0 collective-permute-done.2.refs_3_
  20.0 0.0 copy-start.10
  20.0 0.0 collective-permute-done.1.refs_2_
  20.0 0.0 copy-start.11
  20.0 0.0 collective-permute-done.refs_1_
  20.0 0.6 copy-done.10
  20.6 0.0 copy-done.11
  20.6 0.0 copy-done.12
  20.7 6.7 %forward.2 = (bf16[32,128,512]{2,1,0:T(8,128)(2,1)}, f32[32,128,128]{2,1,0:T(8,128)}, f32[32,64,128]{2,1,0:T(8,128)}, f32[32,128]{1,0:T(8,128)}, f32[4,128,128]{...) custom-call(f32[160,128]{1,0:T(8,128)} %bias.1.refs_0_, ...), custom_call_target="tpu_custom_call" | custom-call | flops 5033164800 | bytes 7340032 | tf_op jit(solution)/shard_map/forward/pallas_call | solution.py:641
  27.4 0.4 collective-permute-start.4
  27.8 2.0 %collective-permute-start.5 = (bf16[32,16,128]{2,1,0:T(8,128)(2,1)}, bf16[32,16,128]{2,1,0:T(8,128)(2,1)S(1)}, u32[]{:S(2)}, u32[]{:S(2)}) collective-permute-start(bf16[32,16,128]{2,1,0:T(8,128)(2,1)} %get-tuple-element.57), channel_id=1, source_target_pairs={{0,2},{1,3},{2,0},{3,1},{4,6},{5,7},{6,4},{7,5},{8,10},{9,11},{10,... | collective-permute-start | bytes 393224 | tf_op jit(solution)/shard_map/ppermute | solution.py:558
  29.9 0.0 collective-permute-start.6
  29.9 6.7 %forward.3 = (bf16[32,128,512]{2,1,0:T(8,128)(2,1)}, f32[32,128,128]{2,1,0:T(8,128)}, f32[32,64,128]{2,1,0:T(8,128)}, f32[32,128]{1,0:T(8,128)}, f32[4,128,128]{...) custom-call(f32[160,128]{1,0:T(8,128)} %bias.1.refs_0_, ...), custom_call_target="tpu_custom_call", output_to_operand_aliasing={{0}: (11, {}), {1}: (12, {}), {2}: (13, {}), {3}: (14, {})} | custom-call | flops 5033164800 | bytes 7340032 | tf_op jit(solution)/shard_map/forward/pallas_call | solution.py:641
  36.6 0.2 collective-permute-start.7
  36.8 2.0 %collective-permute-start.8 = (bf16[32,16,128]{2,1,0:T(8,128)(2,1)}, bf16[32,16,128]{2,1,0:T(8,128)(2,1)S(1)}, u32[]{:S(2)}, u32[]{:S(2)}) collective-permute-start(bf16[32,16,128]{2,1,0:T(8,128)(2,1)} %get-tuple-element.65), channel_id=1, source_target_pairs={{0,2},{1,3},{2,0},{3,1},{4,6},{5,7},{6,4},{7,5},{8,10},{9,11},{10,... | collective-permute-start | bytes 393224 | tf_op jit(solution)/shard_map/ppermute | solution.py:558
  38.8 0.0 collective-permute-done.4.refs_1_
  38.8 0.0 collective-permute-start.9
  38.8 0.0 collective-permute-done.5.refs_2_
  38.8 0.0 collective-permute-done.6.refs_3_
  38.8 0.0 copy-start.6
  38.8 0.0 collective-permute-done.7.refs_5_
  38.9 4.5 %collective-permute-done.8.refs_6_ = bf16[32,16,128]{2,1,0:T(8,128)(2,1)S(1)} collective-permute-done((bf16[32,16,128]{2,1,0:T(8,128)(2,1)}, bf16[32,16,128]{2,1,0:T(8,128)(2,1)S(1)}, u32[]{:S(2)}, u32[]{:S(2)}) %collective-permute-start.8) | collective-permute-done | bytes 131104 | tf_op jit(solution)/shard_map/ppermute | solution.py:558
  43.4 1.7 %collective-permute-done.9.refs_7_ = bf16[32,16,128]{2,1,0:T(8,128)(2,1)S(1)} collective-permute-done((bf16[32,16,128]{2,1,0:T(8,128)(2,1)}, bf16[32,16,128]{2,1,0:T(8,128)(2,1)S(1)}, u32[]{:S(2)}, u32[]{:S(2)}) %collective-permute-start.9) | collective-permute-done | bytes 131104 | tf_op jit(solution)/shard_map/ppermute | solution.py:558
  45.0 0.0 copy-done.4
  45.0 0.6 copy-done.9
  45.7 16.2 %backward.1 = (f32[32,128,128]{2,1,0:T(8,128)}, bf16[4,32,128]{2,1,0:T(8,128)(2,1)}, bf16[4,32,128]{2,1,0:T(8,128)(2,1)}, bf16[4,32,128]{2,1,0:T(8,128)(2,1)}, bf16[4,32,128]{2,1,0:T(8,128)(2,1)}) custom-call(bf16[32,16,128]{2,1,0:T(8,128)(2,1)} %get-tuple-element.55.refs_0_, bf16[32,16,128]{2,1,0:T(8,128)(2,1)} %copy-done.4, ...), custom_call_target="tpu_custom_call" | custom-call | flops 33554432000 | bytes 20971520 | tf_op jit(solution)/shard_map/backward/pallas_call | solution.py:646
  61.9 0.5 collective-permute-start.10
  62.4 1.7 %collective-permute-start.11 = (bf16[4,32,128]{2,1,0:T(8,128)(2,1)}, bf16[4,32,128]{2,1,0:T(8,128)(2,1)S(1)}, u32[]{:S(2)}, u32[]{:S(2)}) collective-permute-start(bf16[4,32,128]{2,1,0:T(8,128)(2,1)} %get-tuple-element.81), channel_id=1, source_target_pairs={{0,2},{1,3},{2,0},{3,1},{4,6},{5,7},{6,4},{7,5},{8,10},{9,11},{10,... | collective-permute-start | bytes 98312 | tf_op jit(solution)/shard_map/ppermute | solution.py:558
  64.1 0.0 collective-permute-start.12
  64.1 0.0 collective-permute-done.10.refs_1_
  64.1 2.4 %collective-permute-done.11.refs_2_ = bf16[4,32,128]{2,1,0:T(8,128)(2,1)S(1)} collective-permute-done((bf16[4,32,128]{2,1,0:T(8,128)(2,1)}, bf16[4,32,128]{2,1,0:T(8,128)(2,1)S(1)}, u32[]{:S(2)}, u32[]{:S(2)}) %collective-permute-start.11) | collective-permute-done | bytes 32800 | tf_op jit(solution)/shard_map/ppermute | solution.py:558
  66.5 1.5 %collective-permute-done.12.refs_3_ = bf16[4,32,128]{2,1,0:T(8,128)(2,1)S(1)} collective-permute-done((bf16[4,32,128]{2,1,0:T(8,128)(2,1)}, bf16[4,32,128]{2,1,0:T(8,128)(2,1)S(1)}, u32[]{:S(2)}, u32[]{:S(2)}) %collective-permute-start.12) | collective-permute-done | bytes 32800 | tf_op jit(solution)/shard_map/ppermute | solution.py:558
  67.9 0.0 copy-done
  68.0 0.6 copy-done.2
  68.6 6.1 %finish.1 = bf16[8,32,16,128]{3,2,1,0:T(8,128)(2,1)} custom-call(s32[8]{0:T(128)} %offsets.3, bf16[4,32,128]{2,1,0:T(8,128)(2,1)} %get-tuple-element.79.refs_0_, bf16[4,32,128]{2,1,0:T(8,128)(2,1)} %copy-done, bf16[4,32,128]{2,1,0:T(8,128)(2,1)} %copy-done.1, bf16[4,32,128]{2,1,0:T(8,128)(2,1)} %copy-done.2, f32[32,128,128]{2,1,0:T(8,128)} %get-tuple-element.83.refs_4_, ...), custom_call_target="tpu_custom_call" | custom-call | tf_op jit(solution)/shard_map/finish/pallas_call | solution.py:676
  74.7 31.2 %all_to_all.5 = bf16[32,8,16,128]{3,2,1,0:T(8,128)(2,1)} all-to-all(bf16[32,8,16,128]{3,2,1,0:T(8,128)(2,1)} %bitcast.17), channel_id=1, replica_groups=mesh['state'=8,'tile'=4] {'state','tile'}, dimensions={0} | all-to-all | bytes 2097152 | tf_op jit(solution)/shard_map/all_to_all | solution.py:702
  105.9 4.2 %place.1 = f32[4,16,2,16,128]{4,3,2,1,0:T(8,128)} custom-call(s32[8]{0:T(128)} %offsets.3, bf16[8,2,16,16,128]{4,3,2,1,0:T(8,128)(2,1)} %bitcast.18), custom_call_target="tpu_custom_call" | custom-call | tf_op jit(solution)/shard_map/place/pallas_call | solution.py:715
  (14 shorter events, 0.0 us)
Async XLA Ops:
  1.1 10.2 %collective-permute-start.3 = (bf16[32,64,128]{2,1,0:T(8,128)(2,1)S(1)}, bf16[32,64,128]{2,1,0:T(8,128)(2,1)S(1)}, u32[]{:S(2)}, u32[]{:S(2)}) collective-permute-start(bf16[32,64,128]{2,1,0:T(8,128)(2,1)S(1)} %bitcast.22), channel_id=1, source_target_pairs={{0,1},{1,0},{2,3},{3,2},{4,5},{5,4},{6,7},{7,6},{8,9},{9,8},{10,11... | collective-permute-start | bytes 1572872 | tf_op jit(solution)/shard_map/ppermute | solution.py:500
  6.5 13.5 %collective-permute-start.2 = (f32[160,128]{1,0:T(8,128)}, f32[160,128]{1,0:T(8,128)S(1)}, u32[]{:S(2)}, u32[]{:S(2)}) collective-permute-start(f32[160,128]{1,0:T(8,128)} %bias.1.refs_0_), channel_id=1, source_target_pairs={{0,3},{1,2},{2,1},{3,0},{4,7},{5,6},{6,5},{7,4},{8,11},{9,10},{10,... | collective-permute-start | bytes 245768 | tf_op jit(solution)/shard_map/ppermute | solution.py:558
  9.1 10.9 %collective-permute-start.1 = (f32[160,128]{1,0:T(8,128)}, f32[160,128]{1,0:T(8,128)S(1)}, u32[]{:S(2)}, u32[]{:S(2)}) collective-permute-start(f32[160,128]{1,0:T(8,128)} %bias.1.refs_0_), channel_id=1, source_target_pairs={{0,2},{1,3},{2,0},{3,1},{4,6},{5,7},{6,4},{7,5},{8,10},{9,11},{10,... | collective-permute-start | bytes 245768 | tf_op jit(solution)/shard_map/ppermute | solution.py:558
  9.1 10.9 %collective-permute-start = (f32[160,128]{1,0:T(8,128)}, f32[160,128]{1,0:T(8,128)S(1)}, u32[]{:S(2)}, u32[]{:S(2)}) collective-permute-start(f32[160,128]{1,0:T(8,128)} %bias.1.refs_0_), channel_id=1, source_target_pairs={{0,1},{1,0},{2,3},{3,2},{4,5},{5,4},{6,7},{7,6},{8,9},{9,8},{10,11... | collective-permute-start | bytes 245768 | tf_op jit(solution)/shard_map/ppermute | solution.py:558
  11.3 0.9 copy-start.3
  20.0 0.6 copy-start.10
  20.0 0.6 copy-start.11
  20.0 0.7 copy-start.12
  27.4 11.4 %collective-permute-start.4 = (bf16[32,16,128]{2,1,0:T(8,128)(2,1)}, bf16[32,16,128]{2,1,0:T(8,128)(2,1)S(1)}, u32[]{:S(2)}, u32[]{:S(2)}) collective-permute-start(bf16[32,16,128]{2,1,0:T(8,128)(2,1)} %get-tuple-element.56), channel_id=1, source_target_pairs={{0,1},{1,0},{2,3},{3,2},{4,5},{5,4},{6,7},{7,6},{8,9},{9,8},{10,11... | collective-permute-start | bytes 393224 | tf_op jit(solution)/shard_map/ppermute | solution.py:558
  27.8 11.0 %collective-permute-start.5 = (bf16[32,16,128]{2,1,0:T(8,128)(2,1)}, bf16[32,16,128]{2,1,0:T(8,128)(2,1)S(1)}, u32[]{:S(2)}, u32[]{:S(2)}) collective-permute-start(bf16[32,16,128]{2,1,0:T(8,128)(2,1)} %get-tuple-element.57), channel_id=1, source_target_pairs={{0,2},{1,3},{2,0},{3,1},{4,6},{5,7},{6,4},{7,5},{8,10},{9,11},{10,... | collective-permute-start | bytes 393224 | tf_op jit(solution)/shard_map/ppermute | solution.py:558
  29.9 9.0 %collective-permute-start.6 = (bf16[32,16,128]{2,1,0:T(8,128)(2,1)}, bf16[32,16,128]{2,1,0:T(8,128)(2,1)S(1)}, u32[]{:S(2)}, u32[]{:S(2)}) collective-permute-start(bf16[32,16,128]{2,1,0:T(8,128)(2,1)} %get-tuple-element.58), channel_id=1, source_target_pairs={{0,3},{1,2},{2,1},{3,0},{4,7},{5,6},{6,5},{7,4},{8,11},{9,10},{10,... | collective-permute-start | bytes 393224 | tf_op jit(solution)/shard_map/ppermute | solution.py:558
  36.6 2.3 %collective-permute-start.7 = (bf16[32,16,128]{2,1,0:T(8,128)(2,1)}, bf16[32,16,128]{2,1,0:T(8,128)(2,1)S(1)}, u32[]{:S(2)}, u32[]{:S(2)}) collective-permute-start(bf16[32,16,128]{2,1,0:T(8,128)(2,1)} %get-tuple-element.64), channel_id=1, source_target_pairs={{0,1},{1,0},{2,3},{3,2},{4,5},{5,4},{6,7},{7,6},{8,9},{9,8},{10,11... | collective-permute-start | bytes 393224 | tf_op jit(solution)/shard_map/ppermute | solution.py:558
  36.8 6.6 %collective-permute-start.8 = (bf16[32,16,128]{2,1,0:T(8,128)(2,1)}, bf16[32,16,128]{2,1,0:T(8,128)(2,1)S(1)}, u32[]{:S(2)}, u32[]{:S(2)}) collective-permute-start(bf16[32,16,128]{2,1,0:T(8,128)(2,1)} %get-tuple-element.65), channel_id=1, source_target_pairs={{0,2},{1,3},{2,0},{3,1},{4,6},{5,7},{6,4},{7,5},{8,10},{9,11},{10,... | collective-permute-start | bytes 393224 | tf_op jit(solution)/shard_map/ppermute | solution.py:558
  38.8 6.2 %copy-start.4 = (bf16[32,16,128]{2,1,0:T(8,128)(2,1)}, bf16[32,16,128]{2,1,0:T(8,128)(2,1)S(1)}, u32[]{:S(2)}) copy-start(bf16[32,16,128]{2,1,0:T(8,128)(2,1)S(1)} %collective-permute-done.4.refs_1_) | copy-start | bytes 393220
  38.8 6.2 %collective-permute-start.9 = (bf16[32,16,128]{2,1,0:T(8,128)(2,1)}, bf16[32,16,128]{2,1,0:T(8,128)(2,1)S(1)}, u32[]{:S(2)}, u32[]{:S(2)}) collective-permute-start(bf16[32,16,128]{2,1,0:T(8,128)(2,1)} %get-tuple-element.66), channel_id=1, source_target_pairs={{0,3},{1,2},{2,1},{3,0},{4,7},{5,6},{6,5},{7,4},{8,11},{9,10},{10,... | collective-permute-start | bytes 393224 | tf_op jit(solution)/shard_map/ppermute | solution.py:558
  38.8 6.2 %copy-start.5 = (bf16[32,16,128]{2,1,0:T(8,128)(2,1)}, bf16[32,16,128]{2,1,0:T(8,128)(2,1)S(1)}, u32[]{:S(2)}) copy-start(bf16[32,16,128]{2,1,0:T(8,128)(2,1)S(1)} %collective-permute-done.5.refs_2_) | copy-start | bytes 393220
  38.8 6.2 %copy-start.6 = (bf16[32,16,128]{2,1,0:T(8,128)(2,1)}, bf16[32,16,128]{2,1,0:T(8,128)(2,1)S(1)}, u32[]{:S(2)}) copy-start(bf16[32,16,128]{2,1,0:T(8,128)(2,1)S(1)} %collective-permute-done.6.refs_3_) | copy-start | bytes 393220
  38.9 6.2 %copy-start.7 = (bf16[32,16,128]{2,1,0:T(8,128)(2,1)}, bf16[32,16,128]{2,1,0:T(8,128)(2,1)S(1)}, u32[]{:S(2)}) copy-start(bf16[32,16,128]{2,1,0:T(8,128)(2,1)S(1)} %collective-permute-done.7.refs_5_) | copy-start | bytes 393220
  43.4 1.7 %copy-start.8 = (bf16[32,16,128]{2,1,0:T(8,128)(2,1)}, bf16[32,16,128]{2,1,0:T(8,128)(2,1)S(1)}, u32[]{:S(2)}) copy-start(bf16[32,16,128]{2,1,0:T(8,128)(2,1)S(1)} %collective-permute-done.8.refs_6_) | copy-start | bytes 393220
  45.0 0.6 copy-start.9
  61.9 2.2 %collective-permute-start.10 = (bf16[4,32,128]{2,1,0:T(8,128)(2,1)}, bf16[4,32,128]{2,1,0:T(8,128)(2,1)S(1)}, u32[]{:S(2)}, u32[]{:S(2)}) collective-permute-start(bf16[4,32,128]{2,1,0:T(8,128)(2,1)} %get-tuple-element.80), channel_id=1, source_target_pairs={{0,1},{1,0},{2,3},{3,2},{4,5},{5,4},{6,7},{7,6},{8,9},{9,8},{10,11... | collective-permute-start | bytes 98312 | tf_op jit(solution)/shard_map/ppermute | solution.py:558
  62.4 4.1 %collective-permute-start.11 = (bf16[4,32,128]{2,1,0:T(8,128)(2,1)}, bf16[4,32,128]{2,1,0:T(8,128)(2,1)S(1)}, u32[]{:S(2)}, u32[]{:S(2)}) collective-permute-start(bf16[4,32,128]{2,1,0:T(8,128)(2,1)} %get-tuple-element.81), channel_id=1, source_target_pairs={{0,2},{1,3},{2,0},{3,1},{4,6},{5,7},{6,4},{7,5},{8,10},{9,11},{10,... | collective-permute-start | bytes 98312 | tf_op jit(solution)/shard_map/ppermute | solution.py:558
  64.1 3.9 %collective-permute-start.12 = (bf16[4,32,128]{2,1,0:T(8,128)(2,1)}, bf16[4,32,128]{2,1,0:T(8,128)(2,1)S(1)}, u32[]{:S(2)}, u32[]{:S(2)}) collective-permute-start(bf16[4,32,128]{2,1,0:T(8,128)(2,1)} %get-tuple-element.82), channel_id=1, source_target_pairs={{0,3},{1,2},{2,1},{3,0},{4,7},{5,6},{6,5},{7,4},{8,11},{9,10},{10,... | collective-permute-start | bytes 98312 | tf_op jit(solution)/shard_map/ppermute | solution.py:558
  64.1 3.9 %copy-start = (bf16[4,32,128]{2,1,0:T(8,128)(2,1)}, bf16[4,32,128]{2,1,0:T(8,128)(2,1)S(1)}, u32[]{:S(2)}) copy-start(bf16[4,32,128]{2,1,0:T(8,128)(2,1)S(1)} %collective-permute-done.10.refs_1_) | copy-start | bytes 98308
  66.5 1.5 %copy-start.1 = (bf16[4,32,128]{2,1,0:T(8,128)(2,1)}, bf16[4,32,128]{2,1,0:T(8,128)(2,1)S(1)}, u32[]{:S(2)}) copy-start(bf16[4,32,128]{2,1,0:T(8,128)(2,1)S(1)} %collective-permute-done.11.refs_2_) | copy-start | bytes 98308
  67.9 0.6 copy-start.2

commit v4 on v3

--- a/solution.py
+++ b/solution.py
@@ -14,9 +14,9 @@
 FWD_ROWS = 8
 BWD_ROWS = 8
 FWD_PACE = (8, 1, 0)
-BWD_PACE = (8, 0, 0)
+BWD_PACE = (2, 0, 3)
 PROJ_PACE = (2, 0, 3)
-FIN_PACE = (8, 0, 0)
+FIN_PACE = (8, 1, 0)
 PROJ_ROWS = 8
 FIN_ROWS = 8
 EPS = 1e-5
@@ -79,12 +79,11 @@
     return pl.BlockSpec(shape, lambda *_: (0,) * len(shape))
 
 
-def prep_kernel(wq, wk, wv, wg, wo, gb, ob, wd, db, wpb, lng, w4t, w3, wod, wdt, wd3, wqg, wkv, gbc, lgc, cst, wgc):
+def prep_kernel(wq, wk, wv, wg, wo, gb, ob, wd, db, wpb, lng, w4t, w2, wod, wdt, wd3, wall, gbc, lgc, cst, wgs):
     wide = gbc.shape[1]
     w4t[...] = jnp.concatenate([transposed(w[...]) for w in (wq, wk, wv, wg)], axis=0)
-    w3[...] = jnp.concatenate([wq[...], wk[...], wv[...]], axis=1)
-    wqg[...] = jnp.concatenate([wq[...], wg[...]], axis=1)
-    wkv[...] = jnp.concatenate([wk[...], wv[...]], axis=1)
+    w2[...] = jnp.concatenate([wk[...], wv[...]], axis=1)
+    wall[...] = jnp.concatenate([wq[...], wk[...], wv[...], wg[...]], axis=1)
     dist_t = wd[...]
     dist = dist_t.T
     dist_hi, dist_lo = split(dist)
@@ -96,18 +95,37 @@
     lgc[...] = column(lng[...], wide)
     shift = 2.0 * jnp.sum(dist_t * ob[...], axis=1, keepdims=True)
     cst[...] = column(db[...], wide) + shift
-    gain = column(lng[...], wide)
-    for h in range(H):
-        wgc[h] = column(wpb[h : h + 1], wide) * gain
+    proj = jnp.concatenate([wpb[...], jnp.zeros((wide - H, wpb.shape[1]), F32)], axis=0).T[:, :H]
+    proj_hi, proj_lo = split(proj)
+    wgs[...] = jnp.concatenate([proj_hi, proj_hi, proj_lo, jnp.zeros_like(proj_lo)], axis=1)
 
 
 def bias_kernel(tile, targets, lng, lnb, wpb, out, *, per_head):
     step = pl.program_id(0)
     fold, lines, side, chans = tile.shape
     pieces = [tile[f, q] for q in range(lines) for f in range(fold)]
-    normed = rows_norm(jnp.concatenate(pieces, axis=0).astype(F32)) * lng[...] + lnb[...]
-    proj = jnp.concatenate([wpb[...], jnp.zeros((8 - H, chans), F32)], axis=0)
-    bias = nt(proj, normed, precision=HIGHEST)
+    pair = jnp.concatenate(pieces, axis=0)
+    proj = wpb[...] * lng[...]
+    high, rest = split(proj)
+    mid = rest
+    last = (proj - high.astype(F32) - mid.astype(F32)).astype(BF)
+    left = jnp.concatenate(
+        [high.astype(F32), mid.astype(F32), last.astype(F32), jnp.ones((H, chans), F32)], axis=0
+    ).astype(BF)
+    left = jnp.concatenate([eye(chans), left], axis=0)
+    total = jnp.sum(proj, axis=1, keepdims=True)
+    const = jnp.sum(wpb[...] * lnb[...], axis=1, keepdims=True)
+    size = fold * side
+    rows_out = []
+    for q in range(lines):
+        up = nt(left, pair[q * size : (q + 1) * size])
+        extra = up[chans:]
+        mean = extra[3 * H : 3 * H + 1] * (1.0 / chans)
+        center = up[:chans] - mean
+        inverse = lax.rsqrt(jnp.mean(center * center, axis=0, keepdims=True) + EPS)
+        dotted = extra[:H] + extra[H : 2 * H] + extra[2 * H : 3 * H]
+        rows_out.append(inverse * (dotted - mean * total) + const)
+    bias = jnp.concatenate(rows_out, axis=1)
     width = fold * side
     for q in range(lines):
         for h in range(H):
@@ -124,8 +142,9 @@
 def project_kernel(own_ref, *refs, parts):
     own = own_ref[0]
     part_refs = refs[:parts]
-    lng, lnb, w4t, w3, gbc, zr, qt, kt, vt, qn, kn, vn, gt = refs[parts:]
+    lng, lnb, w4t, w2, gbc, zr, qt, kt, vt, kn, vn, gt, flat_s = refs[parts:]
     rows, side, _ = part_refs[0].shape
+    wide = zr.shape[1]
     width = H * HD
     for row in range(rows):
         for k in range(parts):
@@ -138,38 +157,51 @@
         yield
         inverse = lax.rsqrt(jnp.mean(center * center, axis=-1, keepdims=True) + EPS)
         yield
-        flat = (center * inverse * lng[...] + lnb[...]).astype(BF)
-        yield
+        flat_s[row * wide : (row + 1) * wide, :] = (
+            center * inverse * lng[...] + lnb[...]
+        ).astype(BF)
+        yield
+
+    def one_pair(first):
+        both = one_row(first), one_row(first + 1)
+        for _ in range(3):
+            for row in both:
+                next(row)
+            yield
+        flat = flat_s[first * wide : (first + 2) * wide, :]
         for k, out in enumerate((qt, kt, vt)):
-            out[row] = nt(w4t[k * width : (k + 1) * width], flat).astype(BF)
+            up = nt(w4t[k * width : (k + 1) * width], flat)
+            for n in range(2):
+                out[first + n] = up[:, n * wide : (n + 1) * wide].astype(BF)
             yield
-        gt[row] = jax.nn.sigmoid(nt(w4t[3 * width :], flat) + gbc[...])
-        yield
-        for k, out in enumerate((qn, kn, vn)):
-            out[row] = nn(flat, w3[:, k * width : (k + 1) * width]).astype(BF)
+        up = nt(w4t[3 * width :], flat)
+        for n in range(2):
+            gt[first + n] = jax.nn.sigmoid(up[:, n * wide : (n + 1) * wide] + gbc[...])
             yield
-
-    interleave([one_row(row) for row in range(rows)], PROJ_PACE)
+        down = nn(flat, w2[...])
+        for n in range(2):
+            kn[first + n] = down[n * wide : (n + 1) * wide, :width].astype(BF)
+            vn[first + n] = down[n * wide : (n + 1) * wide, width:].astype(BF)
+        yield
+
+    interleave([one_pair(row) for row in range(0, rows, 2)], PROJ_PACE)
+
+
+def head_block(part, h):
+    lanes = part.shape[1]
+    pieces = []
+    if h:
+        pieces.append(jnp.zeros((h * HD, lanes), part.dtype))
+    pieces.append(part)
+    if h < H - 1:
+        pieces.append(jnp.zeros(((H - 1 - h) * HD, lanes), part.dtype))
+    return jnp.concatenate(pieces, axis=0)
 
 
 def head_blocks(packed):
-    rows, lanes = packed.shape
-    blocks = []
-    for h in range(H):
-        pieces = []
-        if h:
-            pieces.append(jnp.zeros((h * HD, lanes), packed.dtype))
-        pieces.append(packed[h * HD : (h + 1) * HD])
-        if h < H - 1:
-            pieces.append(jnp.zeros((rows - (h + 1) * HD, lanes), packed.dtype))
-        blocks.append(jnp.concatenate(pieces, axis=0))
-    return jnp.concatenate(blocks, axis=1)
-
-
-def head_rows(packed):
-    lane = lax.broadcasted_iota(jnp.int32, packed.shape, 1) // HD
-    zero = jnp.zeros_like(packed)
-    return jnp.concatenate([jnp.where(lane == h, packed, zero) for h in range(H)], axis=0)
+    return jnp.concatenate(
+        [head_block(packed[h * HD : (h + 1) * HD], h) for h in range(H)], axis=1
+    )
 
 
 def forward_kernel(
@@ -274,13 +306,12 @@
 
 def backward_kernel(*refs, tiles, chunks, grid_side, groups, group_rows):
     rcv = refs[: tiles * chunks]
-    tgt, at, ot, ut, gt, vn, kt, qn, zr, wo, wd3, wqg, wkv, lgc, cst, dzm = refs[
-        tiles * chunks : tiles * chunks + 16
+    tgt, at, ot, ut, gt, vn, kt, qt, wo, wd3, wall, cst, dpt, dzn = refs[
+        tiles * chunks : tiles * chunks + 14
     ]
-    sends = refs[tiles * chunks + 16 : tiles * chunks + 16 + tiles]
-    acc, grad_s, gate_s, value_s, score_s, query_s, mirror_s, order = refs[
-        tiles * chunks + 16 + tiles :
-    ]
+    sends = refs[tiles * chunks + 14 : tiles * chunks + 14 + tiles]
+    acc, grad_s, back_s, mirror_s, order = refs[tiles * chunks + 14 + tiles :]
+    width = H * HD
     step = pl.program_id(0)
     mine = lax.axis_index("tile")
     rows = vn.shape[0]
@@ -288,90 +319,93 @@
     chunk_groups = groups // chunks
     share = groups * group_rows
     inv_root = 1.0 / math.sqrt(HD)
-    ident = eye(wide)
-    adder = jnp.concatenate([ident[:NB, :NB], ident[:NB, :NB]], axis=1)
-    bins = lax.broadcasted_iota(jnp.int32, (NB, wide), 0).astype(F32)
+    adder = jnp.concatenate([eye(NB)] * 2, axis=1)
+    bins = lax.broadcasted_iota(jnp.int32, (NB, 2 * wide), 0).astype(F32)
 
     @pl.when(step == 0)
     def _():
         acc[...] = jnp.zeros_like(acc)
 
-    def one_row(row):
-        for k in range(tiles):
-            source_i = (mine ^ k) // grid_side
-            source_j = lax.rem(mine ^ k, grid_side)
-            for p in range(groups):
-                start = ((source_i * groups + p) * grid_side + source_j) * group_rows
-                local = (p % chunk_groups) * group_rows
-                mirror_s[row, pl.ds(pl.multiple_of(start, group_rows), group_rows), :] = rcv[
-                    (p // chunk_groups) * tiles + k
-                ][row, local : local + group_rows].astype(F32)
-        yield
-        other = nt(adder, mirror_s[row].astype(BF))
-        yield
-        logits = ut[row] + other + cst[...]
+    shift = jnp.concatenate([cst[...]] * 2, axis=1)
+
+    def one_pair(first):
+        pair = (first, first + 1)
+        for row in pair:
+            for k in range(tiles):
+                source_i = (mine ^ k) // grid_side
+                source_j = lax.rem(mine ^ k, grid_side)
+                for p in range(groups):
+                    start = ((source_i * groups + p) * grid_side + source_j) * group_rows
+                    local = (p % chunk_groups) * group_rows
+                    mirror_s[pl.ds(pl.multiple_of(row * wide + start, group_rows), group_rows), :] = rcv[
+                        (p // chunk_groups) * tiles + k
+                    ][row, local : local + group_rows].astype(F32)
+        yield
+        other = nt(adder, mirror_s[first * wide : (first + 2) * wide, :].astype(BF))
+        yield
+        logits = jnp.concatenate([ut[row] for row in pair], axis=1) + other + shift
         peak = jnp.max(logits, axis=0, keepdims=True)
         yield
         probs = jnp.exp(logits - peak)
         total = jnp.sum(probs, axis=0, keepdims=True)
         yield
-        resid = 2.0 * (probs * (1.0 / total) - jnp.where(bins == tgt[row : row + 1, :], 1.0, 0.0))
+        target = jnp.concatenate([tgt[row : row + 1, :] for row in pair], axis=1)
+        resid = 2.0 * (probs * (1.0 / total) - jnp.where(bins == target, 1.0, 0.0))
         res_hi, res_lo = split(resid)
         yield
         pair_grad = nn(wd3[...], jnp.concatenate([res_hi, res_lo, res_hi], axis=0))
-        dzm[row] = pair_grad
+        for n, row in enumerate(pair):
+            dpt[row] = pair_grad[:, n * wide : (n + 1) * wide]
         yield
         out_grad = nn(wo[...], pair_grad.astype(BF))
         yield
-        gate = gt[row]
-        gated = out_grad * gate
-        grad_s[row] = gated.astype(BF)
-        yield
-        gate_s[row] = (gated * ot[row] * (1.0 - gate)).astype(BF)
-        yield
-        grad_n = gated.T.astype(BF)
-        yield
-        value_s[row] = nn(at[row], head_rows(grad_n)).astype(BF)
-        yield
-        blocks = head_blocks(grad_s[row])
-        yield
-        for pair in range(0, H, 2):
-            weight_grad = nn(vn[row], blocks[:, pair * wide : (pair + 2) * wide])
+        for n, row in enumerate(pair):
+            gate = gt[row]
+            gated = out_grad[:, n * wide : (n + 1) * wide] * gate
+            grad_s[row] = gated.astype(BF)
+            back_s[3 * width :, row * wide : (row + 1) * wide] = (
+                gated * ot[row] * (1.0 - gate)
+            ).astype(BF)
             yield
-            for h in range(pair, pair + 2):
+
+        def heads(row):
+            lanes = slice(row * wide, (row + 1) * wide)
+            for h in range(H):
+                part = slice(h * HD, (h + 1) * HD)
+                back_s[2 * width + h * HD : 2 * width + (h + 1) * HD, lanes] = nt(
+                    grad_s[row, part, :], at[row, :, h * wide : (h + 1) * wide]
+                ).astype(BF)
+                yield
+                weight_grad = nn(vn[row], head_block(grad_s[row, part, :], h))
+                yield
                 prob = at[row, :, h * wide : (h + 1) * wide].astype(F32)
-                prod = prob * weight_grad[:, (h - pair) * wide : (h - pair + 1) * wide]
+                prod = prob * weight_grad
                 total = jnp.sum(prod, axis=0, keepdims=True)
                 yield
                 prod = prod - prob * total
-                score_s[row, :, h * wide : (h + 1) * wide] = prod.astype(BF)
+                prod_b = prod.astype(BF)
                 acc[h] += prod
                 yield
-                query_s[row, h * HD : (h + 1) * HD, :] = (
-                    nn(kt[row, h * HD : (h + 1) * HD, :], score_s[row, :, h * wide : (h + 1) * wide])
-                    * inv_root
+                back_s[h * HD : (h + 1) * HD, lanes] = (nn(kt[row, part, :], prod_b) * inv_root).astype(BF)
+                back_s[width + h * HD : width + (h + 1) * HD, lanes] = (
+                    nt(qt[row, part, :], prod_b) * inv_root
                 ).astype(BF)
                 yield
-        key_grad = nn(score_s[row], head_rows(qn[row])) * inv_root
-        yield
-        normed_grad = nn(wqg[...], jnp.concatenate([query_s[row], gate_s[row]], axis=0)) + nt(
-            wkv[...], jnp.concatenate([key_grad.astype(BF), value_s[row]], axis=1)
-        )
-        yield
-        pair_t = nt(ident, zr[row])
-        center = pair_t - jnp.mean(pair_t, axis=0, keepdims=True)
-        yield
-        inverse = lax.rsqrt(jnp.mean(center * center, axis=0, keepdims=True) + EPS)
-        normed = center * inverse
-        yield
-        scaled = normed_grad * lgc[...]
-        mean_a = jnp.mean(scaled, axis=0, keepdims=True)
-        mean_b = jnp.mean(scaled * normed, axis=0, keepdims=True)
-        yield
-        dzm[row] = dzm[row] + inverse * (scaled - mean_a - normed * mean_b)
-        yield
-
-    interleave([one_row(row) for row in range(rows)], BWD_PACE)
+
+        both = [heads(row) for row in pair]
+        while both:
+            for row in list(both):
+                try:
+                    next(row)
+                except StopIteration:
+                    both.remove(row)
+            yield
+        normed_grad = nn(wall[...], back_s[:, first * wide : (first + 2) * wide])
+        for n, row in enumerate(pair):
+            dzn[row] = normed_grad[:, n * wide : (n + 1) * wide]
+        yield
+
+    interleave([one_pair(row) for row in range(0, rows, 2)], BWD_PACE)
 
     @pl.when(step == pl.num_programs(0) - 1)
     def _():
@@ -392,9 +426,9 @@
 
 def finish_kernel(offsets, *refs, tiles):
     rdb = refs[:tiles]
-    dzm, zr, wgc, out, sums = refs[tiles:]
+    dpt, dzn, zr, wgs, lgc, out, sums = refs[tiles:]
     step = pl.program_id(0)
-    rows, chans, wide = dzm.shape
+    rows, chans, wide = dzn.shape
     states, _, piece, _ = out.shape
     total_rows = rdb[0].shape[1]
     turn = offsets[lax.axis_index("state")] // piece
@@ -418,15 +452,16 @@
         inverse = lax.rsqrt(jnp.mean(center * center, axis=0, keepdims=True) + EPS)
         normed = center * inverse
         yield
-        scaled = None
-        for h in range(H):
-            term = wgc[h] * sums[pl.ds(h * total_rows + local, 1), :]
-            scaled = term if scaled is None else scaled + term
+        parts = [sums[pl.ds(h * total_rows + local, 1), :] for h in range(H)]
+        high, low = split(jnp.concatenate(parts, axis=0))
+        spread = jnp.concatenate([high.astype(F32), low.astype(F32), high.astype(F32), jnp.zeros((H, wide), F32)], axis=0)
+        yield
+        scaled = (dzn[row] + nn(wgs[...], spread.astype(BF))) * lgc[...]
         yield
         mean_a = jnp.mean(scaled, axis=0, keepdims=True)
         mean_b = jnp.mean(scaled * normed, axis=0, keepdims=True)
         yield
-        total = dzm[row] + inverse * (scaled - mean_a - normed * mean_b)
+        total = dpt[row] + inverse * (scaled - mean_a - normed * mean_b)
         yield
         total = total.T.astype(BF)
         for c in range(wide // piece):
@@ -503,18 +538,17 @@
     shift_row = ln_bias.reshape(1, chans)
     prep_shapes = shapes(
         ((4 * width, chans), BF),
-        ((chans, 3 * width), BF),
+        ((chans, 2 * width), BF),
         ((2 * NB, width), BF),
         ((2 * NB, chans), BF),
         ((chans, 3 * NB), BF),
-        ((chans, 2 * width), BF),
-        ((chans, 2 * width), BF),
+        ((chans, 4 * width), BF),
         ((width, wide), F32),
         ((chans, wide), F32),
         ((NB, wide), F32),
-        ((H, chans, wide), F32),
+        ((chans, 4 * H), BF),
     )
-    w4t, w3, wod, wdt, wd3, wqg, wkv, gbc, lgc, cst, wgc = pl.pallas_call(
+    w4t, w2, wod, wdt, wd3, wall, gbc, lgc, cst, wgs = pl.pallas_call(
         prep_kernel, out_shape=prep_shapes, name="prep"
     )(
         w_query,
@@ -567,7 +601,7 @@
 
     cell = wide * width * wide
     square_b = ((share, wide, width), BF)
-    zr, qt, kt, vt, qn, kn, vn, gt = pl.pallas_call(
+    zr, qt, kt, vt, kn, vn, gt = pl.pallas_call(
         functools.partial(project_kernel, parts=grid_side),
         grid_spec=pltpu.PrefetchScalarGridSpec(
             num_scalar_prefetch=1,
@@ -578,13 +612,14 @@
                 )
             ]
             + [by_row(side, chans, rows=group_rows)] * (grid_side - 1)
-            + [full((1, chans)), full((1, chans)), full(w4t.shape), full(w3.shape), full(gbc.shape)],
-            out_specs=[by_row(wide, width, rows=group_rows)] * 8,
+            + [full((1, chans)), full((1, chans)), full(w4t.shape), full(w2.shape), full(gbc.shape)],
+            out_specs=[by_row(wide, width, rows=group_rows)] * 7,
+            scratch_shapes=[pltpu.VMEM((group_rows * wide, chans), BF)],
         ),
-        out_shape=shapes(*([square_b] * 7), ((share, width, wide), F32)),
+        out_shape=shapes(*([square_b] * 6), ((share, width, wide), F32)),
         cost_estimate=cost(80 * share * cell, 12 * share * wide * width * 2),
         name="project",
-    )(tile_j.reshape(1), *parts, gain_row, shift_row, w4t, w3, gbc)
+    )(tile_j.reshape(1), *parts, gain_row, shift_row, w4t, w2, gbc)
 
     chunks = 2 if groups % 2 == 0 else 1
     chunk_groups = groups // chunks
@@ -653,24 +688,25 @@
             by_row(width, wide, rows=block),
             by_row(NB, wide, rows=block),
         ]
-        + [by_row(wide, width, rows=block)] * 5
-        + [full(w.shape) for w in (w_output, wd3, wqg, wkv, lgc, cst)],
-        out_specs=[by_row(chans, wide, rows=block)] + [full((H, share, wide))] * tiles,
-        out_shape=shapes(((share, chans, wide), F32), *([((H, share, wide), BF)] * tiles)),
-        scratch_shapes=[pltpu.VMEM((H, wide, wide), F32)]
-        + [
-            pltpu.VMEM((block,) + shape, BF)
-            for shape in ((width, wide), (width, wide), (wide, width), (wide, H * wide), (width, wide))
-        ]
-        + [pltpu.VMEM((block, wide, 2 * NB), F32), pltpu.VMEM((tiles, H * share, wide), F32)],
+        + [by_row(wide, width, rows=block)] * 4
+        + [full(w.shape) for w in (w_output, wd3, wall, cst)],
+        out_specs=[by_row(chans, wide, rows=block)] * 2 + [full((H, share, wide))] * tiles,
+        out_shape=shapes(*([((share, chans, wide), F32)] * 2), *([((H, share, wide), BF)] * tiles)),
+        scratch_shapes=[
+            pltpu.VMEM((H, wide, wide), F32),
+            pltpu.VMEM((block, width, wide), BF),
+            pltpu.VMEM((4 * width, block * wide), BF),
+            pltpu.VMEM((block * wide, 2 * NB), F32),
+            pltpu.VMEM((tiles, H * share, wide), F32),
+        ],
         cost_estimate=cost(500 * share * cell, 20 * share * wide * width * 2),
         name="backward",
     )(
         *[part for parts_c in mirrored for part in parts_c],
-        tgt, at, ot, ut, gt, vn, kt, qn, zr, w_output, wd3, wqg, wkv, lgc, cst,
+        tgt, at, ot, ut, gt, vn, kt, qt, w_output, wd3, wall, cst,
     )
-    dzm = results[0]
-    rdb = [to_partner(results[1 + k], k) for k in range(tiles)]
+    dpt, dzn = results[:2]
+    rdb = [to_partner(results[2 + k], k) for k in range(tiles)]
 
     block = FIN_ROWS if share % FIN_ROWS == 0 else 1
     outgoing = pl.pallas_call(
@@ -681,15 +717,17 @@
             in_specs=[
                 *([full(rdb[0].shape)] * tiles),
                 pl.BlockSpec((block, chans, wide), lambda g, _: (g, 0, 0)),
+                pl.BlockSpec((block, chans, wide), lambda g, _: (g, 0, 0)),
                 pl.BlockSpec((block, wide, chans), lambda g, _: (g, 0, 0)),
-                full(wgc.shape),
+                full(wgs.shape),
+                full(lgc.shape),
             ],
             out_specs=pl.BlockSpec((states, block, piece, chans), lambda g, _: (0, g, 0, 0)),
             scratch_shapes=[pltpu.VMEM((H * share, wide), F32)],
         ),
         out_shape=jax.ShapeDtypeStruct((states, share, piece, chans), BF),
         name="finish",
-    )(offsets, *rdb, dzm, zr, wgc)
+    )(offsets, *rdb, dpt, dzn, zr, wgs, lgc)
 
     if even:
         slots = outgoing.reshape(states * tiles, group_rows, piece, chans)

time: 111 us -> 108 us (0.973)
  Pallas kernels: 54.7 us -> 51.9 us
    pallas_call x1, Pallas kernels: 7.76 us -> 6.48 us  [on_device(): pl.pallas_call(functools.partial(project_kernel, parts=grid_side), grid_s...]
    pallas_call x1, Pallas kernels: 4.86 us -> 3.65 us  [on_device(): pl.pallas_call(functools.partial(bias_kernel, per_head=per_head), grid=(p...]
  transfers between devices with their start and end apart: 13 -> 13, of which waited for: 4 -> 4; matrix products, arithmetic and copies ran while one was open for 0% -> 0% of each run, Pallas kernels for 19% -> 18%
where the time goes in v4:
time: 108 us; the launch traced here: 107 us
  Pallas kernels  51.9 us (48%)
  blocking collectives  31.2 us (29%)
  starting transfers between devices  10.1 us (9%)
  waiting for transfers between devices  10 us (9%)
  local copies, waits for them, and re-layouts  3.8 us (4%)
    all_to_all x1, blocking collectives, on_device(): lax.all_to_all(slots, ('state', 'tile'), split_axis=0, concat_axis=0, til...  31.2 us
    pallas_call x1, Pallas kernels, on_device(): pl.pallas_call(functools.partial(backward_kernel, tiles=tiles, chunks=chu...  15.5 us
    pallas_call x2, Pallas kernels, on_device(): results = call(*inputs, *saved)  13.6 us
    ppermute x12, waiting for transfers between devices, to_partner(): lax.ppermute(value, 'tile', [(t, t ^ k) for t in range(tiles)])  10 us
    ppermute x12, starting transfers between devices, to_partner(): lax.ppermute(value, 'tile', [(t, t ^ k) for t in range(tiles)])  9.58 us
    pallas_call x1, Pallas kernels, on_device(): pl.pallas_call(functools.partial(project_kernel, parts=grid_side), grid_s...  6.48 us
    pallas_call x1, Pallas kernels, on_device(): pl.pallas_call(functools.partial(finish_kernel, tiles=tiles), grid_spec=p...  6.36 us
    pallas_call x1, Pallas kernels, on_device(): pl.pallas_call(functools.partial(place_kernel, side=side), grid_spec=pltp...  4.16 us
  transfers between devices with their start and end apart: 13, of which 4 were waited for; matrix products, arithmetic and copies ran while one was open for 0% of the time, Pallas kernels for 18%

profile of v4, /device:TPU:0, one launch (start us, length us, event | category | flops | bytes accessed | tf_op | source)
XLA Modules:
  0.0 107.2 jit_solution(15996190131899804312)
XLA Ops:
  0.0 1.1 %constant_dynamic-slice_fusion = bf16[4,1,8,64,128]{4,3,2,1,0:T(8,128)(2,1)S(1)} fusion(bf16[4,2,8,64,128]{4,3,2,1,0:T(8,128)(2,1)} %bitcast.19, s32[]{:T(128)S(6)} %select_n.4), kind=kLoop, calls=%fused_computation | loop fusion | bytes 1048580 | tf_op jit(solution)/shard_map/jit(dynamic_index_in_dim)/dynamic_slice | solution.py:526
  1.1 0.6 collective-permute-start.3
  1.6 3.7 %bias.1.refs_0_ = f32[160,128]{1,0:T(8,128)} custom-call(bf16[2,32,64,128]{3,2,1,0:T(8,128)(2,1)} %bitcast.20, s32[32,128]{1,0:T(8,128)} %bitcast.24, f32[1,128]{1,0:T(1,128)} %bitcast.27, f32[1,128]{1,0:T(1,128)} %bitcast.33, f32[4,128]{1,0:T(4,128)} %bitcast.25), custom_call_target="tpu_custom_call" | custom-call | tf_op jit(solution)/shard_map/bias/pallas_call | solution.py:570
  5.3 2.6 %collective-permute-start.2 = (f32[160,128]{1,0:T(8,128)}, f32[160,128]{1,0:T(8,128)S(1)}, u32[]{:S(2)}, u32[]{:S(2)}) collective-permute-start(f32[160,128]{1,0:T(8,128)} %bias.1.refs_0_), channel_id=1, source_target_pairs={{0,3},{1,2},{2,1},{3,0},{4,7},{5,6},{6,5},{7,4},{8,11},{9,10},{10,... | collective-permute-start | bytes 245768 | tf_op jit(solution)/shard_map/ppermute | solution.py:592
  7.9 0.0 collective-permute-start.1
  7.9 0.1 collective-permute-start
  8.0 2.1 %prep.1 = (bf16[512,128]{1,0:T(8,128)(2,1)}, bf16[128,256]{1,0:T(8,128)(2,1)}, bf16[128,128]{1,0:T(8,128)(2,1)}, bf16[128,128]{1,0:T(8,128)(2,1)}, bf16[128,192]...) custom-call(bf16[128,128]{1,0:T(8,128)(2,1)} %wq.1, ...), custom_call_target="tpu_custom_call" | custom-call | tf_op jit(solution)/shard_map/prep/pallas_call | solution.py:551
  10.1 0.0 collective-permute-done.3.refs_1_
  10.1 0.0 copy-start.3
  10.1 0.8 copy-done.3
  10.9 6.5 %project.1 = (bf16[32,128,128]{2,1,0:T(8,128)(2,1)}, bf16[32,128,128]{2,1,0:T(8,128)(2,1)}, bf16[32,128,128]{2,1,0:T(8,128)(2,1)}, bf16[32,128,128]{2,1,0:T(8,12...) custom-call(s32[1]{0:T(128)} %bitcast.5.own_ref, ...), custom_call_target="tpu_custom_call" | custom-call | flops 5368709120 | bytes 12582912 | tf_op jit(solution)/shard_map/project/pallas_call | solution.py:604
  17.4 0.0 collective-permute-done.2.refs_3_
  17.4 0.0 copy-start.10
  17.4 0.0 collective-permute-done.1.refs_2_
  17.4 0.0 copy-start.11
  17.4 0.0 collective-permute-done.refs_1_
  17.4 0.6 copy-done.10
  18.0 0.0 copy-done.11
  18.0 0.0 copy-done.12
  18.1 6.8 %forward.2 = (bf16[32,128,512]{2,1,0:T(8,128)(2,1)}, f32[32,128,128]{2,1,0:T(8,128)}, f32[32,64,128]{2,1,0:T(8,128)}, f32[32,128]{1,0:T(8,128)}, f32[4,128,128]{...) custom-call(f32[160,128]{1,0:T(8,128)} %bias.1.refs_0_, ...), custom_call_target="tpu_custom_call" | custom-call | flops 5033164800 | bytes 7340032 | tf_op jit(solution)/shard_map/forward/pallas_call | solution.py:676
  24.9 0.5 collective-permute-start.4
  25.4 2.0 %collective-permute-start.5 = (bf16[32,16,128]{2,1,0:T(8,128)(2,1)}, bf16[32,16,128]{2,1,0:T(8,128)(2,1)S(1)}, u32[]{:S(2)}, u32[]{:S(2)}) collective-permute-start(bf16[32,16,128]{2,1,0:T(8,128)(2,1)} %get-tuple-element.56), channel_id=1, source_target_pairs={{0,2},{1,3},{2,0},{3,1},{4,6},{5,7},{6,4},{7,5},{8,10},{9,11},{10,... | collective-permute-start | bytes 393224 | tf_op jit(solution)/shard_map/ppermute | solution.py:592
  27.4 0.0 collective-permute-start.6
  27.4 6.8 %forward.3 = (bf16[32,128,512]{2,1,0:T(8,128)(2,1)}, f32[32,128,128]{2,1,0:T(8,128)}, f32[32,64,128]{2,1,0:T(8,128)}, f32[32,128]{1,0:T(8,128)}, f32[4,128,128]{...) custom-call(f32[160,128]{1,0:T(8,128)} %bias.1.refs_0_, ...), custom_call_target="tpu_custom_call", output_to_operand_aliasing={{0}: (11, {}), {1}: (12, {}), {2}: (13, {}), {3}: (14, {})} | custom-call | flops 5033164800 | bytes 7340032 | tf_op jit(solution)/shard_map/forward/pallas_call | solution.py:676
  34.2 0.2 collective-permute-start.7
  34.4 2.0 %collective-permute-start.8 = (bf16[32,16,128]{2,1,0:T(8,128)(2,1)}, bf16[32,16,128]{2,1,0:T(8,128)(2,1)S(1)}, u32[]{:S(2)}, u32[]{:S(2)}) collective-permute-start(bf16[32,16,128]{2,1,0:T(8,128)(2,1)} %get-tuple-element.64), channel_id=1, source_target_pairs={{0,2},{1,3},{2,0},{3,1},{4,6},{5,7},{6,4},{7,5},{8,10},{9,11},{10,... | collective-permute-start | bytes 393224 | tf_op jit(solution)/shard_map/ppermute | solution.py:592
  36.4 0.0 collective-permute-done.4.refs_1_
  36.4 0.0 collective-permute-start.9
  36.4 0.0 collective-permute-done.5.refs_2_
  36.5 0.0 collective-permute-done.6.refs_3_
  36.5 0.0 collective-permute-done.7.refs_5_
  36.5 0.0 copy-start.7
  36.5 4.5 %collective-permute-done.8.refs_6_ = bf16[32,16,128]{2,1,0:T(8,128)(2,1)S(1)} collective-permute-done((bf16[32,16,128]{2,1,0:T(8,128)(2,1)}, bf16[32,16,128]{2,1,0:T(8,128)(2,1)S(1)}, u32[]{:S(2)}, u32[]{:S(2)}) %collective-permute-start.8) | collective-permute-done | bytes 131104 | tf_op jit(solution)/shard_map/ppermute | solution.py:592
  41.0 1.6 %collective-permute-done.9.refs_7_ = bf16[32,16,128]{2,1,0:T(8,128)(2,1)S(1)} collective-permute-done((bf16[32,16,128]{2,1,0:T(8,128)(2,1)}, bf16[32,16,128]{2,1,0:T(8,128)(2,1)S(1)}, u32[]{:S(2)}, u32[]{:S(2)}) %collective-permute-start.9) | collective-permute-done | bytes 131104 | tf_op jit(solution)/shard_map/ppermute | solution.py:592
  42.7 0.0 copy-done.6
  42.7 0.6 copy-done.9
  43.3 15.5 %backward.1 = (f32[32,128,128]{2,1,0:T(8,128)}, f32[32,128,128]{2,1,0:T(8,128)}, bf16[4,32,128]{2,1,0:T(8,128)(2,1)}, bf16[4,32,128]{2,1,0:T(8,128)(2,1)}, bf16[...) custom-call(bf16[32,16,128]{2,1,0:T(8,128)(2,1)} %get-tuple-element.54.refs_0_, bf16[32,16,128]{2,1,0:T(8,128)(2,1)} %copy-done.4, ...), custom_call_target="tpu_custom_call" | custom-call | flops 33554432000 | bytes 20971520 | tf_op jit(solution)/shard_map/backward/pallas_call | solution.py:681
  58.8 0.5 collective-permute-start.10
  59.3 1.7 %collective-permute-start.11 = (bf16[4,32,128]{2,1,0:T(8,128)(2,1)}, bf16[4,32,128]{2,1,0:T(8,128)(2,1)S(1)}, u32[]{:S(2)}, u32[]{:S(2)}) collective-permute-start(bf16[4,32,128]{2,1,0:T(8,128)(2,1)} %get-tuple-element.77), channel_id=1, source_target_pairs={{0,2},{1,3},{2,0},{3,1},{4,6},{5,7},{6,4},{7,5},{8,10},{9,11},{10,... | collective-permute-start | bytes 98312 | tf_op jit(solution)/shard_map/ppermute | solution.py:592
  61.0 0.0 collective-permute-start.12
  61.0 0.0 collective-permute-done.10.refs_1_
  61.0 2.4 %collective-permute-done.11.refs_2_ = bf16[4,32,128]{2,1,0:T(8,128)(2,1)S(1)} collective-permute-done((bf16[4,32,128]{2,1,0:T(8,128)(2,1)}, bf16[4,32,128]{2,1,0:T(8,128)(2,1)S(1)}, u32[]{:S(2)}, u32[]{:S(2)}) %collective-permute-start.11) | collective-permute-done | bytes 32800 | tf_op jit(solution)/shard_map/ppermute | solution.py:592
  63.4 1.5 %collective-permute-done.12.refs_3_ = bf16[4,32,128]{2,1,0:T(8,128)(2,1)S(1)} collective-permute-done((bf16[4,32,128]{2,1,0:T(8,128)(2,1)}, bf16[4,32,128]{2,1,0:T(8,128)(2,1)S(1)}, u32[]{:S(2)}, u32[]{:S(2)}) %collective-permute-start.12) | collective-permute-done | bytes 32800 | tf_op jit(solution)/shard_map/ppermute | solution.py:592
  64.9 0.0 copy-done
  64.9 0.6 copy-done.2
  65.5 6.4 %finish.1 = bf16[8,32,16,128]{3,2,1,0:T(8,128)(2,1)} custom-call(s32[8]{0:T(128)} %offsets.3, bf16[4,32,128]{2,1,0:T(8,128)(2,1)} %get-tuple-element.75.refs_0_, bf16[4,32,128]{2,1,0:T(8,128)(2,1)} %copy-done, bf16[4,32,128]{2,1,0:T(8,128)(2,1)} %copy-done.1, bf16[4,32,128]{2,1,0:T(8,128)(2,1)} %copy-done.2, f32[32,128,128]{2,1,0:T(8,128)} %get-tuple-element.79.refs_4_, ...), custom_call_target="tpu_custom_call" | custom-call | tf_op jit(solution)/shard_map/finish/pallas_call | solution.py:712
  71.8 31.2 %all_to_all.5 = bf16[32,8,16,128]{3,2,1,0:T(8,128)(2,1)} all-to-all(bf16[32,8,16,128]{3,2,1,0:T(8,128)(2,1)} %bitcast.17), channel_id=1, replica_groups=mesh['state'=8,'tile'=4] {'state','tile'}, dimensions={0} | all-to-all | bytes 2097152 | tf_op jit(solution)/shard_map/all_to_all | solution.py:740
  103.1 4.2 %place.1 = f32[4,16,2,16,128]{4,3,2,1,0:T(8,128)} custom-call(s32[8]{0:T(128)} %offsets.3, bf16[8,2,16,16,128]{4,3,2,1,0:T(8,128)(2,1)} %bitcast.18), custom_call_target="tpu_custom_call" | custom-call | tf_op jit(solution)/shard_map/place/pallas_call | solution.py:753
  (14 shorter events, 0.0 us)
Async XLA Ops:
  1.1 9.0 %collective-permute-start.3 = (bf16[32,64,128]{2,1,0:T(8,128)(2,1)S(1)}, bf16[32,64,128]{2,1,0:T(8,128)(2,1)S(1)}, u32[]{:S(2)}, u32[]{:S(2)}) collective-permute-start(bf16[32,64,128]{2,1,0:T(8,128)(2,1)S(1)} %bitcast.22), channel_id=1, source_target_pairs={{0,1},{1,0},{2,3},{3,2},{4,5},{5,4},{6,7},{7,6},{8,9},{9,8},{10,11... | collective-permute-start | bytes 1572872 | tf_op jit(solution)/shard_map/ppermute | solution.py:535
  5.3 12.1 %collective-permute-start.2 = (f32[160,128]{1,0:T(8,128)}, f32[160,128]{1,0:T(8,128)S(1)}, u32[]{:S(2)}, u32[]{:S(2)}) collective-permute-start(f32[160,128]{1,0:T(8,128)} %bias.1.refs_0_), channel_id=1, source_target_pairs={{0,3},{1,2},{2,1},{3,0},{4,7},{5,6},{6,5},{7,4},{8,11},{9,10},{10,... | collective-permute-start | bytes 245768 | tf_op jit(solution)/shard_map/ppermute | solution.py:592
  7.9 9.5 %collective-permute-start.1 = (f32[160,128]{1,0:T(8,128)}, f32[160,128]{1,0:T(8,128)S(1)}, u32[]{:S(2)}, u32[]{:S(2)}) collective-permute-start(f32[160,128]{1,0:T(8,128)} %bias.1.refs_0_), channel_id=1, source_target_pairs={{0,2},{1,3},{2,0},{3,1},{4,6},{5,7},{6,4},{7,5},{8,10},{9,11},{10,... | collective-permute-start | bytes 245768 | tf_op jit(solution)/shard_map/ppermute | solution.py:592
  7.9 9.5 %collective-permute-start = (f32[160,128]{1,0:T(8,128)}, f32[160,128]{1,0:T(8,128)S(1)}, u32[]{:S(2)}, u32[]{:S(2)}) collective-permute-start(f32[160,128]{1,0:T(8,128)} %bias.1.refs_0_), channel_id=1, source_target_pairs={{0,1},{1,0},{2,3},{3,2},{4,5},{5,4},{6,7},{7,6},{8,9},{9,8},{10,11... | collective-permute-start | bytes 245768 | tf_op jit(solution)/shard_map/ppermute | solution.py:592
  10.1 0.8 copy-start.3
  17.4 0.6 copy-start.10
  17.4 0.7 copy-start.11
  17.4 0.7 copy-start.12
  24.9 11.5 %collective-permute-start.4 = (bf16[32,16,128]{2,1,0:T(8,128)(2,1)}, bf16[32,16,128]{2,1,0:T(8,128)(2,1)S(1)}, u32[]{:S(2)}, u32[]{:S(2)}) collective-permute-start(bf16[32,16,128]{2,1,0:T(8,128)(2,1)} %get-tuple-element.55), channel_id=1, source_target_pairs={{0,1},{1,0},{2,3},{3,2},{4,5},{5,4},{6,7},{7,6},{8,9},{9,8},{10,11... | collective-permute-start | bytes 393224 | tf_op jit(solution)/shard_map/ppermute | solution.py:592
  25.4 11.1 %collective-permute-start.5 = (bf16[32,16,128]{2,1,0:T(8,128)(2,1)}, bf16[32,16,128]{2,1,0:T(8,128)(2,1)S(1)}, u32[]{:S(2)}, u32[]{:S(2)}) collective-permute-start(bf16[32,16,128]{2,1,0:T(8,128)(2,1)} %get-tuple-element.56), channel_id=1, source_target_pairs={{0,2},{1,3},{2,0},{3,1},{4,6},{5,7},{6,4},{7,5},{8,10},{9,11},{10,... | collective-permute-start | bytes 393224 | tf_op jit(solution)/shard_map/ppermute | solution.py:592
  27.4 9.1 %collective-permute-start.6 = (bf16[32,16,128]{2,1,0:T(8,128)(2,1)}, bf16[32,16,128]{2,1,0:T(8,128)(2,1)S(1)}, u32[]{:S(2)}, u32[]{:S(2)}) collective-permute-start(bf16[32,16,128]{2,1,0:T(8,128)(2,1)} %get-tuple-element.57), channel_id=1, source_target_pairs={{0,3},{1,2},{2,1},{3,0},{4,7},{5,6},{6,5},{7,4},{8,11},{9,10},{10,... | collective-permute-start | bytes 393224 | tf_op jit(solution)/shard_map/ppermute | solution.py:592
  34.2 2.3 %collective-permute-start.7 = (bf16[32,16,128]{2,1,0:T(8,128)(2,1)}, bf16[32,16,128]{2,1,0:T(8,128)(2,1)S(1)}, u32[]{:S(2)}, u32[]{:S(2)}) collective-permute-start(bf16[32,16,128]{2,1,0:T(8,128)(2,1)} %get-tuple-element.63), channel_id=1, source_target_pairs={{0,1},{1,0},{2,3},{3,2},{4,5},{5,4},{6,7},{7,6},{8,9},{9,8},{10,11... | collective-permute-start | bytes 393224 | tf_op jit(solution)/shard_map/ppermute | solution.py:592
  34.4 6.6 %collective-permute-start.8 = (bf16[32,16,128]{2,1,0:T(8,128)(2,1)}, bf16[32,16,128]{2,1,0:T(8,128)(2,1)S(1)}, u32[]{:S(2)}, u32[]{:S(2)}) collective-permute-start(bf16[32,16,128]{2,1,0:T(8,128)(2,1)} %get-tuple-element.64), channel_id=1, source_target_pairs={{0,2},{1,3},{2,0},{3,1},{4,6},{5,7},{6,4},{7,5},{8,10},{9,11},{10,... | collective-permute-start | bytes 393224 | tf_op jit(solution)/shard_map/ppermute | solution.py:592
  36.4 6.2 %copy-start.4 = (bf16[32,16,128]{2,1,0:T(8,128)(2,1)}, bf16[32,16,128]{2,1,0:T(8,128)(2,1)S(1)}, u32[]{:S(2)}) copy-start(bf16[32,16,128]{2,1,0:T(8,128)(2,1)S(1)} %collective-permute-done.4.refs_1_) | copy-start | bytes 393220
  36.4 6.2 %collective-permute-start.9 = (bf16[32,16,128]{2,1,0:T(8,128)(2,1)}, bf16[32,16,128]{2,1,0:T(8,128)(2,1)S(1)}, u32[]{:S(2)}, u32[]{:S(2)}) collective-permute-start(bf16[32,16,128]{2,1,0:T(8,128)(2,1)} %get-tuple-element.65), channel_id=1, source_target_pairs={{0,3},{1,2},{2,1},{3,0},{4,7},{5,6},{6,5},{7,4},{8,11},{9,10},{10,... | collective-permute-start | bytes 393224 | tf_op jit(solution)/shard_map/ppermute | solution.py:592
  36.5 6.2 %copy-start.5 = (bf16[32,16,128]{2,1,0:T(8,128)(2,1)}, bf16[32,16,128]{2,1,0:T(8,128)(2,1)S(1)}, u32[]{:S(2)}) copy-start(bf16[32,16,128]{2,1,0:T(8,128)(2,1)S(1)} %collective-permute-done.5.refs_2_) | copy-start | bytes 393220
  36.5 6.2 %copy-start.6 = (bf16[32,16,128]{2,1,0:T(8,128)(2,1)}, bf16[32,16,128]{2,1,0:T(8,128)(2,1)S(1)}, u32[]{:S(2)}) copy-start(bf16[32,16,128]{2,1,0:T(8,128)(2,1)S(1)} %collective-permute-done.6.refs_3_) | copy-start | bytes 393220
  36.5 6.2 %copy-start.7 = (bf16[32,16,128]{2,1,0:T(8,128)(2,1)}, bf16[32,16,128]{2,1,0:T(8,128)(2,1)S(1)}, u32[]{:S(2)}) copy-start(bf16[32,16,128]{2,1,0:T(8,128)(2,1)S(1)} %collective-permute-done.7.refs_5_) | copy-start | bytes 393220
  41.0 1.7 %copy-start.8 = (bf16[32,16,128]{2,1,0:T(8,128)(2,1)}, bf16[32,16,128]{2,1,0:T(8,128)(2,1)S(1)}, u32[]{:S(2)}) copy-start(bf16[32,16,128]{2,1,0:T(8,128)(2,1)S(1)} %collective-permute-done.8.refs_6_) | copy-start | bytes 393220
  42.7 0.6 copy-start.9
  58.8 2.2 %collective-permute-start.10 = (bf16[4,32,128]{2,1,0:T(8,128)(2,1)}, bf16[4,32,128]{2,1,0:T(8,128)(2,1)S(1)}, u32[]{:S(2)}, u32[]{:S(2)}) collective-permute-start(bf16[4,32,128]{2,1,0:T(8,128)(2,1)} %get-tuple-element.76), channel_id=1, source_target_pairs={{0,1},{1,0},{2,3},{3,2},{4,5},{5,4},{6,7},{7,6},{8,9},{9,8},{10,11... | collective-permute-start | bytes 98312 | tf_op jit(solution)/shard_map/ppermute | solution.py:592
  59.3 4.1 %collective-permute-start.11 = (bf16[4,32,128]{2,1,0:T(8,128)(2,1)}, bf16[4,32,128]{2,1,0:T(8,128)(2,1)S(1)}, u32[]{:S(2)}, u32[]{:S(2)}) collective-permute-start(bf16[4,32,128]{2,1,0:T(8,128)(2,1)} %get-tuple-element.77), channel_id=1, source_target_pairs={{0,2},{1,3},{2,0},{3,1},{4,6},{5,7},{6,4},{7,5},{8,10},{9,11},{10,... | collective-permute-start | bytes 98312 | tf_op jit(solution)/shard_map/ppermute | solution.py:592
  61.0 3.9 %collective-permute-start.12 = (bf16[4,32,128]{2,1,0:T(8,128)(2,1)}, bf16[4,32,128]{2,1,0:T(8,128)(2,1)S(1)}, u32[]{:S(2)}, u32[]{:S(2)}) collective-permute-start(bf16[4,32,128]{2,1,0:T(8,128)(2,1)} %get-tuple-element.78), channel_id=1, source_target_pairs={{0,3},{1,2},{2,1},{3,0},{4,7},{5,6},{6,5},{7,4},{8,11},{9,10},{10,... | collective-permute-start | bytes 98312 | tf_op jit(solution)/shard_map/ppermute | solution.py:592
  61.0 3.9 %copy-start = (bf16[4,32,128]{2,1,0:T(8,128)(2,1)}, bf16[4,32,128]{2,1,0:T(8,128)(2,1)S(1)}, u32[]{:S(2)}) copy-start(bf16[4,32,128]{2,1,0:T(8,128)(2,1)S(1)} %collective-permute-done.10.refs_1_) | copy-start | bytes 98308
  63.4 1.5 %copy-start.1 = (bf16[4,32,128]{2,1,0:T(8,128)(2,1)}, bf16[4,32,128]{2,1,0:T(8,128)(2,1)S(1)}, u32[]{:S(2)}) copy-start(bf16[4,32,128]{2,1,0:T(8,128)(2,1)S(1)} %collective-permute-done.11.refs_2_) | copy-start | bytes 98308
  64.9 0.6 copy-start.2

commit v5 on v4

--- a/solution.py
+++ b/solution.py
@@ -8,6 +8,7 @@
 from jax.experimental.pallas import tpu as pltpu
 from jax.sharding import PartitionSpec as P
 
+VMEM_BYTES = 16 << 20
 H = 4
 HD = 32
 NB = 64
@@ -549,7 +550,8 @@
         ((chans, 4 * H), BF),
     )
     w4t, w2, wod, wdt, wd3, wall, gbc, lgc, cst, wgs = pl.pallas_call(
-        prep_kernel, out_shape=prep_shapes, name="prep"
+        prep_kernel, out_shape=prep_shapes, name="prep",
+        compiler_params=pltpu.CompilerParams(vmem_limit_bytes=VMEM_BYTES)
     )(
         w_query,
         w_key,
@@ -580,6 +582,7 @@
         out_specs=full((bias_rows + target_rows, wide)),
         out_shape=jax.ShapeDtypeStruct((bias_rows + target_rows, wide), F32),
         name="bias",
+        compiler_params=pltpu.CompilerParams(vmem_limit_bytes=VMEM_BYTES),
     )(
         pair_tiles.reshape(grid_side, per_head, side, chans),
         targets.reshape(target_rows, wide),
@@ -619,6 +622,7 @@
         out_shape=shapes(*([square_b] * 6), ((share, width, wide), F32)),
         cost_estimate=cost(80 * share * cell, 12 * share * wide * width * 2),
         name="project",
+        compiler_params=pltpu.CompilerParams(vmem_limit_bytes=VMEM_BYTES),
     )(tile_j.reshape(1), *parts, gain_row, shift_row, w4t, w2, gbc)
 
     chunks = 2 if groups % 2 == 0 else 1
@@ -672,6 +676,7 @@
             input_output_aliases={first + n: n for n in range(len(saved))},
             cost_estimate=cost(150 * count * cell, 14 * count * wide * width * 2),
             name="forward",
+        compiler_params=pltpu.CompilerParams(vmem_limit_bytes=VMEM_BYTES),
         )
         results = call(*inputs, *saved)
         saved = list(results[:4])
@@ -701,6 +706,7 @@
         ],
         cost_estimate=cost(500 * share * cell, 20 * share * wide * width * 2),
         name="backward",
+        compiler_params=pltpu.CompilerParams(vmem_limit_bytes=VMEM_BYTES),
     )(
         *[part for parts_c in mirrored for part in parts_c],
         tgt, at, ot, ut, gt, vn, kt, qt, w_output, wd3, wall, cst,
@@ -727,6 +733,7 @@
         ),
         out_shape=jax.ShapeDtypeStruct((states, share, piece, chans), BF),
         name="finish",
+        compiler_params=pltpu.CompilerParams(vmem_limit_bytes=VMEM_BYTES),
     )(offsets, *rdb, dpt, dzn, zr, wgs, lgc)
 
     if even:
@@ -766,6 +773,7 @@
         ),
         out_shape=jax.ShapeDtypeStruct(out_shape, F32),
         name="place",
+        compiler_params=pltpu.CompilerParams(vmem_limit_bytes=VMEM_BYTES),
     )(offsets, received)
     return placed.reshape(2 * grid_side, 1, owner_rows, 2, piece, chans)
 

time: 108 us -> 92.1 us (0.85)
  Pallas kernels: 51.9 us -> 31.8 us
  local copies, waits for them, and re-layouts: 3.8 us -> 8.91 us
    pallas_call x2, Pallas kernels: 13.6 us -> 8.36 us  [on_device(): results = call(*inputs, *saved)]
    unnamed x26 -> x38, local copies, waits for them, and re-layouts: 2.73 us -> 7.75 us
    pallas_call x1, Pallas kernels: 15.5 us -> 12.2 us  [on_device(): pl.pallas_call(functools.partial(backward_kernel, tiles=tiles, chunks=chu...]
    pallas_call x1, Pallas kernels: 6.36 us -> 3.31 us  [on_device(): pl.pallas_call(functools.partial(finish_kernel, tiles=tiles), grid_spec=p...]
    pallas_call x1, Pallas kernels: 6.48 us -> 3.64 us  [on_device(): pl.pallas_call(functools.partial(project_kernel, parts=grid_side), grid_s...]
    pallas_call x1, Pallas kernels: 3.65 us -> 1.53 us  [on_device(): pl.pallas_call(functools.partial(bias_kernel, per_head=per_head), grid=(p...]
    pallas_call x1, Pallas kernels: 4.16 us -> 2.31 us  [on_device(): pl.pallas_call(functools.partial(place_kernel, side=side), grid_spec=pltp...]
    pallas_call x1, Pallas kernels: 2.06 us -> 0.43 us  [on_device(): pl.pallas_call(prep_kernel, out_shape=prep_shapes, name='prep', compiler_...]
  transfers between devices with their start and end apart: 13 -> 13, of which waited for: 4 -> 4; matrix products, arithmetic and copies ran while one was open for 0% -> 0% of each run, Pallas kernels for 18% -> 11%
where the time goes in v5:
time: 92.1 us; the launch traced here: 91.5 us
  Pallas kernels  31.8 us (35%)
  blocking collectives  30.9 us (34%)
  starting transfers between devices  10 us (11%)
  waiting for transfers between devices  9.66 us (10%)
  local copies, waits for them, and re-layouts  8.91 us (10%)
    all_to_all x1, blocking collectives, on_device(): lax.all_to_all(slots, ('state', 'tile'), split_axis=0, concat_axis=0, til...  30.9 us
    pallas_call x1, Pallas kernels, on_device(): pl.pallas_call(functools.partial(backward_kernel, tiles=tiles, chunks=chu...  12.2 us
    ppermute x12, waiting for transfers between devices, to_partner(): lax.ppermute(value, 'tile', [(t, t ^ k) for t in range(tiles)])  9.66 us
    ppermute x12, starting transfers between devices, to_partner(): lax.ppermute(value, 'tile', [(t, t ^ k) for t in range(tiles)])  9.44 us
    pallas_call x2, Pallas kernels, on_device(): results = call(*inputs, *saved)  8.36 us
    unnamed x38, local copies, waits for them, and re-layouts  7.75 us
    pallas_call x1, Pallas kernels, on_device(): pl.pallas_call(functools.partial(project_kernel, parts=grid_side), grid_s...  3.64 us
    pallas_call x1, Pallas kernels, on_device(): pl.pallas_call(functools.partial(finish_kernel, tiles=tiles), grid_spec=p...  3.31 us
  transfers between devices with their start and end apart: 13, of which 4 were waited for; matrix products, arithmetic and copies ran while one was open for 0% of the time, Pallas kernels for 11%

profile of v5, /device:TPU:0, one launch (start us, length us, event | category | flops | bytes accessed | tf_op | source)
XLA Modules:
  0.0 91.5 jit_solution(15429660521182871977)
XLA Ops:
  0.0 1.2 %constant_dynamic-slice_fusion = bf16[4,1,8,64,128]{4,3,2,1,0:T(8,128)(2,1)S(1)} fusion(bf16[4,2,8,64,128]{4,3,2,1,0:T(8,128)(2,1)} %bitcast.19, s32[]{:T(128)S(6)} %select_n.4), kind=kLoop, calls=%fused_computation | loop fusion | bytes 1048580 | tf_op jit(solution)/shard_map/jit(dynamic_index_in_dim)/dynamic_slice | solution.py:527
  1.2 0.6 collective-permute-start.3
  1.8 1.2 %copy-done = bf16[1,1,64,64,128]{4,3,2,1,0:T(8,128)(2,1)S(1)} copy-done((bf16[1,1,64,64,128]{4,3,2,1,0:T(8,128)(2,1)S(1)}, bf16[1,1,64,64,128]{4,3,2,1,0:T(8,128)(2,1)}, u32[]{:S(2)}) %copy-start) | copy-done | bytes 1048600
  3.0 0.7 copy-done.9
  3.7 0.7 copy-done.10
  4.4 0.7 copy-done.11
  5.1 0.7 copy-done.17
  5.7 1.5 %bias.1.refs_0_ = f32[160,128]{1,0:T(8,128)S(1)} custom-call(bf16[2,32,64,128]{3,2,1,0:T(8,128)(2,1)S(1)} %bitcast.20, s32[32,128]{1,0:T(8,128)S(1)} %bitcast.23, f32[1,128]{1,0:T(1,128)S(1)} %bitcast.26, f32[1,128]{1,0:T(1,128)S(1)} %bitcast.32, f32[4,128]{1,0:T(4,128)S(1)} %bitcast.24), custom_call_target="tpu_custom_call" | custom-call | tf_op jit(solution)/shard_map/bias/pallas_call | solution.py:572
  7.3 2.7 %collective-permute-start.2 = (f32[160,128]{1,0:T(8,128)S(1)}, f32[160,128]{1,0:T(8,128)S(1)}, u32[]{:S(2)}, u32[]{:S(2)}) collective-permute-start(f32[160,128]{1,0:T(8,128)S(1)} %bias.1.refs_0_), channel_id=1, source_target_pairs={{0,3},{1,2},{2,1},{3,0},{4,7},{5,6},{6,5},{7,4},{8,11},{9,10},{10,... | collective-permute-start | bytes 245768 | tf_op jit(solution)/shard_map/ppermute | solution.py:595
  9.9 0.0 collective-permute-start.1
  9.9 0.2 collective-permute-start
  10.1 0.0 copy-start.3
  10.1 0.7 copy-done.3
  10.9 0.8 copy-done.4
  11.6 0.8 copy-done.5
  12.4 0.8 copy-done.6
  13.2 0.8 copy-done.7
  13.9 0.4 prep.1
  14.4 0.0 collective-permute-done.3.refs_1_
  14.4 0.0 copy-done.1
  14.4 3.6 %project.1 = (bf16[32,128,128]{2,1,0:T(8,128)(2,1)S(1)}, bf16[32,128,128]{2,1,0:T(8,128)(2,1)S(1)}, bf16[32,128,128]{2,1,0:T(8,128)(2,1)S(1)}, bf16[32,128,128]{...) custom-call(s32[1]{0:T(128)} %bitcast.5.own_ref, ...), custom_call_target="tpu_custom_call" | custom-call | flops 5368709120 | bytes 12582912 | tf_op jit(solution)/shard_map/project/pallas_call | solution.py:607
  18.1 0.0 collective-permute-done.2.refs_3_
  18.1 0.0 collective-permute-done.1.refs_2_
  18.1 0.0 collective-permute-done.refs_1_
  18.1 4.2 %forward.2 = (bf16[32,128,512]{2,1,0:T(8,128)(2,1)S(1)}, f32[32,128,128]{2,1,0:T(8,128)S(1)}, f32[32,64,128]{2,1,0:T(8,128)S(1)}, f32[32,128]{1,0:T(8,128)S(1)},...) custom-call(f32[160,128]{1,0:T(8,128)S(1)} %bias.1.refs_0_, ...), custom_call_target="tpu_custom_call" | custom-call | flops 5033164800 | bytes 7340032 | tf_op jit(solution)/shard_map/forward/pallas_call | solution.py:681
  22.3 0.3 collective-permute-start.4
  22.6 2.0 %collective-permute-start.5 = (bf16[32,16,128]{2,1,0:T(8,128)(2,1)S(1)}, bf16[32,16,128]{2,1,0:T(8,128)(2,1)S(1)}, u32[]{:S(2)}, u32[]{:S(2)}) collective-permute-start(bf16[32,16,128]{2,1,0:T(8,128)(2,1)S(1)} %get-tuple-element.56), channel_id=1, source_target_pairs={{0,2},{1,3},{2,0},{3,1},{4,6},{5,7},{6,4},{7,5},{8,10},{9,11},{10,... | collective-permute-start | bytes 393224 | tf_op jit(solution)/shard_map/ppermute | solution.py:595
  24.6 0.0 collective-permute-start.6
  24.6 4.2 %forward.3 = (bf16[32,128,512]{2,1,0:T(8,128)(2,1)S(1)}, f32[32,128,128]{2,1,0:T(8,128)S(1)}, f32[32,64,128]{2,1,0:T(8,128)S(1)}, f32[32,128]{1,0:T(8,128)S(1)},...) custom-call(f32[160,128]{1,0:T(8,128)S(1)} %bias.1.refs_0_, ...), custom_call_target="tpu_custom_call", output_to_operand_aliasing={{0}: (11, {}), {1}: (12, {}), {2}: (13, {}), {3}: (14, {})} | custom-call | flops 5033164800 | bytes 7340032 | tf_op jit(solution)/shard_map/forward/pallas_call | solution.py:681
  28.8 0.1 collective-permute-start.7
  28.9 2.0 %collective-permute-start.8 = (bf16[32,16,128]{2,1,0:T(8,128)(2,1)S(1)}, bf16[32,16,128]{2,1,0:T(8,128)(2,1)S(1)}, u32[]{:S(2)}, u32[]{:S(2)}) collective-permute-start(bf16[32,16,128]{2,1,0:T(8,128)(2,1)S(1)} %get-tuple-element.64), channel_id=1, source_target_pairs={{0,2},{1,3},{2,0},{3,1},{4,6},{5,7},{6,4},{7,5},{8,10},{9,11},{10,... | collective-permute-start | bytes 393224 | tf_op jit(solution)/shard_map/ppermute | solution.py:595
  30.9 0.0 collective-permute-done.4.refs_1_
  30.9 0.0 collective-permute-start.9
  30.9 0.0 collective-permute-done.5.refs_2_
  31.0 0.0 collective-permute-done.6.refs_3_
  31.0 0.0 collective-permute-done.7.refs_5_
  31.0 4.3 %collective-permute-done.8.refs_6_ = bf16[32,16,128]{2,1,0:T(8,128)(2,1)S(1)} collective-permute-done((bf16[32,16,128]{2,1,0:T(8,128)(2,1)S(1)}, bf16[32,16,128]{2,1,0:T(8,128)(2,1)S(1)}, u32[]{:S(2)}, u32[]{:S(2)}) %collective-permute-start.8) | collective-permute-done | bytes 131104 | tf_op jit(solution)/shard_map/ppermute | solution.py:595
  35.3 1.7 %collective-permute-done.9.refs_7_ = bf16[32,16,128]{2,1,0:T(8,128)(2,1)S(1)} collective-permute-done((bf16[32,16,128]{2,1,0:T(8,128)(2,1)S(1)}, bf16[32,16,128]{2,1,0:T(8,128)(2,1)S(1)}, u32[]{:S(2)}, u32[]{:S(2)}) %collective-permute-start.9) | collective-permute-done | bytes 131104 | tf_op jit(solution)/shard_map/ppermute | solution.py:595
  37.0 12.2 %backward.1 = (f32[32,128,128]{2,1,0:T(8,128)S(1)}, f32[32,128,128]{2,1,0:T(8,128)S(1)}, bf16[4,32,128]{2,1,0:T(8,128)(2,1)S(1)}, bf16[4,32,128]{2,1,0:T(8,128)(...) custom-call(bf16[32,16,128]{2,1,0:T(8,128)(2,1)S(1)} %get-tuple-element.54.refs_0_, ...), custom_call_target="tpu_custom_call" | custom-call | flops 33554432000 | bytes 20971520 | tf_op jit(solution)/shard_map/backward/pallas_call | solution.py:686
  49.2 0.5 collective-permute-start.10
  49.6 1.6 %collective-permute-start.11 = (bf16[4,32,128]{2,1,0:T(8,128)(2,1)S(1)}, bf16[4,32,128]{2,1,0:T(8,128)(2,1)S(1)}, u32[]{:S(2)}, u32[]{:S(2)}) collective-permute-start(bf16[4,32,128]{2,1,0:T(8,128)(2,1)S(1)} %get-tuple-element.77), channel_id=1, source_target_pairs={{0,2},{1,3},{2,0},{3,1},{4,6},{5,7},{6,4},{7,5},{8,10},{9,11},{10,... | collective-permute-start | bytes 98312 | tf_op jit(solution)/shard_map/ppermute | solution.py:595
  51.3 0.0 collective-permute-start.12
  51.3 0.0 collective-permute-done.10.refs_1_
  51.3 2.3 %collective-permute-done.11.refs_2_ = bf16[4,32,128]{2,1,0:T(8,128)(2,1)S(1)} collective-permute-done((bf16[4,32,128]{2,1,0:T(8,128)(2,1)S(1)}, bf16[4,32,128]{2,1,0:T(8,128)(2,1)S(1)}, u32[]{:S(2)}, u32[]{:S(2)}) %collective-permute-start.11) | collective-permute-done | bytes 32800 | tf_op jit(solution)/shard_map/ppermute | solution.py:595
  53.6 1.4 %collective-permute-done.12.refs_3_ = bf16[4,32,128]{2,1,0:T(8,128)(2,1)S(1)} collective-permute-done((bf16[4,32,128]{2,1,0:T(8,128)(2,1)S(1)}, bf16[4,32,128]{2,1,0:T(8,128)(2,1)S(1)}, u32[]{:S(2)}, u32[]{:S(2)}) %collective-permute-start.12) | collective-permute-done | bytes 32800 | tf_op jit(solution)/shard_map/ppermute | solution.py:595
  55.0 3.3 %finish.1 = bf16[8,32,16,128]{3,2,1,0:T(8,128)(2,1)S(1)} custom-call(s32[8]{0:T(128)S(1)} %copy-done.13, bf16[4,32,128]{2,1,0:T(8,128)(2,1)S(1)} %get-tuple-element.75.refs_0_, bf16[4,32,128]{2,1,0:T(8,128)(2,1)S(1)} %collective-permute-done.10.refs_1_, bf16[4,32,128]{2,1,0:T(8,128)(2,1)S(1)} %collective-permute-done.11.refs_2_, ...), custom_call_target="tpu_custom_call" | custom-call | tf_op jit(solution)/shard_map/finish/pallas_call | solution.py:718
  58.3 30.9 %all_to_all.5 = bf16[32,8,16,128]{3,2,1,0:T(8,128)(2,1)S(1)} all-to-all(bf16[32,8,16,128]{3,2,1,0:T(8,128)(2,1)S(1)} %bitcast.17), channel_id=1, replica_groups=mesh['state'=8,'tile'=4] {'state','tile'}, dimensions={0} | all-to-all | bytes 2097152 | tf_op jit(solution)/shard_map/all_to_all | solution.py:747
  89.2 2.3 %place.1 = f32[4,16,2,16,128]{4,3,2,1,0:T(8,128)} custom-call(s32[8]{0:T(128)S(1)} %copy-done.13, bf16[8,2,16,16,128]{4,3,2,1,0:T(8,128)(2,1)S(1)} %bitcast.18), custom_call_target="tpu_custom_call" | custom-call | tf_op jit(solution)/shard_map/place/pallas_call | solution.py:760
  (26 shorter events, 0.0 us)
Async XLA Ops:
  0.0 14.4 %copy-start.1 = (bf16[1,1,64,64,128]{4,3,2,1,0:T(8,128)(2,1)S(1)}, bf16[1,1,64,64,128]{4,3,2,1,0:T(8,128)(2,1)}, u32[]{:S(2)}) copy-start(bf16[1,1,64,64,128]{4,3,2,1,0:T(8,128)(2,1)} %param.15) | copy-start | bytes 3145732
  0.0 14.4 %copy-start.18 = (f32[128]{0:T(128)S(1)}, f32[128]{0:T(128)}, u32[]{:S(2)}) copy-start(f32[128]{0:T(128)} %param.19) | copy-start | bytes 1540
  0.0 14.4 %copy-start.12 = (f32[128]{0:T(128)S(1)}, f32[128]{0:T(128)}, u32[]{:S(2)}) copy-start(f32[128]{0:T(128)} %param.18) | copy-start | bytes 1540
  0.0 10.1 %copy-start.16 = (f32[64]{0:T(128)S(1)}, f32[64]{0:T(128)}, u32[]{:S(2)}) copy-start(f32[64]{0:T(128)} %param.29) | copy-start | bytes 772
  0.0 10.1 %copy-start.15 = (f32[128]{0:T(128)S(1)}, f32[128]{0:T(128)}, u32[]{:S(2)}) copy-start(f32[128]{0:T(128)} %param.27) | copy-start | bytes 1540
  0.0 10.1 %copy-start.14 = (f32[128]{0:T(128)S(1)}, f32[128]{0:T(128)}, u32[]{:S(2)}) copy-start(f32[128]{0:T(128)} %param.25) | copy-start | bytes 1540
  0.0 10.1 %copy-start.2 = (bf16[128,128]{1,0:T(8,128)(2,1)S(1)}, bf16[128,128]{1,0:T(8,128)(2,1)}, u32[]{:S(2)}) copy-start(bf16[128,128]{1,0:T(8,128)(2,1)} %wq.1) | copy-start | bytes 98308
  1.2 13.2 %collective-permute-start.3 = (bf16[32,64,128]{2,1,0:T(8,128)(2,1)S(1)}, bf16[32,64,128]{2,1,0:T(8,128)(2,1)S(1)}, u32[]{:S(2)}, u32[]{:S(2)}) collective-permute-start(bf16[32,64,128]{2,1,0:T(8,128)(2,1)S(1)} %bitcast.34), channel_id=1, source_target_pairs={{0,1},{1,0},{2,3},{3,2},{4,5},{5,4},{6,7},{7,6},{8,9},{9,8},{10,11... | collective-permute-start | bytes 1572872 | tf_op jit(solution)/shard_map/ppermute | solution.py:536
  1.8 1.2 %copy-start = (bf16[1,1,64,64,128]{4,3,2,1,0:T(8,128)(2,1)S(1)}, bf16[1,1,64,64,128]{4,3,2,1,0:T(8,128)(2,1)}, u32[]{:S(2)}) copy-start(bf16[1,1,64,64,128]{4,3,2,1,0:T(8,128)(2,1)} %param.15) | copy-start | bytes 3145732
  3.0 0.7 copy-start.9
  3.7 0.7 copy-start.10
  4.4 0.7 copy-start.11
  5.1 0.7 copy-start.17
  7.3 10.8 %collective-permute-start.2 = (f32[160,128]{1,0:T(8,128)S(1)}, f32[160,128]{1,0:T(8,128)S(1)}, u32[]{:S(2)}, u32[]{:S(2)}) collective-permute-start(f32[160,128]{1,0:T(8,128)S(1)} %bias.1.refs_0_), channel_id=1, source_target_pairs={{0,3},{1,2},{2,1},{3,0},{4,7},{5,6},{6,5},{7,4},{8,11},{9,10},{10,... | collective-permute-start | bytes 245768 | tf_op jit(solution)/shard_map/ppermute | solution.py:595
  9.9 8.1 %collective-permute-start.1 = (f32[160,128]{1,0:T(8,128)S(1)}, f32[160,128]{1,0:T(8,128)S(1)}, u32[]{:S(2)}, u32[]{:S(2)}) collective-permute-start(f32[160,128]{1,0:T(8,128)S(1)} %bias.1.refs_0_), channel_id=1, source_target_pairs={{0,2},{1,3},{2,0},{3,1},{4,6},{5,7},{6,4},{7,5},{8,10},{9,11},{10,... | collective-permute-start | bytes 245768 | tf_op jit(solution)/shard_map/ppermute | solution.py:595
  9.9 8.2 %collective-permute-start = (f32[160,128]{1,0:T(8,128)S(1)}, f32[160,128]{1,0:T(8,128)S(1)}, u32[]{:S(2)}, u32[]{:S(2)}) collective-permute-start(f32[160,128]{1,0:T(8,128)S(1)} %bias.1.refs_0_), channel_id=1, source_target_pairs={{0,1},{1,0},{2,3},{3,2},{4,5},{5,4},{6,7},{7,6},{8,9},{9,8},{10,11... | collective-permute-start | bytes 245768 | tf_op jit(solution)/shard_map/ppermute | solution.py:595
  10.1 0.8 copy-start.3
  10.9 0.8 copy-start.4
  11.6 0.8 copy-start.5
  12.4 0.8 copy-start.6
  13.2 0.8 copy-start.7
  22.3 8.7 %collective-permute-start.4 = (bf16[32,16,128]{2,1,0:T(8,128)(2,1)S(1)}, bf16[32,16,128]{2,1,0:T(8,128)(2,1)S(1)}, u32[]{:S(2)}, u32[]{:S(2)}) collective-permute-start(bf16[32,16,128]{2,1,0:T(8,128)(2,1)S(1)} %get-tuple-element.55), channel_id=1, source_target_pairs={{0,1},{1,0},{2,3},{3,2},{4,5},{5,4},{6,7},{7,6},{8,9},{9,8},{10,11... | collective-permute-start | bytes 393224 | tf_op jit(solution)/shard_map/ppermute | solution.py:595
  22.6 8.3 %collective-permute-start.5 = (bf16[32,16,128]{2,1,0:T(8,128)(2,1)S(1)}, bf16[32,16,128]{2,1,0:T(8,128)(2,1)S(1)}, u32[]{:S(2)}, u32[]{:S(2)}) collective-permute-start(bf16[32,16,128]{2,1,0:T(8,128)(2,1)S(1)} %get-tuple-element.56), channel_id=1, source_target_pairs={{0,2},{1,3},{2,0},{3,1},{4,6},{5,7},{6,4},{7,5},{8,10},{9,11},{10,... | collective-permute-start | bytes 393224 | tf_op jit(solution)/shard_map/ppermute | solution.py:595
  24.6 6.3 %collective-permute-start.6 = (bf16[32,16,128]{2,1,0:T(8,128)(2,1)S(1)}, bf16[32,16,128]{2,1,0:T(8,128)(2,1)S(1)}, u32[]{:S(2)}, u32[]{:S(2)}) collective-permute-start(bf16[32,16,128]{2,1,0:T(8,128)(2,1)S(1)} %get-tuple-element.57), channel_id=1, source_target_pairs={{0,3},{1,2},{2,1},{3,0},{4,7},{5,6},{6,5},{7,4},{8,11},{9,10},{10,... | collective-permute-start | bytes 393224 | tf_op jit(solution)/shard_map/ppermute | solution.py:595
  24.6 12.3 %copy-start.8 = (bf16[128,128]{1,0:T(8,128)(2,1)S(1)}, bf16[128,128]{1,0:T(8,128)(2,1)}, u32[]{:S(2)}) copy-start(bf16[128,128]{1,0:T(8,128)(2,1)} %refs_16_.1) | copy-start | bytes 98308
  28.8 2.2 %collective-permute-start.7 = (bf16[32,16,128]{2,1,0:T(8,128)(2,1)S(1)}, bf16[32,16,128]{2,1,0:T(8,128)(2,1)S(1)}, u32[]{:S(2)}, u32[]{:S(2)}) collective-permute-start(bf16[32,16,128]{2,1,0:T(8,128)(2,1)S(1)} %get-tuple-element.63), channel_id=1, source_target_pairs={{0,1},{1,0},{2,3},{3,2},{4,5},{5,4},{6,7},{7,6},{8,9},{9,8},{10,11... | collective-permute-start | bytes 393224 | tf_op jit(solution)/shard_map/ppermute | solution.py:595
  28.9 6.4 %collective-permute-start.8 = (bf16[32,16,128]{2,1,0:T(8,128)(2,1)S(1)}, bf16[32,16,128]{2,1,0:T(8,128)(2,1)S(1)}, u32[]{:S(2)}, u32[]{:S(2)}) collective-permute-start(bf16[32,16,128]{2,1,0:T(8,128)(2,1)S(1)} %get-tuple-element.64), channel_id=1, source_target_pairs={{0,2},{1,3},{2,0},{3,1},{4,6},{5,7},{6,4},{7,5},{8,10},{9,11},{10,... | collective-permute-start | bytes 393224 | tf_op jit(solution)/shard_map/ppermute | solution.py:595
  30.9 6.0 %collective-permute-start.9 = (bf16[32,16,128]{2,1,0:T(8,128)(2,1)S(1)}, bf16[32,16,128]{2,1,0:T(8,128)(2,1)S(1)}, u32[]{:S(2)}, u32[]{:S(2)}) collective-permute-start(bf16[32,16,128]{2,1,0:T(8,128)(2,1)S(1)} %get-tuple-element.65), channel_id=1, source_target_pairs={{0,3},{1,2},{2,1},{3,0},{4,7},{5,6},{6,5},{7,4},{8,11},{9,10},{10,... | collective-permute-start | bytes 393224 | tf_op jit(solution)/shard_map/ppermute | solution.py:595
  37.0 18.0 %copy-start.13 = (s32[8]{0:T(128)S(1)}, s32[8]{0:T(128)}, u32[]{:S(2)}) copy-start(s32[8]{0:T(128)} %offsets.3) | copy-start | bytes 100
  49.2 2.1 %collective-permute-start.10 = (bf16[4,32,128]{2,1,0:T(8,128)(2,1)S(1)}, bf16[4,32,128]{2,1,0:T(8,128)(2,1)S(1)}, u32[]{:S(2)}, u32[]{:S(2)}) collective-permute-start(bf16[4,32,128]{2,1,0:T(8,128)(2,1)S(1)} %get-tuple-element.76), channel_id=1, source_target_pairs={{0,1},{1,0},{2,3},{3,2},{4,5},{5,4},{6,7},{7,6},{8,9},{9,8},{10,11... | collective-permute-start | bytes 98312 | tf_op jit(solution)/shard_map/ppermute | solution.py:595
  49.6 3.9 %collective-permute-start.11 = (bf16[4,32,128]{2,1,0:T(8,128)(2,1)S(1)}, bf16[4,32,128]{2,1,0:T(8,128)(2,1)S(1)}, u32[]{:S(2)}, u32[]{:S(2)}) collective-permute-start(bf16[4,32,128]{2,1,0:T(8,128)(2,1)S(1)} %get-tuple-element.77), channel_id=1, source_target_pairs={{0,2},{1,3},{2,0},{3,1},{4,6},{5,7},{6,4},{7,5},{8,10},{9,11},{10,... | collective-permute-start | bytes 98312 | tf_op jit(solution)/shard_map/ppermute | solution.py:595
  51.3 3.7 %collective-permute-start.12 = (bf16[4,32,128]{2,1,0:T(8,128)(2,1)S(1)}, bf16[4,32,128]{2,1,0:T(8,128)(2,1)S(1)}, u32[]{:S(2)}, u32[]{:S(2)}) collective-permute-start(bf16[4,32,128]{2,1,0:T(8,128)(2,1)S(1)} %get-tuple-element.78), channel_id=1, source_target_pairs={{0,3},{1,2},{2,1},{3,0},{4,7},{5,6},{6,5},{7,4},{8,11},{9,10},{10,... | collective-permute-start | bytes 98312 | tf_op jit(solution)/shard_map/ppermute | solution.py:595

commit v6 on v5

--- a/solution.py
+++ b/solution.py
@@ -518,6 +518,9 @@
     per_head = side * side // wide
     piece = wide // states
 
+    def stay(value):
+        return pltpu.with_memory_space_constraint(value, pltpu.HBM)
+
     def shapes(*pairs):
         return [jax.ShapeDtypeStruct(s, t) for s, t in pairs]
 
@@ -553,17 +556,22 @@
         prep_kernel, out_shape=prep_shapes, name="prep",
         compiler_params=pltpu.CompilerParams(vmem_limit_bytes=VMEM_BYTES)
     )(
-        w_query,
-        w_key,
-        w_value,
-        w_gate,
-        w_output,
-        gate_bias.reshape(1, width),
-        out_bias.reshape(1, chans),
-        w_distogram.T,
-        dist_bias.reshape(1, NB),
-        w_pairbias.T,
-        gain_row,
+        *map(
+            stay,
+            (
+                w_query,
+                w_key,
+                w_value,
+                w_gate,
+                w_output,
+                gate_bias.reshape(1, width),
+                out_bias.reshape(1, chans),
+                w_distogram.T,
+                dist_bias.reshape(1, NB),
+                w_pairbias.T,
+                gain_row,
+            ),
+        )
     )
 
     lines = 8
@@ -584,11 +592,16 @@
         name="bias",
         compiler_params=pltpu.CompilerParams(vmem_limit_bytes=VMEM_BYTES),
     )(
-        pair_tiles.reshape(grid_side, per_head, side, chans),
-        targets.reshape(target_rows, wide),
-        gain_row,
-        shift_row,
-        w_pairbias.T,
+        *map(
+            stay,
+            (
+                pair_tiles.reshape(grid_side, per_head, side, chans),
+                targets.reshape(target_rows, wide),
+                gain_row,
+                shift_row,
+                w_pairbias.T,
+            ),
+        )
     )
 
     def to_partner(value, k):

time: 92.1 us -> 86.4 us (0.938)
  local copies, waits for them, and re-layouts: 8.91 us -> 1.18 us
  Pallas kernels: 31.8 us -> 34.2 us
    unnamed x38 -> x10, local copies, waits for them, and re-layouts: 7.75 us -> 0.02 us
    pallas_call x1, Pallas kernels: 1.53 us -> 3.04 us  [on_device(): pl.pallas_call(functools.partial(bias_kernel, per_head=per_head), grid=(p...]
  transfers between devices with their start and end apart: 13 -> 13, of which waited for: 4 -> 4; matrix products, arithmetic and copies ran while one was open for 0% -> 0% of each run, Pallas kernels for 11% -> 14%
where the time goes in v6:
time: 86.4 us; the launch traced here: 86.2 us
  Pallas kernels  34.2 us (40%)
  blocking collectives  31 us (36%)
  starting transfers between devices  10 us (12%)
  waiting for transfers between devices  9.64 us (11%)
  local copies, waits for them, and re-layouts  1.18 us (1%)
    all_to_all x1, blocking collectives, on_device(): lax.all_to_all(slots, ('state', 'tile'), split_axis=0, concat_axis=0, til...  31 us
    pallas_call x1, Pallas kernels, on_device(): pl.pallas_call(functools.partial(backward_kernel, tiles=tiles, chunks=chu...  12.2 us
    ppermute x12, waiting for transfers between devices, to_partner(): lax.ppermute(value, 'tile', [(t, t ^ k) for t in range(tiles)])  9.64 us
    ppermute x12, starting transfers between devices, to_partner(): lax.ppermute(value, 'tile', [(t, t ^ k) for t in range(tiles)])  9.46 us
    pallas_call x2, Pallas kernels, on_device(): results = call(*inputs, *saved)  8.36 us
    pallas_call x1, Pallas kernels, on_device(): pl.pallas_call(functools.partial(project_kernel, parts=grid_side), grid_s...  3.67 us
    pallas_call x1, Pallas kernels, on_device(): pl.pallas_call(functools.partial(finish_kernel, tiles=tiles), grid_spec=p...  3.3 us
    pallas_call x1, Pallas kernels, on_device(): pl.pallas_call(functools.partial(bias_kernel, per_head=per_head), grid=(p...  3.04 us
  transfers between devices with their start and end apart: 13, of which 4 were waited for; matrix products, arithmetic and copies ran while one was open for 0% of the time, Pallas kernels for 14%

profile of v6, /device:TPU:0, one launch (start us, length us, event | category | flops | bytes accessed | tf_op | source)
XLA Modules:
  0.0 86.2 jit_solution(8367908012656926536)
XLA Ops:
  0.0 0.0 copy-start
  0.0 0.0 copy-start.4
  0.0 0.0 copy-start.2
  0.0 1.2 %constant_dynamic-slice_fusion = bf16[4,1,8,64,128]{4,3,2,1,0:T(8,128)(2,1)S(1)} fusion(bf16[4,2,8,64,128]{4,3,2,1,0:T(8,128)(2,1)} %bitcast.19, s32[]{:T(128)S(6)} %select_n.4), kind=kLoop, calls=%fused_computation | loop fusion | bytes 1048580 | tf_op jit(solution)/shard_map/jit(dynamic_index_in_dim)/dynamic_slice | solution.py:530
  1.2 0.6 collective-permute-start.3
  1.8 3.0 %bias.1.refs_0_ = f32[160,128]{1,0:T(8,128)S(1)} custom-call(bf16[2,32,64,128]{3,2,1,0:T(8,128)(2,1)} %bitcast.20, s32[32,128]{1,0:T(8,128)} %bitcast.29, f32[1,128]{1,0:T(1,128)} %bitcast.22, f32[1,128]{1,0:T(1,128)} %bitcast.25, f32[4,128]{1,0:T(4,128)} %bitcast.30), custom_call_target="tpu_custom_call" | custom-call | tf_op jit(solution)/shard_map/bias/pallas_call | solution.py:580
  4.8 2.7 %collective-permute-start.2 = (f32[160,128]{1,0:T(8,128)S(1)}, f32[160,128]{1,0:T(8,128)S(1)}, u32[]{:S(2)}, u32[]{:S(2)}) collective-permute-start(f32[160,128]{1,0:T(8,128)S(1)} %bias.1.refs_0_), channel_id=1, source_target_pairs={{0,3},{1,2},{2,1},{3,0},{4,7},{5,6},{6,5},{7,4},{8,11},{9,10},{10,... | collective-permute-start | bytes 245768 | tf_op jit(solution)/shard_map/ppermute | solution.py:608
  7.4 0.0 collective-permute-start.1
  7.5 0.2 collective-permute-start
  7.6 1.3 %prep.1 = (bf16[512,128]{1,0:T(8,128)(2,1)S(1)}, bf16[128,256]{1,0:T(8,128)(2,1)S(1)}, bf16[128,128]{1,0:T(8,128)(2,1)S(1)}, bf16[128,128]{1,0:T(8,128)(2,1)S(1)...) custom-call(bf16[128,128]{1,0:T(8,128)(2,1)} %wq.1, ...), custom_call_target="tpu_custom_call" | custom-call | tf_op jit(solution)/shard_map/prep/pallas_call | solution.py:555
  9.0 0.0 collective-permute-done.3.refs_1_
  9.0 0.0 copy-done
  9.0 0.0 copy-done.4
  9.0 0.0 copy-done.2
  9.0 3.7 %project.1 = (bf16[32,128,128]{2,1,0:T(8,128)(2,1)S(1)}, bf16[32,128,128]{2,1,0:T(8,128)(2,1)S(1)}, bf16[32,128,128]{2,1,0:T(8,128)(2,1)S(1)}, bf16[32,128,128]{...) custom-call(s32[1]{0:T(128)} %bitcast.5.own_ref, ...), custom_call_target="tpu_custom_call" | custom-call | flops 5368709120 | bytes 12582912 | tf_op jit(solution)/shard_map/project/pallas_call | solution.py:620
  12.7 0.0 collective-permute-done.2.refs_3_
  12.7 0.0 collective-permute-done.1.refs_2_
  12.7 0.0 collective-permute-done.refs_1_
  12.7 4.2 %forward.2 = (bf16[32,128,512]{2,1,0:T(8,128)(2,1)S(1)}, f32[32,128,128]{2,1,0:T(8,128)S(1)}, f32[32,64,128]{2,1,0:T(8,128)S(1)}, f32[32,128]{1,0:T(8,128)S(1)},...) custom-call(f32[160,128]{1,0:T(8,128)S(1)} %bias.1.refs_0_, ...), custom_call_target="tpu_custom_call" | custom-call | flops 5033164800 | bytes 7340032 | tf_op jit(solution)/shard_map/forward/pallas_call | solution.py:694
  16.9 0.3 collective-permute-start.4
  17.3 2.0 %collective-permute-start.5 = (bf16[32,16,128]{2,1,0:T(8,128)(2,1)S(1)}, bf16[32,16,128]{2,1,0:T(8,128)(2,1)S(1)}, u32[]{:S(2)}, u32[]{:S(2)}) collective-permute-start(bf16[32,16,128]{2,1,0:T(8,128)(2,1)S(1)} %get-tuple-element.56), channel_id=1, source_target_pairs={{0,2},{1,3},{2,0},{3,1},{4,6},{5,7},{6,4},{7,5},{8,10},{9,11},{10,... | collective-permute-start | bytes 393224 | tf_op jit(solution)/shard_map/ppermute | solution.py:608
  19.3 0.0 collective-permute-start.6
  19.3 0.0 copy-start.1
  19.3 4.2 %forward.3 = (bf16[32,128,512]{2,1,0:T(8,128)(2,1)S(1)}, f32[32,128,128]{2,1,0:T(8,128)S(1)}, f32[32,64,128]{2,1,0:T(8,128)S(1)}, f32[32,128]{1,0:T(8,128)S(1)},...) custom-call(f32[160,128]{1,0:T(8,128)S(1)} %bias.1.refs_0_, ...), custom_call_target="tpu_custom_call", output_to_operand_aliasing={{0}: (11, {}), {1}: (12, {}), {2}: (13, {}), {3}: (14, {})} | custom-call | flops 5033164800 | bytes 7340032 | tf_op jit(solution)/shard_map/forward/pallas_call | solution.py:694
  23.4 0.1 collective-permute-start.7
  23.6 2.0 %collective-permute-start.8 = (bf16[32,16,128]{2,1,0:T(8,128)(2,1)S(1)}, bf16[32,16,128]{2,1,0:T(8,128)(2,1)S(1)}, u32[]{:S(2)}, u32[]{:S(2)}) collective-permute-start(bf16[32,16,128]{2,1,0:T(8,128)(2,1)S(1)} %get-tuple-element.64), channel_id=1, source_target_pairs={{0,2},{1,3},{2,0},{3,1},{4,6},{5,7},{6,4},{7,5},{8,10},{9,11},{10,... | collective-permute-start | bytes 393224 | tf_op jit(solution)/shard_map/ppermute | solution.py:608
  25.6 0.0 collective-permute-done.4.refs_1_
  25.6 0.0 collective-permute-start.9
  25.6 0.0 collective-permute-done.5.refs_2_
  25.6 0.0 collective-permute-done.6.refs_3_
  25.6 0.0 collective-permute-done.7.refs_5_
  25.6 4.3 %collective-permute-done.8.refs_6_ = bf16[32,16,128]{2,1,0:T(8,128)(2,1)S(1)} collective-permute-done((bf16[32,16,128]{2,1,0:T(8,128)(2,1)S(1)}, bf16[32,16,128]{2,1,0:T(8,128)(2,1)S(1)}, u32[]{:S(2)}, u32[]{:S(2)}) %collective-permute-start.8) | collective-permute-done | bytes 131104 | tf_op jit(solution)/shard_map/ppermute | solution.py:608
  29.9 1.6 %collective-permute-done.9.refs_7_ = bf16[32,16,128]{2,1,0:T(8,128)(2,1)S(1)} collective-permute-done((bf16[32,16,128]{2,1,0:T(8,128)(2,1)S(1)}, bf16[32,16,128]{2,1,0:T(8,128)(2,1)S(1)}, u32[]{:S(2)}, u32[]{:S(2)}) %collective-permute-start.9) | collective-permute-done | bytes 131104 | tf_op jit(solution)/shard_map/ppermute | solution.py:608
  31.6 0.0 copy-done.1
  31.6 0.0 copy-start.3
  31.6 12.2 %backward.1 = (f32[32,128,128]{2,1,0:T(8,128)S(1)}, f32[32,128,128]{2,1,0:T(8,128)S(1)}, bf16[4,32,128]{2,1,0:T(8,128)(2,1)S(1)}, bf16[4,32,128]{2,1,0:T(8,128)(...) custom-call(bf16[32,16,128]{2,1,0:T(8,128)(2,1)S(1)} %get-tuple-element.54.refs_0_, ...), custom_call_target="tpu_custom_call" | custom-call | flops 33554432000 | bytes 20971520 | tf_op jit(solution)/shard_map/backward/pallas_call | solution.py:699
  43.8 0.5 collective-permute-start.10
  44.3 1.6 %collective-permute-start.11 = (bf16[4,32,128]{2,1,0:T(8,128)(2,1)S(1)}, bf16[4,32,128]{2,1,0:T(8,128)(2,1)S(1)}, u32[]{:S(2)}, u32[]{:S(2)}) collective-permute-start(bf16[4,32,128]{2,1,0:T(8,128)(2,1)S(1)} %get-tuple-element.77), channel_id=1, source_target_pairs={{0,2},{1,3},{2,0},{3,1},{4,6},{5,7},{6,4},{7,5},{8,10},{9,11},{10,... | collective-permute-start | bytes 98312 | tf_op jit(solution)/shard_map/ppermute | solution.py:608
  45.9 0.0 collective-permute-start.12
  45.9 0.0 collective-permute-done.10.refs_1_
  45.9 2.3 %collective-permute-done.11.refs_2_ = bf16[4,32,128]{2,1,0:T(8,128)(2,1)S(1)} collective-permute-done((bf16[4,32,128]{2,1,0:T(8,128)(2,1)S(1)}, bf16[4,32,128]{2,1,0:T(8,128)(2,1)S(1)}, u32[]{:S(2)}, u32[]{:S(2)}) %collective-permute-start.11) | collective-permute-done | bytes 32800 | tf_op jit(solution)/shard_map/ppermute | solution.py:608
  48.2 1.4 %collective-permute-done.12.refs_3_ = bf16[4,32,128]{2,1,0:T(8,128)(2,1)S(1)} collective-permute-done((bf16[4,32,128]{2,1,0:T(8,128)(2,1)S(1)}, bf16[4,32,128]{2,1,0:T(8,128)(2,1)S(1)}, u32[]{:S(2)}, u32[]{:S(2)}) %collective-permute-start.12) | collective-permute-done | bytes 32800 | tf_op jit(solution)/shard_map/ppermute | solution.py:608
  49.6 0.0 copy-done.3
  49.6 3.3 %finish.1 = bf16[8,32,16,128]{3,2,1,0:T(8,128)(2,1)S(1)} custom-call(s32[8]{0:T(128)S(1)} %copy-done.3, bf16[4,32,128]{2,1,0:T(8,128)(2,1)S(1)} %get-tuple-element.75.refs_0_, bf16[4,32,128]{2,1,0:T(8,128)(2,1)S(1)} %collective-permute-done.10.refs_1_, bf16[4,32,128]{2,1,0:T(8,128)(2,1)S(1)} %collective-permute-done.11.refs_2_, ...), custom_call_target="tpu_custom_call" | custom-call | tf_op jit(solution)/shard_map/finish/pallas_call | solution.py:731
  52.9 31.0 %all_to_all.5 = bf16[32,8,16,128]{3,2,1,0:T(8,128)(2,1)S(1)} all-to-all(bf16[32,8,16,128]{3,2,1,0:T(8,128)(2,1)S(1)} %bitcast.17), channel_id=1, replica_groups=mesh['state'=8,'tile'=4] {'state','tile'}, dimensions={0} | all-to-all | bytes 2097152 | tf_op jit(solution)/shard_map/all_to_all | solution.py:760
  83.9 2.3 %place.1 = f32[4,16,2,16,128]{4,3,2,1,0:T(8,128)} custom-call(s32[8]{0:T(128)S(1)} %copy-done.3, bf16[8,2,16,16,128]{4,3,2,1,0:T(8,128)(2,1)S(1)} %bitcast.18), custom_call_target="tpu_custom_call" | custom-call | tf_op jit(solution)/shard_map/place/pallas_call | solution.py:773
Async XLA Ops:
  0.0 9.0 %copy-start = (bf16[1,1,64,64,128]{4,3,2,1,0:T(8,128)(2,1)S(1)}, bf16[1,1,64,64,128]{4,3,2,1,0:T(8,128)(2,1)}, u32[]{:S(2)}) copy-start(bf16[1,1,64,64,128]{4,3,2,1,0:T(8,128)(2,1)} %param.15) | copy-start | bytes 3145732
  0.0 9.0 %copy-start.4 = (f32[128]{0:T(128)S(1)}, f32[128]{0:T(128)}, u32[]{:S(2)}) copy-start(f32[128]{0:T(128)} %param.19) | copy-start | bytes 1540
  0.0 9.0 %copy-start.2 = (f32[128]{0:T(128)S(1)}, f32[128]{0:T(128)}, u32[]{:S(2)}) copy-start(f32[128]{0:T(128)} %param.18) | copy-start | bytes 1540
  1.2 7.8 %collective-permute-start.3 = (bf16[32,64,128]{2,1,0:T(8,128)(2,1)S(1)}, bf16[32,64,128]{2,1,0:T(8,128)(2,1)S(1)}, u32[]{:S(2)}, u32[]{:S(2)}) collective-permute-start(bf16[32,64,128]{2,1,0:T(8,128)(2,1)S(1)} %bitcast.27), channel_id=1, source_target_pairs={{0,1},{1,0},{2,3},{3,2},{4,5},{5,4},{6,7},{7,6},{8,9},{9,8},{10,11... | collective-permute-start | bytes 1572872 | tf_op jit(solution)/shard_map/ppermute | solution.py:539
  4.8 7.9 %collective-permute-start.2 = (f32[160,128]{1,0:T(8,128)S(1)}, f32[160,128]{1,0:T(8,128)S(1)}, u32[]{:S(2)}, u32[]{:S(2)}) collective-permute-start(f32[160,128]{1,0:T(8,128)S(1)} %bias.1.refs_0_), channel_id=1, source_target_pairs={{0,3},{1,2},{2,1},{3,0},{4,7},{5,6},{6,5},{7,4},{8,11},{9,10},{10,... | collective-permute-start | bytes 245768 | tf_op jit(solution)/shard_map/ppermute | solution.py:608
  7.4 5.3 %collective-permute-start.1 = (f32[160,128]{1,0:T(8,128)S(1)}, f32[160,128]{1,0:T(8,128)S(1)}, u32[]{:S(2)}, u32[]{:S(2)}) collective-permute-start(f32[160,128]{1,0:T(8,128)S(1)} %bias.1.refs_0_), channel_id=1, source_target_pairs={{0,2},{1,3},{2,0},{3,1},{4,6},{5,7},{6,4},{7,5},{8,10},{9,11},{10,... | collective-permute-start | bytes 245768 | tf_op jit(solution)/shard_map/ppermute | solution.py:608
  7.5 5.3 %collective-permute-start = (f32[160,128]{1,0:T(8,128)S(1)}, f32[160,128]{1,0:T(8,128)S(1)}, u32[]{:S(2)}, u32[]{:S(2)}) collective-permute-start(f32[160,128]{1,0:T(8,128)S(1)} %bias.1.refs_0_), channel_id=1, source_target_pairs={{0,1},{1,0},{2,3},{3,2},{4,5},{5,4},{6,7},{7,6},{8,9},{9,8},{10,11... | collective-permute-start | bytes 245768 | tf_op jit(solution)/shard_map/ppermute | solution.py:608
  16.9 8.7 %collective-permute-start.4 = (bf16[32,16,128]{2,1,0:T(8,128)(2,1)S(1)}, bf16[32,16,128]{2,1,0:T(8,128)(2,1)S(1)}, u32[]{:S(2)}, u32[]{:S(2)}) collective-permute-start(bf16[32,16,128]{2,1,0:T(8,128)(2,1)S(1)} %get-tuple-element.55), channel_id=1, source_target_pairs={{0,1},{1,0},{2,3},{3,2},{4,5},{5,4},{6,7},{7,6},{8,9},{9,8},{10,11... | collective-permute-start | bytes 393224 | tf_op jit(solution)/shard_map/ppermute | solution.py:608
  17.3 8.3 %collective-permute-start.5 = (bf16[32,16,128]{2,1,0:T(8,128)(2,1)S(1)}, bf16[32,16,128]{2,1,0:T(8,128)(2,1)S(1)}, u32[]{:S(2)}, u32[]{:S(2)}) collective-permute-start(bf16[32,16,128]{2,1,0:T(8,128)(2,1)S(1)} %get-tuple-element.56), channel_id=1, source_target_pairs={{0,2},{1,3},{2,0},{3,1},{4,6},{5,7},{6,4},{7,5},{8,10},{9,11},{10,... | collective-permute-start | bytes 393224 | tf_op jit(solution)/shard_map/ppermute | solution.py:608
  19.3 6.3 %collective-permute-start.6 = (bf16[32,16,128]{2,1,0:T(8,128)(2,1)S(1)}, bf16[32,16,128]{2,1,0:T(8,128)(2,1)S(1)}, u32[]{:S(2)}, u32[]{:S(2)}) collective-permute-start(bf16[32,16,128]{2,1,0:T(8,128)(2,1)S(1)} %get-tuple-element.57), channel_id=1, source_target_pairs={{0,3},{1,2},{2,1},{3,0},{4,7},{5,6},{6,5},{7,4},{8,11},{9,10},{10,... | collective-permute-start | bytes 393224 | tf_op jit(solution)/shard_map/ppermute | solution.py:608
  19.3 12.3 %copy-start.1 = (bf16[128,128]{1,0:T(8,128)(2,1)S(1)}, bf16[128,128]{1,0:T(8,128)(2,1)}, u32[]{:S(2)}) copy-start(bf16[128,128]{1,0:T(8,128)(2,1)} %refs_16_.1) | copy-start | bytes 98308
  23.4 2.2 %collective-permute-start.7 = (bf16[32,16,128]{2,1,0:T(8,128)(2,1)S(1)}, bf16[32,16,128]{2,1,0:T(8,128)(2,1)S(1)}, u32[]{:S(2)}, u32[]{:S(2)}) collective-permute-start(bf16[32,16,128]{2,1,0:T(8,128)(2,1)S(1)} %get-tuple-element.63), channel_id=1, source_target_pairs={{0,1},{1,0},{2,3},{3,2},{4,5},{5,4},{6,7},{7,6},{8,9},{9,8},{10,11... | collective-permute-start | bytes 393224 | tf_op jit(solution)/shard_map/ppermute | solution.py:608
  23.6 6.4 %collective-permute-start.8 = (bf16[32,16,128]{2,1,0:T(8,128)(2,1)S(1)}, bf16[32,16,128]{2,1,0:T(8,128)(2,1)S(1)}, u32[]{:S(2)}, u32[]{:S(2)}) collective-permute-start(bf16[32,16,128]{2,1,0:T(8,128)(2,1)S(1)} %get-tuple-element.64), channel_id=1, source_target_pairs={{0,2},{1,3},{2,0},{3,1},{4,6},{5,7},{6,4},{7,5},{8,10},{9,11},{10,... | collective-permute-start | bytes 393224 | tf_op jit(solution)/shard_map/ppermute | solution.py:608
  25.6 6.0 %collective-permute-start.9 = (bf16[32,16,128]{2,1,0:T(8,128)(2,1)S(1)}, bf16[32,16,128]{2,1,0:T(8,128)(2,1)S(1)}, u32[]{:S(2)}, u32[]{:S(2)}) collective-permute-start(bf16[32,16,128]{2,1,0:T(8,128)(2,1)S(1)} %get-tuple-element.65), channel_id=1, source_target_pairs={{0,3},{1,2},{2,1},{3,0},{4,7},{5,6},{6,5},{7,4},{8,11},{9,10},{10,... | collective-permute-start | bytes 393224 | tf_op jit(solution)/shard_map/ppermute | solution.py:608
  31.6 18.0 %copy-start.3 = (s32[8]{0:T(128)S(1)}, s32[8]{0:T(128)}, u32[]{:S(2)}) copy-start(s32[8]{0:T(128)} %offsets.3) | copy-start | bytes 100
  43.8 2.1 %collective-permute-start.10 = (bf16[4,32,128]{2,1,0:T(8,128)(2,1)S(1)}, bf16[4,32,128]{2,1,0:T(8,128)(2,1)S(1)}, u32[]{:S(2)}, u32[]{:S(2)}) collective-permute-start(bf16[4,32,128]{2,1,0:T(8,128)(2,1)S(1)} %get-tuple-element.76), channel_id=1, source_target_pairs={{0,1},{1,0},{2,3},{3,2},{4,5},{5,4},{6,7},{7,6},{8,9},{9,8},{10,11... | collective-permute-start | bytes 98312 | tf_op jit(solution)/shard_map/ppermute | solution.py:608
  44.3 3.9 %collective-permute-start.11 = (bf16[4,32,128]{2,1,0:T(8,128)(2,1)S(1)}, bf16[4,32,128]{2,1,0:T(8,128)(2,1)S(1)}, u32[]{:S(2)}, u32[]{:S(2)}) collective-permute-start(bf16[4,32,128]{2,1,0:T(8,128)(2,1)S(1)} %get-tuple-element.77), channel_id=1, source_target_pairs={{0,2},{1,3},{2,0},{3,1},{4,6},{5,7},{6,4},{7,5},{8,10},{9,11},{10,... | collective-permute-start | bytes 98312 | tf_op jit(solution)/shard_map/ppermute | solution.py:608
  45.9 3.7 %collective-permute-start.12 = (bf16[4,32,128]{2,1,0:T(8,128)(2,1)S(1)}, bf16[4,32,128]{2,1,0:T(8,128)(2,1)S(1)}, u32[]{:S(2)}, u32[]{:S(2)}) collective-permute-start(bf16[4,32,128]{2,1,0:T(8,128)(2,1)S(1)} %get-tuple-element.78), channel_id=1, source_target_pairs={{0,3},{1,2},{2,1},{3,0},{4,7},{5,6},{6,5},{7,4},{8,11},{9,10},{10,... | collective-permute-start | bytes 98312 | tf_op jit(solution)/shard_map/ppermute | solution.py:608

commit v7 on v6

--- a/solution.py
+++ b/solution.py
@@ -18,6 +18,7 @@
 BWD_PACE = (2, 0, 3)
 PROJ_PACE = (2, 0, 3)
 FIN_PACE = (8, 1, 0)
+MID_PACE = (8, 1, 0)
 PROJ_ROWS = 8
 FIN_ROWS = 8
 EPS = 1e-5
@@ -80,25 +81,57 @@
     return pl.BlockSpec(shape, lambda *_: (0,) * len(shape))
 
 
-def prep_kernel(wq, wk, wv, wg, wo, gb, ob, wd, db, wpb, lng, w4t, w2, wod, wdt, wd3, wall, gbc, lgc, cst, wgs):
-    wide = gbc.shape[1]
+def prep_kernel(wq, wk, wv, wg, wo, gb, wd, w4t, w2, wod, wdt, gbc):
     w4t[...] = jnp.concatenate([transposed(w[...]) for w in (wq, wk, wv, wg)], axis=0)
     w2[...] = jnp.concatenate([wk[...], wv[...]], axis=1)
-    wall[...] = jnp.concatenate([wq[...], wk[...], wv[...], wg[...]], axis=1)
-    dist_t = wd[...]
-    dist = dist_t.T
-    dist_hi, dist_lo = split(dist)
-    wd3[...] = jnp.concatenate([dist_hi, dist_hi, dist_lo], axis=1)
-    wdt[...] = jnp.concatenate(split(dist_t), axis=0)
-    both = nn(wo[...].astype(F32), dist, precision=HIGHEST)
-    wod[...] = jnp.concatenate(split(both.T), axis=0)
-    gbc[...] = column(gb[...], wide)
-    lgc[...] = column(lng[...], wide)
-    shift = 2.0 * jnp.sum(dist_t * ob[...], axis=1, keepdims=True)
-    cst[...] = column(db[...], wide) + shift
-    proj = jnp.concatenate([wpb[...], jnp.zeros((wide - H, wpb.shape[1]), F32)], axis=0).T[:, :H]
-    proj_hi, proj_lo = split(proj)
-    wgs[...] = jnp.concatenate([proj_hi, proj_hi, proj_lo, jnp.zeros_like(proj_lo)], axis=1)
+    wdt[...] = jnp.concatenate(split(wd[...]), axis=0)
+    both = nt(wd[...], wo[...].astype(F32), precision=HIGHEST)
+    wod[...] = jnp.concatenate(split(both), axis=0)
+    gbc[...] = column(gb[...], gbc.shape[1])
+
+
+def middle_kernel(after, zr, wq, wk, wv, wg, ob, wd, db, wpb, lng, nrm, inv, wd3, wall, lgc, cst, wgs):
+    del after
+    rows, wide, chans = zr.shape
+
+    @pl.when(pl.program_id(0) == 0)
+    def _():
+        wall[...] = jnp.concatenate([wq[...], wk[...], wv[...], wg[...]], axis=1)
+        dist_hi, dist_lo = split(wd[...].T)
+        wd3[...] = jnp.concatenate([dist_hi, dist_hi, dist_lo], axis=1)
+        lgc[...] = column(lng[...], wide)
+        shift = 2.0 * jnp.sum(wd[...] * ob[...], axis=1, keepdims=True)
+        cst[...] = column(db[...], wide) + shift
+        proj = wpb[...] * lng[...]
+        proj = jnp.concatenate([proj, jnp.zeros((wide - H, chans), F32)], axis=0).T[:, :H]
+        proj_hi, proj_lo = split(proj)
+        wgs[...] = jnp.concatenate([proj_hi, proj_hi, proj_lo, jnp.zeros_like(proj_lo)], axis=1)
+
+    ident = eye(chans)
+
+    def one_row(row):
+        pair_t = nt(ident, zr[row])
+        yield
+        center = pair_t - jnp.mean(pair_t, axis=0, keepdims=True)
+        yield
+        inverse = lax.rsqrt(jnp.mean(center * center, axis=0, keepdims=True) + EPS)
+        inv[row : row + 1, :] = inverse
+        nrm[row] = center * inverse
+        yield
+
+    interleave([one_row(row) for row in range(rows)], MID_PACE)
+
+
+def main_kernel(dpt, dzn, nrm, inv, lgc, base):
+    def one_row(row):
+        scaled = dzn[row] * lgc[...]
+        mean_a = jnp.mean(scaled, axis=0, keepdims=True)
+        mean_b = jnp.mean(scaled * nrm[row], axis=0, keepdims=True)
+        yield
+        base[row] = dpt[row] + inv[row : row + 1, :] * (scaled - mean_a - nrm[row] * mean_b)
+        yield
+
+    interleave([one_row(row) for row in range(dzn.shape[0])], MID_PACE)
 
 
 def bias_kernel(tile, targets, lng, lnb, wpb, out, *, per_head):
@@ -278,9 +311,9 @@
         yield
         logit = both[:NB] + both[NB:]
         ut[row] = logit
-        high = logit.astype(BF).astype(F32)
-        yield
-        packed = jnp.concatenate([high, logit - high], axis=0).T
+        logit = logit - jnp.max(logit, axis=0, keepdims=True)
+        yield
+        packed = jnp.concatenate([logit, logit], axis=0).T
         here = step * rows + row
         yield
         for i in range(grid_side):
@@ -297,12 +330,12 @@
 
     @pl.when(step == pl.num_programs(0) - 1)
     def _():
+        left = lax.broadcasted_iota(jnp.int32, (count // 2, 2 * NB), 1) < NB
         for k in range(tiles):
             start = (mine ^ k) * (share * count)
             for r in range(share):
-                sends[k][r] = stage[
-                    pl.ds(pl.multiple_of(start + r * count, 8), count), :
-                ].astype(BF)
+                both = stage[pl.ds(pl.multiple_of(start + r * count, 8), count), :]
+                sends[k][r] = jnp.where(left, both[: count // 2], both[count // 2 :]).astype(BF)
 
 
 def backward_kernel(*refs, tiles, chunks, grid_side, groups, group_rows):
@@ -328,6 +361,7 @@
         acc[...] = jnp.zeros_like(acc)
 
     shift = jnp.concatenate([cst[...]] * 2, axis=1)
+    left = lax.broadcasted_iota(jnp.int32, (rcv[0].shape[1], 2 * NB), 1) < NB
 
     def one_pair(first):
         pair = (first, first + 1)
@@ -335,12 +369,18 @@
             for k in range(tiles):
                 source_i = (mine ^ k) // grid_side
                 source_j = lax.rem(mine ^ k, grid_side)
-                for p in range(groups):
-                    start = ((source_i * groups + p) * grid_side + source_j) * group_rows
-                    local = (p % chunk_groups) * group_rows
-                    mirror_s[pl.ds(pl.multiple_of(row * wide + start, group_rows), group_rows), :] = rcv[
-                        (p // chunk_groups) * tiles + k
-                    ][row, local : local + group_rows].astype(F32)
+                for c in range(chunks):
+                    part = rcv[c * tiles + k][row].astype(F32)
+                    part = jnp.concatenate(
+                        [jnp.where(left, part, 0.0), jnp.where(left, 0.0, part)], axis=0
+                    )
+                    for p in range(chunk_groups):
+                        start = (
+                            (source_i * groups + c * chunk_groups + p) * grid_side + source_j
+                        ) * group_rows + row * wide
+                        mirror_s[pl.ds(pl.multiple_of(start, group_rows), group_rows), :] = part[
+                            p * group_rows : (p + 1) * group_rows
+                        ]
         yield
         other = nt(adder, mirror_s[first * wide : (first + 2) * wide, :].astype(BF))
         yield
@@ -427,9 +467,9 @@
 
 def finish_kernel(offsets, *refs, tiles):
     rdb = refs[:tiles]
-    dpt, dzn, zr, wgs, lgc, out, sums = refs[tiles:]
+    base, nrm, inv, wgs, out, sums = refs[tiles:]
     step = pl.program_id(0)
-    rows, chans, wide = dzn.shape
+    rows, chans, wide = base.shape
     states, _, piece, _ = out.shape
     total_rows = rdb[0].shape[1]
     turn = offsets[lax.axis_index("state")] // piece
@@ -442,27 +482,19 @@
                 total = total + part[h].astype(F32)
             sums[pl.ds(h * total_rows, total_rows), :] = total
 
-    ident = eye(chans)
-
     def one_row(row):
         local = step * rows + row
-        pair_t = nt(ident, zr[row])
-        yield
-        center = pair_t - jnp.mean(pair_t, axis=0, keepdims=True)
-        yield
-        inverse = lax.rsqrt(jnp.mean(center * center, axis=0, keepdims=True) + EPS)
-        normed = center * inverse
-        yield
         parts = [sums[pl.ds(h * total_rows + local, 1), :] for h in range(H)]
         high, low = split(jnp.concatenate(parts, axis=0))
-        spread = jnp.concatenate([high.astype(F32), low.astype(F32), high.astype(F32), jnp.zeros((H, wide), F32)], axis=0)
-        yield
-        scaled = (dzn[row] + nn(wgs[...], spread.astype(BF))) * lgc[...]
+        high, low = high.astype(F32), low.astype(F32)
+        spread = jnp.concatenate([high, low, high, jnp.zeros((H, wide), F32)], axis=0)
+        yield
+        scaled = nn(wgs[...], spread.astype(BF))
         yield
         mean_a = jnp.mean(scaled, axis=0, keepdims=True)
-        mean_b = jnp.mean(scaled * normed, axis=0, keepdims=True)
-        yield
-        total = dpt[row] + inverse * (scaled - mean_a - normed * mean_b)
+        mean_b = jnp.mean(scaled * nrm[row], axis=0, keepdims=True)
+        yield
+        total = base[row] + inv[row : row + 1, :] * (scaled - mean_a - nrm[row] * mean_b)
         yield
         total = total.T.astype(BF)
         for c in range(wide // piece):
@@ -545,16 +577,13 @@
         ((chans, 2 * width), BF),
         ((2 * NB, width), BF),
         ((2 * NB, chans), BF),
-        ((chans, 3 * NB), BF),
-        ((chans, 4 * width), BF),
         ((width, wide), F32),
-        ((chans, wide), F32),
-        ((NB, wide), F32),
-        ((chans, 4 * H), BF),
     )
-    w4t, w2, wod, wdt, wd3, wall, gbc, lgc, cst, wgs = pl.pallas_call(
-        prep_kernel, out_shape=prep_shapes, name="prep",
-        compiler_params=pltpu.CompilerParams(vmem_limit_bytes=VMEM_BYTES)
+    w4t, w2, wod, wdt, gbc = pl.pallas_call(
+        prep_kernel,
+        out_shape=prep_shapes,
+        name="prep",
+        compiler_params=pltpu.CompilerParams(vmem_limit_bytes=VMEM_BYTES),
     )(
         *map(
             stay,
@@ -565,11 +594,7 @@
                 w_gate,
                 w_output,
                 gate_bias.reshape(1, width),
-                out_bias.reshape(1, chans),
                 w_distogram.T,
-                dist_bias.reshape(1, NB),
-                w_pairbias.T,
-                gain_row,
             ),
         )
     )
@@ -650,7 +675,7 @@
         ((share, wide), F32),
         ((H, wide, wide), F32),
     )
-    packed_shape = (share, count, 2 * NB)
+    packed_shape = (share, count // 2, 2 * NB)
     saved = []
     mirrored = []
     for c in range(chunks):
@@ -696,10 +721,41 @@
         mirrored.append([to_partner(results[5 + k], k) for k in range(tiles)])
     at, ot, ut, tgt = saved
 
+    late = (
+        w_query,
+        w_key,
+        w_value,
+        w_gate,
+        out_bias.reshape(1, chans),
+        w_distogram.T,
+        dist_bias.reshape(1, NB),
+        w_pairbias.T,
+        gain_row,
+    )
+    late_shapes = (
+        ((chans, 3 * NB), BF),
+        ((chans, 4 * width), BF),
+        ((chans, wide), F32),
+        ((NB, wide), F32),
+        ((chans, 4 * H), BF),
+    )
+    nrm, inv, wd3, wall, lgc, cst, wgs = pl.pallas_call(
+        middle_kernel,
+        grid=(share // block,),
+        in_specs=[pl.BlockSpec((8, wide), lambda g: (0, 0)), by_row(wide, chans, rows=block)]
+        + [full(w.shape) for w in late],
+        out_specs=[by_row(chans, wide, rows=block), by_row(wide, rows=block)]
+        + [full(shape) for shape, _ in late_shapes],
+        out_shape=shapes(((share, chans, wide), F32), ((share, wide), F32), *late_shapes),
+        cost_estimate=cost(20 * share * cell, 3 * share * wide * width * 2),
+        name="middle",
+        compiler_params=pltpu.CompilerParams(vmem_limit_bytes=VMEM_BYTES),
+    )(tgt, zr, *map(stay, late))
+
     results = pl.pallas_call(
         functools.partial(backward_kernel, tiles=tiles, chunks=chunks, **layout),
         grid=(share // block,),
-        in_specs=[by_row(count, 2 * NB, rows=block)] * (tiles * chunks)
+        in_specs=[by_row(count // 2, 2 * NB, rows=block)] * (tiles * chunks)
         + [
             by_row(wide, rows=block),
             by_row(wide, H * wide, rows=block),
@@ -727,6 +783,18 @@
     dpt, dzn = results[:2]
     rdb = [to_partner(results[2 + k], k) for k in range(tiles)]
 
+    base = pl.pallas_call(
+        main_kernel,
+        grid=(share // block,),
+        in_specs=[by_row(chans, wide, rows=block)] * 3
+        + [by_row(wide, rows=block), full(lgc.shape)],
+        out_specs=by_row(chans, wide, rows=block),
+        out_shape=jax.ShapeDtypeStruct((share, chans, wide), F32),
+        cost_estimate=cost(20 * share * cell, 8 * share * wide * width * 2),
+        name="main",
+        compiler_params=pltpu.CompilerParams(vmem_limit_bytes=VMEM_BYTES),
+    )(dpt, dzn, nrm, inv, lgc)
+
     block = FIN_ROWS if share % FIN_ROWS == 0 else 1
     outgoing = pl.pallas_call(
         functools.partial(finish_kernel, tiles=tiles),
@@ -735,11 +803,10 @@
             grid=(share // block,),
             in_specs=[
                 *([full(rdb[0].shape)] * tiles),
-                pl.BlockSpec((block, chans, wide), lambda g, _: (g, 0, 0)),
-                pl.BlockSpec((block, chans, wide), lambda g, _: (g, 0, 0)),
-                pl.BlockSpec((block, wide, chans), lambda g, _: (g, 0, 0)),
+                by_row(chans, wide, rows=block),
+                by_row(chans, wide, rows=block),
+                by_row(wide, rows=block),
                 full(wgs.shape),
-                full(lgc.shape),
             ],
             out_specs=pl.BlockSpec((states, block, piece, chans), lambda g, _: (0, g, 0, 0)),
             scratch_shapes=[pltpu.VMEM((H * share, wide), F32)],
@@ -747,7 +814,7 @@
         out_shape=jax.ShapeDtypeStruct((states, share, piece, chans), BF),
         name="finish",
         compiler_params=pltpu.CompilerParams(vmem_limit_bytes=VMEM_BYTES),
-    )(offsets, *rdb, dpt, dzn, zr, wgs, lgc)
+    )(offsets, *rdb, base, nrm, inv, wgs)
 
     if even:
         slots = outgoing.reshape(states * tiles, group_rows, piece, chans)

time: 86.4 us -> 83 us (0.961)
  waiting for transfers between devices: 9.64 us -> 3.44 us
  Pallas kernels: 34.2 us -> 36.7 us
    ppermute x12, waiting for transfers between devices: 9.64 us -> 3.44 us  [to_partner(): lax.ppermute(value, 'tile', [(t, t ^ k) for t in range(tiles)])]
    pallas_call x0 -> x2, Pallas kernels: none -> 3.57 us  [the longest x1 2.73 us: on_device(): pl.pallas_call(middle_kernel, grid=(share // block,), in_specs=[pl.BlockS...]
  transfers between devices with their start and end apart: 13 -> 13, of which waited for: 4 -> 3; matrix products, arithmetic and copies ran while one was open for 0% -> 0% of each run, Pallas kernels for 14% -> 19%
where the time goes in v7:
time: 83 us; the launch traced here: 82.6 us
  Pallas kernels  36.7 us (44%)
  blocking collectives  31.2 us (38%)
  starting transfers between devices  9.85 us (12%)
  waiting for transfers between devices  3.44 us (4%)
  local copies, waits for them, and re-layouts  1.18 us (1%)
    all_to_all x1, blocking collectives, on_device(): lax.all_to_all(slots, ('state', 'tile'), split_axis=0, concat_axis=0, til...  31.2 us
    pallas_call x1, Pallas kernels, on_device(): pl.pallas_call(functools.partial(backward_kernel, tiles=tiles, chunks=chu...  12.2 us
    ppermute x12, starting transfers between devices, to_partner(): lax.ppermute(value, 'tile', [(t, t ^ k) for t in range(tiles)])  9.27 us
    pallas_call x2, Pallas kernels, on_device(): results = call(*inputs, *saved)  8.43 us
    pallas_call x1, Pallas kernels, on_device(): pl.pallas_call(functools.partial(project_kernel, parts=grid_side), grid_s...  3.67 us
    ppermute x12, waiting for transfers between devices, to_partner(): lax.ppermute(value, 'tile', [(t, t ^ k) for t in range(tiles)])  3.44 us
    pallas_call x1, Pallas kernels, on_device(): pl.pallas_call(functools.partial(bias_kernel, per_head=per_head), grid=(p...  3.04 us
    pallas_call x1, Pallas kernels, on_device(): pl.pallas_call(middle_kernel, grid=(share // block,), in_specs=[pl.BlockS...  2.73 us
  transfers between devices with their start and end apart: 13, of which 3 were waited for; matrix products, arithmetic and copies ran while one was open for 0% of the time, Pallas kernels for 19%

profile of v7, /device:TPU:0, one launch (start us, length us, event | category | flops | bytes accessed | tf_op | source)
XLA Modules:
  0.0 82.6 jit_solution(18382790029342675794)
XLA Ops:
  0.0 0.0 copy-start
  0.0 0.0 copy-start.3
  0.0 0.0 copy-start.4
  0.0 1.2 %constant_dynamic-slice_fusion = bf16[4,1,8,64,128]{4,3,2,1,0:T(8,128)(2,1)S(1)} fusion(bf16[4,2,8,64,128]{4,3,2,1,0:T(8,128)(2,1)} %bitcast.19, s32[]{:T(128)S(6)} %select_n.4), kind=kLoop, calls=%fused_computation | loop fusion | bytes 1048580 | tf_op jit(solution)/shard_map/jit(dynamic_index_in_dim)/dynamic_slice | solution.py:562
  1.2 0.6 collective-permute-start.3
  1.8 3.0 %bias.1.refs_0_ = f32[160,128]{1,0:T(8,128)S(1)} custom-call(bf16[2,32,64,128]{3,2,1,0:T(8,128)(2,1)} %bitcast.20, s32[32,128]{1,0:T(8,128)} %bitcast.30, f32[1,128]{1,0:T(1,128)} %bitcast.24, f32[1,128]{1,0:T(1,128)} %bitcast.22, f32[4,128]{1,0:T(4,128)} %bitcast.31), custom_call_target="tpu_custom_call" | custom-call | tf_op jit(solution)/shard_map/bias/pallas_call | solution.py:605
  4.8 2.7 %collective-permute-start.2 = (f32[160,128]{1,0:T(8,128)S(1)}, f32[160,128]{1,0:T(8,128)S(1)}, u32[]{:S(2)}, u32[]{:S(2)}) collective-permute-start(f32[160,128]{1,0:T(8,128)S(1)} %bias.1.refs_0_), channel_id=1, source_target_pairs={{0,3},{1,2},{2,1},{3,0},{4,7},{5,6},{6,5},{7,4},{8,11},{9,10},{10,... | collective-permute-start | bytes 245768 | tf_op jit(solution)/shard_map/ppermute | solution.py:633
  7.4 0.0 collective-permute-start.1
  7.5 0.2 collective-permute-start
  7.6 1.1 %prep.1 = (bf16[512,128]{1,0:T(8,128)(2,1)S(1)}, bf16[128,256]{1,0:T(8,128)(2,1)S(1)}, bf16[128,128]{1,0:T(8,128)(2,1)S(1)}, bf16[128,128]{1,0:T(8,128)(2,1)S(1)}, f32[128,128]{1,0:T(8,128)S(1)}) custom-call(bf16[128,128]{1,0:T(8,128)(2,1)} %wq.3, bf16[128,128]{1,0:T(8,128)(2,1)} %wk.3, bf16[128,128]{1,0:T(8,128)(2,1)} %wv.3, bf16[128,128]{1,0:T(8,128)(2,1)} %wg.3, ...), custom_call_target="tpu_custom_call" | custom-call | tf_op jit(solution)/shard_map/prep/pallas_call | solution.py:582
  8.8 0.0 collective-permute-done.3.refs_1_
  8.8 0.0 copy-done
  8.8 0.0 copy-done.3
  8.8 0.0 copy-done.4
  8.8 3.7 %project.1 = (bf16[32,128,128]{2,1,0:T(8,128)(2,1)S(1)}, bf16[32,128,128]{2,1,0:T(8,128)(2,1)S(1)}, bf16[32,128,128]{2,1,0:T(8,128)(2,1)S(1)}, bf16[32,128,128]{...) custom-call(s32[1]{0:T(128)} %bitcast.5.own_ref, ...), custom_call_target="tpu_custom_call" | custom-call | flops 5368709120 | bytes 12582912 | tf_op jit(solution)/shard_map/project/pallas_call | solution.py:645
  12.5 0.0 collective-permute-done.2.refs_3_
  12.5 0.0 collective-permute-done.1.refs_2_
  12.5 0.0 collective-permute-done.refs_1_
  12.5 4.2 %forward.2 = (bf16[32,128,512]{2,1,0:T(8,128)(2,1)S(1)}, f32[32,128,128]{2,1,0:T(8,128)S(1)}, f32[32,64,128]{2,1,0:T(8,128)S(1)}, f32[32,128]{1,0:T(8,128)S(1)},...) custom-call(f32[160,128]{1,0:T(8,128)S(1)} %bias.1.refs_0_, ...), custom_call_target="tpu_custom_call" | custom-call | flops 5033164800 | bytes 7340032 | tf_op jit(solution)/shard_map/forward/pallas_call | solution.py:719
  16.7 0.3 collective-permute-start.4
  17.1 2.0 %collective-permute-start.5 = (bf16[32,8,128]{2,1,0:T(8,128)(2,1)S(1)}, bf16[32,8,128]{2,1,0:T(8,128)(2,1)S(1)}, u32[]{:S(2)}, u32[]{:S(2)}) collective-permute-start(bf16[32,8,128]{2,1,0:T(8,128)(2,1)S(1)} %get-tuple-element.58), channel_id=1, source_target_pairs={{0,2},{1,3},{2,0},{3,1},{4,6},{5,7},{6,4},{7,5},{8,10},{9,11},{10,... | collective-permute-start | bytes 196616 | tf_op jit(solution)/shard_map/ppermute | solution.py:633
  19.1 0.0 collective-permute-start.6
  19.1 4.2 %forward.3 = (bf16[32,128,512]{2,1,0:T(8,128)(2,1)S(1)}, f32[32,128,128]{2,1,0:T(8,128)S(1)}, f32[32,64,128]{2,1,0:T(8,128)S(1)}, f32[32,128]{1,0:T(8,128)S(1)},...) custom-call(f32[160,128]{1,0:T(8,128)S(1)} %bias.1.refs_0_, ...), custom_call_target="tpu_custom_call", output_to_operand_aliasing={{0}: (11, {}), {1}: (12, {}), {2}: (13, {}), {3}: (14, {})} | custom-call | flops 5033164800 | bytes 7340032 | tf_op jit(solution)/shard_map/forward/pallas_call | solution.py:719
  23.3 0.1 collective-permute-start.7
  23.4 2.0 %collective-permute-start.8 = (bf16[32,8,128]{2,1,0:T(8,128)(2,1)S(1)}, bf16[32,8,128]{2,1,0:T(8,128)(2,1)S(1)}, u32[]{:S(2)}, u32[]{:S(2)}) collective-permute-start(bf16[32,8,128]{2,1,0:T(8,128)(2,1)S(1)} %get-tuple-element.66), channel_id=1, source_target_pairs={{0,2},{1,3},{2,0},{3,1},{4,6},{5,7},{6,4},{7,5},{8,10},{9,11},{10,... | collective-permute-start | bytes 196616 | tf_op jit(solution)/shard_map/ppermute | solution.py:633
  25.4 0.0 collective-permute-done.4.refs_1_
  25.4 0.0 collective-permute-start.9
  25.4 0.0 copy-start.1
  25.4 2.7 %middle.1 = (f32[32,128,128]{2,1,0:T(8,128)S(1)}, f32[32,128]{1,0:T(8,128)S(1)}, bf16[128,192]{1,0:T(8,128)(2,1)S(1)}, bf16[128,512]{1,0:T(8,128)(2,1)S(1)}, f32...) custom-call(f32[32,128]{1,0:T(8,128)S(1)} %get-tuple-element.68.after.refs_8_, ...), custom_call_target="tpu_custom_call" | custom-call | flops 1342177280 | bytes 3145728 | tf_op jit(solution)/shard_map/middle/pallas_call | solution.py:742
  28.2 0.0 collective-permute-done.5.refs_2_
  28.2 0.0 collective-permute-done.6.refs_3_
  28.2 0.0 collective-permute-done.7.refs_5_
  28.2 0.0 collective-permute-done.8.refs_6_
  28.2 1.5 %collective-permute-done.9.refs_7_ = bf16[32,8,128]{2,1,0:T(8,128)(2,1)S(1)} collective-permute-done((bf16[32,8,128]{2,1,0:T(8,128)(2,1)S(1)}, bf16[32,8,128]{2,1,0:T(8,128)(2,1)S(1)}, u32[]{:S(2)}, u32[]{:S(2)}) %collective-permute-start.9) | collective-permute-done | bytes 65568 | tf_op jit(solution)/shard_map/ppermute | solution.py:633
  29.7 0.0 copy-done.1
  29.7 12.2 %backward.1 = (f32[32,128,128]{2,1,0:T(8,128)S(1)}, f32[32,128,128]{2,1,0:T(8,128)S(1)}, bf16[4,32,128]{2,1,0:T(8,128)(2,1)S(1)}, bf16[4,32,128]{2,1,0:T(8,128)(...) custom-call(bf16[32,8,128]{2,1,0:T(8,128)(2,1)S(1)} %get-tuple-element.56.refs_0_, ...), custom_call_target="tpu_custom_call" | custom-call | flops 33554432000 | bytes 20971520 | tf_op jit(solution)/shard_map/backward/pallas_call | solution.py:755
  41.9 0.1 collective-permute-start.10
  42.0 0.9 %collective-permute-start.11 = (bf16[4,32,128]{2,1,0:T(8,128)(2,1)S(1)}, bf16[4,32,128]{2,1,0:T(8,128)(2,1)S(1)}, u32[]{:S(2)}, u32[]{:S(2)}) collective-permute-start(bf16[4,32,128]{2,1,0:T(8,128)(2,1)S(1)} %get-tuple-element.79), channel_id=1, source_target_pairs={{0,2},{1,3},{2,0},{3,1},{4,6},{5,7},{6,4},{7,5},{8,10},{9,11},{10,... | collective-permute-start | bytes 98312 | tf_op jit(solution)/shard_map/ppermute | solution.py:633
  42.9 0.9 %collective-permute-start.12 = (bf16[4,32,128]{2,1,0:T(8,128)(2,1)S(1)}, bf16[4,32,128]{2,1,0:T(8,128)(2,1)S(1)}, u32[]{:S(2)}, u32[]{:S(2)}) collective-permute-start(bf16[4,32,128]{2,1,0:T(8,128)(2,1)S(1)} %get-tuple-element.80), channel_id=1, source_target_pairs={{0,3},{1,2},{2,1},{3,0},{4,7},{5,6},{6,5},{7,4},{8,11},{9,10},{10,... | collective-permute-start | bytes 98312 | tf_op jit(solution)/shard_map/ppermute | solution.py:633
  43.8 0.0 copy-start.2
  43.9 0.8 %main.1.refs_4_ = f32[32,128,128]{2,1,0:T(8,128)S(1)} custom-call(f32[32,128,128]{2,1,0:T(8,128)S(1)} %get-tuple-element.81.dpt, f32[32,128,128]{2,1,0:T(8,128)S(1)} %get-tuple-element.82.dzn, f32[32,128,128]{2,1,0:T(8,128)S(1)} %get-tuple-element.83.nrm.refs_5_, f32[32,128]{1,0:T(8,128)S(1)} %get-tuple-element.84.inv.refs_6_, ...), custom_call_target="tpu_custom_call" | custom-call | flops 1342177280 | bytes 8388608 | tf_op jit(solution)/shard_map/main/pallas_call | solution.py:786
  44.7 0.0 collective-permute-done.10.refs_1_
  44.7 1.3 %collective-permute-done.11.refs_2_ = bf16[4,32,128]{2,1,0:T(8,128)(2,1)S(1)} collective-permute-done((bf16[4,32,128]{2,1,0:T(8,128)(2,1)S(1)}, bf16[4,32,128]{2,1,0:T(8,128)(2,1)S(1)}, u32[]{:S(2)}, u32[]{:S(2)}) %collective-permute-start.11) | collective-permute-done | bytes 32800 | tf_op jit(solution)/shard_map/ppermute | solution.py:633
  46.0 0.6 collective-permute-done.12.refs_3_
  46.6 0.0 copy-done.2
  46.6 2.5 %finish.1 = bf16[8,32,16,128]{3,2,1,0:T(8,128)(2,1)S(1)} custom-call(s32[8]{0:T(128)S(1)} %copy-done.2, bf16[4,32,128]{2,1,0:T(8,128)(2,1)S(1)} %get-tuple-element.77.refs_0_, bf16[4,32,128]{2,1,0:T(8,128)(2,1)S(1)} %collective-permute-done.10.refs_1_, bf16[4,32,128]{2,1,0:T(8,128)(2,1)S(1)} %collective-permute-done.11.refs_2_, ...), custom_call_target="tpu_custom_call" | custom-call | tf_op jit(solution)/shard_map/finish/pallas_call | solution.py:799
  49.1 31.2 %all_to_all.5 = bf16[32,8,16,128]{3,2,1,0:T(8,128)(2,1)S(1)} all-to-all(bf16[32,8,16,128]{3,2,1,0:T(8,128)(2,1)S(1)} %bitcast.18), channel_id=1, replica_groups=mesh['state'=8,'tile'=4] {'state','tile'}, dimensions={0} | all-to-all | bytes 2097152 | tf_op jit(solution)/shard_map/all_to_all | solution.py:827
  80.3 2.3 %place.1 = f32[4,16,2,16,128]{4,3,2,1,0:T(8,128)} custom-call(s32[8]{0:T(128)S(1)} %copy-done.2, bf16[8,2,16,16,128]{4,3,2,1,0:T(8,128)(2,1)S(1)} %bitcast.17), custom_call_target="tpu_custom_call" | custom-call | tf_op jit(solution)/shard_map/place/pallas_call | solution.py:840
Async XLA Ops:
  0.0 8.8 %copy-start = (bf16[1,1,64,64,128]{4,3,2,1,0:T(8,128)(2,1)S(1)}, bf16[1,1,64,64,128]{4,3,2,1,0:T(8,128)(2,1)}, u32[]{:S(2)}) copy-start(bf16[1,1,64,64,128]{4,3,2,1,0:T(8,128)(2,1)} %param.15) | copy-start | bytes 3145732
  0.0 8.8 %copy-start.3 = (f32[128]{0:T(128)S(1)}, f32[128]{0:T(128)}, u32[]{:S(2)}) copy-start(f32[128]{0:T(128)} %param.19) | copy-start | bytes 1540
  0.0 8.8 %copy-start.4 = (f32[128]{0:T(128)S(1)}, f32[128]{0:T(128)}, u32[]{:S(2)}) copy-start(f32[128]{0:T(128)} %param.18) | copy-start | bytes 1540
  1.2 7.6 %collective-permute-start.3 = (bf16[32,64,128]{2,1,0:T(8,128)(2,1)S(1)}, bf16[32,64,128]{2,1,0:T(8,128)(2,1)S(1)}, u32[]{:S(2)}, u32[]{:S(2)}) collective-permute-start(bf16[32,64,128]{2,1,0:T(8,128)(2,1)S(1)} %bitcast.27), channel_id=1, source_target_pairs={{0,1},{1,0},{2,3},{3,2},{4,5},{5,4},{6,7},{7,6},{8,9},{9,8},{10,11... | collective-permute-start | bytes 1572872 | tf_op jit(solution)/shard_map/ppermute | solution.py:571
  4.8 7.7 %collective-permute-start.2 = (f32[160,128]{1,0:T(8,128)S(1)}, f32[160,128]{1,0:T(8,128)S(1)}, u32[]{:S(2)}, u32[]{:S(2)}) collective-permute-start(f32[160,128]{1,0:T(8,128)S(1)} %bias.1.refs_0_), channel_id=1, source_target_pairs={{0,3},{1,2},{2,1},{3,0},{4,7},{5,6},{6,5},{7,4},{8,11},{9,10},{10,... | collective-permute-start | bytes 245768 | tf_op jit(solution)/shard_map/ppermute | solution.py:633
  7.4 5.0 %collective-permute-start.1 = (f32[160,128]{1,0:T(8,128)S(1)}, f32[160,128]{1,0:T(8,128)S(1)}, u32[]{:S(2)}, u32[]{:S(2)}) collective-permute-start(f32[160,128]{1,0:T(8,128)S(1)} %bias.1.refs_0_), channel_id=1, source_target_pairs={{0,2},{1,3},{2,0},{3,1},{4,6},{5,7},{6,4},{7,5},{8,10},{9,11},{10,... | collective-permute-start | bytes 245768 | tf_op jit(solution)/shard_map/ppermute | solution.py:633
  7.5 5.0 %collective-permute-start = (f32[160,128]{1,0:T(8,128)S(1)}, f32[160,128]{1,0:T(8,128)S(1)}, u32[]{:S(2)}, u32[]{:S(2)}) collective-permute-start(f32[160,128]{1,0:T(8,128)S(1)} %bias.1.refs_0_), channel_id=1, source_target_pairs={{0,1},{1,0},{2,3},{3,2},{4,5},{5,4},{6,7},{7,6},{8,9},{9,8},{10,11... | collective-permute-start | bytes 245768 | tf_op jit(solution)/shard_map/ppermute | solution.py:633
  16.7 8.7 %collective-permute-start.4 = (bf16[32,8,128]{2,1,0:T(8,128)(2,1)S(1)}, bf16[32,8,128]{2,1,0:T(8,128)(2,1)S(1)}, u32[]{:S(2)}, u32[]{:S(2)}) collective-permute-start(bf16[32,8,128]{2,1,0:T(8,128)(2,1)S(1)} %get-tuple-element.57), channel_id=1, source_target_pairs={{0,1},{1,0},{2,3},{3,2},{4,5},{5,4},{6,7},{7,6},{8,9},{9,8},{10,11... | collective-permute-start | bytes 196616 | tf_op jit(solution)/shard_map/ppermute | solution.py:633
  17.1 11.1 %collective-permute-start.5 = (bf16[32,8,128]{2,1,0:T(8,128)(2,1)S(1)}, bf16[32,8,128]{2,1,0:T(8,128)(2,1)S(1)}, u32[]{:S(2)}, u32[]{:S(2)}) collective-permute-start(bf16[32,8,128]{2,1,0:T(8,128)(2,1)S(1)} %get-tuple-element.58), channel_id=1, source_target_pairs={{0,2},{1,3},{2,0},{3,1},{4,6},{5,7},{6,4},{7,5},{8,10},{9,11},{10,... | collective-permute-start | bytes 196616 | tf_op jit(solution)/shard_map/ppermute | solution.py:633
  19.1 9.1 %collective-permute-start.6 = (bf16[32,8,128]{2,1,0:T(8,128)(2,1)S(1)}, bf16[32,8,128]{2,1,0:T(8,128)(2,1)S(1)}, u32[]{:S(2)}, u32[]{:S(2)}) collective-permute-start(bf16[32,8,128]{2,1,0:T(8,128)(2,1)S(1)} %get-tuple-element.59), channel_id=1, source_target_pairs={{0,3},{1,2},{2,1},{3,0},{4,7},{5,6},{6,5},{7,4},{8,11},{9,10},{10,... | collective-permute-start | bytes 196616 | tf_op jit(solution)/shard_map/ppermute | solution.py:633
  23.3 4.9 %collective-permute-start.7 = (bf16[32,8,128]{2,1,0:T(8,128)(2,1)S(1)}, bf16[32,8,128]{2,1,0:T(8,128)(2,1)S(1)}, u32[]{:S(2)}, u32[]{:S(2)}) collective-permute-start(bf16[32,8,128]{2,1,0:T(8,128)(2,1)S(1)} %get-tuple-element.65), channel_id=1, source_target_pairs={{0,1},{1,0},{2,3},{3,2},{4,5},{5,4},{6,7},{7,6},{8,9},{9,8},{10,11... | collective-permute-start | bytes 196616 | tf_op jit(solution)/shard_map/ppermute | solution.py:633
  23.4 4.8 %collective-permute-start.8 = (bf16[32,8,128]{2,1,0:T(8,128)(2,1)S(1)}, bf16[32,8,128]{2,1,0:T(8,128)(2,1)S(1)}, u32[]{:S(2)}, u32[]{:S(2)}) collective-permute-start(bf16[32,8,128]{2,1,0:T(8,128)(2,1)S(1)} %get-tuple-element.66), channel_id=1, source_target_pairs={{0,2},{1,3},{2,0},{3,1},{4,6},{5,7},{6,4},{7,5},{8,10},{9,11},{10,... | collective-permute-start | bytes 196616 | tf_op jit(solution)/shard_map/ppermute | solution.py:633
  25.4 4.3 %collective-permute-start.9 = (bf16[32,8,128]{2,1,0:T(8,128)(2,1)S(1)}, bf16[32,8,128]{2,1,0:T(8,128)(2,1)S(1)}, u32[]{:S(2)}, u32[]{:S(2)}) collective-permute-start(bf16[32,8,128]{2,1,0:T(8,128)(2,1)S(1)} %get-tuple-element.67), channel_id=1, source_target_pairs={{0,3},{1,2},{2,1},{3,0},{4,7},{5,6},{6,5},{7,4},{8,11},{9,10},{10,... | collective-permute-start | bytes 196616 | tf_op jit(solution)/shard_map/ppermute | solution.py:633
  25.4 4.3 %copy-start.1 = (bf16[128,128]{1,0:T(8,128)(2,1)S(1)}, bf16[128,128]{1,0:T(8,128)(2,1)}, u32[]{:S(2)}) copy-start(bf16[128,128]{1,0:T(8,128)(2,1)} %refs_16_.1) | copy-start | bytes 98308
  41.9 2.8 %collective-permute-start.10 = (bf16[4,32,128]{2,1,0:T(8,128)(2,1)S(1)}, bf16[4,32,128]{2,1,0:T(8,128)(2,1)S(1)}, u32[]{:S(2)}, u32[]{:S(2)}) collective-permute-start(bf16[4,32,128]{2,1,0:T(8,128)(2,1)S(1)} %get-tuple-element.78), channel_id=1, source_target_pairs={{0,1},{1,0},{2,3},{3,2},{4,5},{5,4},{6,7},{7,6},{8,9},{9,8},{10,11... | collective-permute-start | bytes 98312 | tf_op jit(solution)/shard_map/ppermute | solution.py:633
  42.0 4.0 %collective-permute-start.11 = (bf16[4,32,128]{2,1,0:T(8,128)(2,1)S(1)}, bf16[4,32,128]{2,1,0:T(8,128)(2,1)S(1)}, u32[]{:S(2)}, u32[]{:S(2)}) collective-permute-start(bf16[4,32,128]{2,1,0:T(8,128)(2,1)S(1)} %get-tuple-element.79), channel_id=1, source_target_pairs={{0,2},{1,3},{2,0},{3,1},{4,6},{5,7},{6,4},{7,5},{8,10},{9,11},{10,... | collective-permute-start | bytes 98312 | tf_op jit(solution)/shard_map/ppermute | solution.py:633
  42.9 3.7 %collective-permute-start.12 = (bf16[4,32,128]{2,1,0:T(8,128)(2,1)S(1)}, bf16[4,32,128]{2,1,0:T(8,128)(2,1)S(1)}, u32[]{:S(2)}, u32[]{:S(2)}) collective-permute-start(bf16[4,32,128]{2,1,0:T(8,128)(2,1)S(1)} %get-tuple-element.80), channel_id=1, source_target_pairs={{0,3},{1,2},{2,1},{3,0},{4,7},{5,6},{6,5},{7,4},{8,11},{9,10},{10,... | collective-permute-start | bytes 98312 | tf_op jit(solution)/shard_map/ppermute | solution.py:633
  43.8 2.8 %copy-start.2 = (s32[8]{0:T(128)S(1)}, s32[8]{0:T(128)}, u32[]{:S(2)}) copy-start(s32[8]{0:T(128)} %offsets.3) | copy-start | bytes 100

commit v8 on v7

--- a/solution.py
+++ b/solution.py
@@ -12,16 +12,13 @@
 H = 4
 HD = 32
 NB = 64
-FWD_ROWS = 8
-BWD_ROWS = 8
 FWD_PACE = (8, 1, 0)
-BWD_PACE = (2, 0, 3)
+BWD_PACE = (4, 1, 0)
 PROJ_PACE = (2, 0, 3)
 FIN_PACE = (8, 1, 0)
 MID_PACE = (8, 1, 0)
-PROJ_ROWS = 8
-FIN_ROWS = 8
 EPS = 1e-5
+BLOCK = 8
 LOG2E = 1.0 / math.log(2.0)
 BF = jnp.bfloat16
 F32 = jnp.float32
@@ -77,6 +74,18 @@
         tick += 1
 
 
+def blocks_of(refs, block):
+    return [ref.at[pl.ds(pl.multiple_of(block * BLOCK, BLOCK), BLOCK)] for ref in refs]
+
+
+def loop_blocks(rows, body):
+    def one(block, carry):
+        body(block)
+        return carry
+
+    lax.fori_loop(0, rows // BLOCK, one, 0)
+
+
 def full(shape):
     return pl.BlockSpec(shape, lambda *_: (0,) * len(shape))
 
@@ -93,45 +102,54 @@
 def middle_kernel(after, zr, wq, wk, wv, wg, ob, wd, db, wpb, lng, nrm, inv, wd3, wall, lgc, cst, wgs):
     del after
     rows, wide, chans = zr.shape
-
-    @pl.when(pl.program_id(0) == 0)
-    def _():
-        wall[...] = jnp.concatenate([wq[...], wk[...], wv[...], wg[...]], axis=1)
-        dist_hi, dist_lo = split(wd[...].T)
-        wd3[...] = jnp.concatenate([dist_hi, dist_hi, dist_lo], axis=1)
-        lgc[...] = column(lng[...], wide)
-        shift = 2.0 * jnp.sum(wd[...] * ob[...], axis=1, keepdims=True)
-        cst[...] = column(db[...], wide) + shift
-        proj = wpb[...] * lng[...]
-        proj = jnp.concatenate([proj, jnp.zeros((wide - H, chans), F32)], axis=0).T[:, :H]
-        proj_hi, proj_lo = split(proj)
-        wgs[...] = jnp.concatenate([proj_hi, proj_hi, proj_lo, jnp.zeros_like(proj_lo)], axis=1)
+    wall[...] = jnp.concatenate([wq[...], wk[...], wv[...], wg[...]], axis=1)
+    dist_hi, dist_lo = split(wd[...].T)
+    wd3[...] = jnp.concatenate([dist_hi, dist_hi, dist_lo], axis=1)
+    lgc[...] = column(lng[...], wide)
+    shift = 2.0 * jnp.sum(wd[...] * ob[...], axis=1, keepdims=True)
+    cst[...] = column(db[...], wide) + shift
+    proj = wpb[...] * lng[...]
+    proj = jnp.concatenate([proj, jnp.zeros((wide - H, chans), F32)], axis=0).T[:, :H]
+    proj_hi, proj_lo = split(proj)
+    wgs[...] = jnp.concatenate([proj_hi, proj_hi, proj_lo, jnp.zeros_like(proj_lo)], axis=1)
 
     ident = eye(chans)
 
-    def one_row(row):
-        pair_t = nt(ident, zr[row])
-        yield
-        center = pair_t - jnp.mean(pair_t, axis=0, keepdims=True)
-        yield
-        inverse = lax.rsqrt(jnp.mean(center * center, axis=0, keepdims=True) + EPS)
-        inv[row : row + 1, :] = inverse
-        nrm[row] = center * inverse
-        yield
-
-    interleave([one_row(row) for row in range(rows)], MID_PACE)
+    def one_block(step):
+        zr_b, nrm_b, inv_b = blocks_of((zr, nrm, inv), step)
+
+        def one_row(row):
+            pair_t = nt(ident, zr_b[row])
+            yield
+            center = pair_t - jnp.mean(pair_t, axis=0, keepdims=True)
+            yield
+            inverse = lax.rsqrt(jnp.mean(center * center, axis=0, keepdims=True) + EPS)
+            inv_b[row : row + 1, :] = inverse
+            nrm_b[row] = center * inverse
+            yield
+
+        interleave([one_row(row) for row in range(BLOCK)], MID_PACE)
+
+    loop_blocks(rows, one_block)
 
 
 def main_kernel(dpt, dzn, nrm, inv, lgc, base):
-    def one_row(row):
-        scaled = dzn[row] * lgc[...]
-        mean_a = jnp.mean(scaled, axis=0, keepdims=True)
-        mean_b = jnp.mean(scaled * nrm[row], axis=0, keepdims=True)
-        yield
-        base[row] = dpt[row] + inv[row : row + 1, :] * (scaled - mean_a - nrm[row] * mean_b)
-        yield
-
-    interleave([one_row(row) for row in range(dzn.shape[0])], MID_PACE)
+    def one_block(step):
+        dpt_b, dzn_b, nrm_b, inv_b, base_b = blocks_of((dpt, dzn, nrm, inv, base), step)
+
+        def one_row(row):
+            scaled = dzn_b[row] * lgc[...]
+            mean_a = jnp.mean(scaled, axis=0, keepdims=True)
+            mean_b = jnp.mean(scaled * nrm_b[row], axis=0, keepdims=True)
+            yield
+            base_b[row] = dpt_b[row] + inv_b[row : row + 1, :] * (
+                scaled - mean_a - nrm_b[row] * mean_b
+            )
+            yield
+
+        interleave([one_row(row) for row in range(BLOCK)], MID_PACE)
+
+    loop_blocks(dzn.shape[0], one_block)
 
 
 def bias_kernel(tile, targets, lng, lnb, wpb, out, *, per_head):
@@ -177,6 +195,21 @@
     own = own_ref[0]
     part_refs = refs[:parts]
     lng, lnb, w4t, w2, gbc, zr, qt, kt, vt, kn, vn, gt, flat_s = refs[parts:]
+    loop_blocks(
+        zr.shape[0],
+        lambda step: project_block(
+            own,
+            [part_refs[0].at[step]] + blocks_of(part_refs[1:], step),
+            (lng, lnb, w4t, w2, gbc, flat_s),
+            blocks_of((zr, qt, kt, vt, kn, vn, gt), step),
+        ),
+    )
+
+
+def project_block(own, part_refs, weights, outs):
+    lng, lnb, w4t, w2, gbc, flat_s = weights
+    zr, qt, kt, vt, kn, vn, gt = outs
+    parts = len(part_refs)
     rows, side, _ = part_refs[0].shape
     wide = zr.shape[1]
     width = H * HD
@@ -246,96 +279,97 @@
     at, ot, ut, tgt, bias_t = refs[tiles + 7 + extra : tiles + 12 + extra]
     sends = refs[tiles + 12 + extra : 2 * tiles + 12 + extra]
     order, stage = refs[2 * tiles + 12 + extra :]
-    step = pl.program_id(0)
     mine = lax.axis_index("tile")
     tile_i = mine // grid_side
     tile_j = lax.rem(mine, grid_side)
-    rows = kn.shape[0]
     wide = kn.shape[1]
     side = wide // grid_side
     per_head = side * side // wide
     share = groups * group_rows
     span = side // groups
 
-    @pl.when(step == 0)
-    def _():
-        for k in range(tiles):
-            order[mine ^ k] = gath[k][...]
-        lane = lax.broadcasted_iota(jnp.int32, (per_head, wide), 1) // side
-        for h in range(H):
-            pieces = []
+    for k in range(tiles):
+        order[mine ^ k] = gath[k][...]
+    lane = lax.broadcasted_iota(jnp.int32, (per_head, wide), 1) // side
+    for h in range(H):
+        pieces = []
+        for i in range(grid_side):
+            for f in range(grid_side):
+                total = None
+                for j in range(grid_side):
+                    part = order[i * grid_side + j, h * per_head : (h + 1) * per_head, :]
+                    turn = ((j - f) * side) % wide
+                    if turn:
+                        part = pltpu.roll(part, turn, 1)
+                    total = part if total is None else jnp.where(lane == j, part, total)
+                pieces.append(total)
+        bias_t[h] = jnp.concatenate(pieces, axis=0).T * LOG2E
+
+    whole = (kn, qt, vt, gt, zr, at, ot, ut, tgt)
+
+    def one_block(step):
+        rows = BLOCK
+        kn, qt, vt, gt, zr, at, ot, ut, tgt = blocks_of(whole, step)
+        for row in range(rows):
+            within = (base + step) * span + tile_j * group_rows + row
+            tgt[row : row + 1, :] = order[
+                within // owner_rows,
+                pl.ds(bias_rows + lax.rem(within, owner_rows) * grid_side + tile_i, 1),
+                :,
+            ]
+
+        scale = LOG2E / math.sqrt(HD)
+
+        def one_row(row):
+            blocks = head_blocks(qt[row])
+            outs = []
+            for pair in range(0, H, 2):
+                scores = nn(kn[row], blocks[:, pair * wide : (pair + 2) * wide])
+                yield
+                for h in range(pair, pair + 2):
+                    part = scores[:, (h - pair) * wide : (h - pair + 1) * wide] * scale + bias_t[h]
+                    peak = jnp.max(part, axis=0, keepdims=True)
+                    yield
+                    part = jnp.exp2(part - peak)
+                    total = jnp.sum(part, axis=0, keepdims=True)
+                    yield
+                    part_b = (part * (1.0 / total)).astype(BF)
+                    at[row, :, h * wide : (h + 1) * wide] = part_b
+                    yield
+                    outs.append(nn(vt[row, h * HD : (h + 1) * HD, :], part_b))
+                    ot[row, h * HD : (h + 1) * HD, :] = outs[-1]
+                    yield
+            gated = (gt[row] * ot[row]).astype(BF)
+            yield
+            both = nn(wod[...], gated) + nt(wdt[...], zr[row])
+            yield
+            logit = both[:NB] + both[NB:]
+            ut[row] = logit
+            logit = logit - jnp.max(logit, axis=0, keepdims=True)
+            yield
+            packed = jnp.concatenate([logit, logit], axis=0).T
+            here = step * rows + row
+            yield
             for i in range(grid_side):
-                for f in range(grid_side):
-                    total = None
+                for p in range(groups):
                     for j in range(grid_side):
-                        part = order[i * grid_side + j, h * per_head : (h + 1) * per_head, :]
-                        turn = ((j - f) * side) % wide
-                        if turn:
-                            part = pltpu.roll(part, turn, 1)
-                        total = part if total is None else jnp.where(lane == j, part, total)
-                    pieces.append(total)
-            bias_t[h] = jnp.concatenate(pieces, axis=0).T * LOG2E
-
-    for row in range(rows):
-        within = (base + step) * span + tile_j * group_rows + row
-        tgt[row : row + 1, :] = order[
-            within // owner_rows,
-            pl.ds(bias_rows + lax.rem(within, owner_rows) * grid_side + tile_i, 1),
-            :,
-        ]
-
-    scale = LOG2E / math.sqrt(HD)
-
-    def one_row(row):
-        blocks = head_blocks(qt[row])
-        outs = []
-        for pair in range(0, H, 2):
-            scores = nn(kn[row], blocks[:, pair * wide : (pair + 2) * wide])
-            yield
-            for h in range(pair, pair + 2):
-                part = scores[:, (h - pair) * wide : (h - pair + 1) * wide] * scale + bias_t[h]
-                peak = jnp.max(part, axis=0, keepdims=True)
-                yield
-                part = jnp.exp2(part - peak)
-                total = jnp.sum(part, axis=0, keepdims=True)
-                yield
-                part_b = (part * (1.0 / total)).astype(BF)
-                at[row, :, h * wide : (h + 1) * wide] = part_b
-                yield
-                outs.append(nn(vt[row, h * HD : (h + 1) * HD, :], part_b))
-                ot[row, h * HD : (h + 1) * HD, :] = outs[-1]
-                yield
-        gated = (gt[row] * ot[row]).astype(BF)
-        yield
-        both = nn(wod[...], gated) + nt(wdt[...], zr[row])
-        yield
-        logit = both[:NB] + both[NB:]
-        ut[row] = logit
-        logit = logit - jnp.max(logit, axis=0, keepdims=True)
-        yield
-        packed = jnp.concatenate([logit, logit], axis=0).T
-        here = step * rows + row
-        yield
-        for i in range(grid_side):
-            for p in range(groups):
-                for j in range(grid_side):
-                    source = ((i * groups + p) * grid_side + j) * group_rows
-                    target = ((i * grid_side + j) * share + p * group_rows) * count
-                    stage[pl.ds(target + here, group_rows, stride=count), :] = packed[
-                        source : source + group_rows
-                    ]
-                yield
-
-    interleave([one_row(row) for row in range(rows)], FWD_PACE)
-
-    @pl.when(step == pl.num_programs(0) - 1)
-    def _():
-        left = lax.broadcasted_iota(jnp.int32, (count // 2, 2 * NB), 1) < NB
-        for k in range(tiles):
-            start = (mine ^ k) * (share * count)
-            for r in range(share):
-                both = stage[pl.ds(pl.multiple_of(start + r * count, 8), count), :]
-                sends[k][r] = jnp.where(left, both[: count // 2], both[count // 2 :]).astype(BF)
+                        source = ((i * groups + p) * grid_side + j) * group_rows
+                        target = ((i * grid_side + j) * share + p * group_rows) * count
+                        stage[pl.ds(target + here, group_rows, stride=count), :] = packed[
+                            source : source + group_rows
+                        ]
+                    yield
+
+        interleave([one_row(row) for row in range(rows)], FWD_PACE)
+
+    loop_blocks(count, one_block)
+
+    left = lax.broadcasted_iota(jnp.int32, (count // 2, 2 * NB), 1) < NB
+    for k in range(tiles):
+        start = (mine ^ k) * (share * count)
+        for r in range(share):
+            both = stage[pl.ds(pl.multiple_of(start + r * count, 8), count), :]
+            sends[k][r] = jnp.where(left, both[: count // 2], both[count // 2 :]).astype(BF)
 
 
 def backward_kernel(*refs, tiles, chunks, grid_side, groups, group_rows):
@@ -346,9 +380,7 @@
     sends = refs[tiles * chunks + 14 : tiles * chunks + 14 + tiles]
     acc, grad_s, back_s, mirror_s, order = refs[tiles * chunks + 14 + tiles :]
     width = H * HD
-    step = pl.program_id(0)
     mine = lax.axis_index("tile")
-    rows = vn.shape[0]
     wide = vn.shape[1]
     chunk_groups = groups // chunks
     share = groups * group_rows
@@ -356,152 +388,158 @@
     adder = jnp.concatenate([eye(NB)] * 2, axis=1)
     bins = lax.broadcasted_iota(jnp.int32, (NB, 2 * wide), 0).astype(F32)
 
-    @pl.when(step == 0)
-    def _():
-        acc[...] = jnp.zeros_like(acc)
+    acc[...] = jnp.zeros_like(acc)
 
     shift = jnp.concatenate([cst[...]] * 2, axis=1)
     left = lax.broadcasted_iota(jnp.int32, (rcv[0].shape[1], 2 * NB), 1) < NB
 
-    def one_pair(first):
-        pair = (first, first + 1)
-        for row in pair:
-            for k in range(tiles):
-                source_i = (mine ^ k) // grid_side
-                source_j = lax.rem(mine ^ k, grid_side)
-                for c in range(chunks):
-                    part = rcv[c * tiles + k][row].astype(F32)
-                    part = jnp.concatenate(
-                        [jnp.where(left, part, 0.0), jnp.where(left, 0.0, part)], axis=0
-                    )
-                    for p in range(chunk_groups):
-                        start = (
-                            (source_i * groups + c * chunk_groups + p) * grid_side + source_j
-                        ) * group_rows + row * wide
-                        mirror_s[pl.ds(pl.multiple_of(start, group_rows), group_rows), :] = part[
-                            p * group_rows : (p + 1) * group_rows
-                        ]
-        yield
-        other = nt(adder, mirror_s[first * wide : (first + 2) * wide, :].astype(BF))
-        yield
-        logits = jnp.concatenate([ut[row] for row in pair], axis=1) + other + shift
-        peak = jnp.max(logits, axis=0, keepdims=True)
-        yield
-        probs = jnp.exp(logits - peak)
-        total = jnp.sum(probs, axis=0, keepdims=True)
-        yield
-        target = jnp.concatenate([tgt[row : row + 1, :] for row in pair], axis=1)
-        resid = 2.0 * (probs * (1.0 / total) - jnp.where(bins == target, 1.0, 0.0))
-        res_hi, res_lo = split(resid)
-        yield
-        pair_grad = nn(wd3[...], jnp.concatenate([res_hi, res_lo, res_hi], axis=0))
-        for n, row in enumerate(pair):
-            dpt[row] = pair_grad[:, n * wide : (n + 1) * wide]
-        yield
-        out_grad = nn(wo[...], pair_grad.astype(BF))
-        yield
-        for n, row in enumerate(pair):
-            gate = gt[row]
-            gated = out_grad[:, n * wide : (n + 1) * wide] * gate
-            grad_s[row] = gated.astype(BF)
-            back_s[3 * width :, row * wide : (row + 1) * wide] = (
-                gated * ot[row] * (1.0 - gate)
-            ).astype(BF)
-            yield
-
-        def heads(row):
-            lanes = slice(row * wide, (row + 1) * wide)
-            for h in range(H):
-                part = slice(h * HD, (h + 1) * HD)
-                back_s[2 * width + h * HD : 2 * width + (h + 1) * HD, lanes] = nt(
-                    grad_s[row, part, :], at[row, :, h * wide : (h + 1) * wide]
+    whole = (tgt, at, ot, ut, gt, vn, kt, qt, dpt, dzn) + tuple(rcv)
+
+    def one_block(step):
+        rows = BLOCK
+        tgt, at, ot, ut, gt, vn, kt, qt, dpt, dzn, *rcv = blocks_of(whole, step)
+
+        def one_pair(first):
+            pair = (first, first + 1)
+            for row in pair:
+                for k in range(tiles):
+                    source_i = (mine ^ k) // grid_side
+                    source_j = lax.rem(mine ^ k, grid_side)
+                    for c in range(chunks):
+                        part = rcv[c * tiles + k][row].astype(F32)
+                        part = jnp.concatenate(
+                            [jnp.where(left, part, 0.0), jnp.where(left, 0.0, part)], axis=0
+                        )
+                        for p in range(chunk_groups):
+                            start = (
+                                (source_i * groups + c * chunk_groups + p) * grid_side + source_j
+                            ) * group_rows + row * wide
+                            mirror_s[pl.ds(pl.multiple_of(start, group_rows), group_rows), :] = part[
+                                p * group_rows : (p + 1) * group_rows
+                            ]
+            yield
+            other = nt(adder, mirror_s[first * wide : (first + 2) * wide, :].astype(BF))
+            yield
+            logits = jnp.concatenate([ut[row] for row in pair], axis=1) + other + shift
+            peak = jnp.max(logits, axis=0, keepdims=True)
+            yield
+            probs = jnp.exp(logits - peak)
+            total = jnp.sum(probs, axis=0, keepdims=True)
+            yield
+            target = jnp.concatenate([tgt[row : row + 1, :] for row in pair], axis=1)
+            resid = 2.0 * (probs * (1.0 / total) - jnp.where(bins == target, 1.0, 0.0))
+            res_hi, res_lo = split(resid)
+            yield
+            pair_grad = nn(wd3[...], jnp.concatenate([res_hi, res_lo, res_hi], axis=0))
+            for n, row in enumerate(pair):
+                dpt[row] = pair_grad[:, n * wide : (n + 1) * wide]
+            yield
+            out_grad = nn(wo[...], pair_grad.astype(BF))
+            yield
+            for n, row in enumerate(pair):
+                gate = gt[row]
+                gated = out_grad[:, n * wide : (n + 1) * wide] * gate
+                grad_s[row] = gated.astype(BF)
+                back_s[3 * width :, row * wide : (row + 1) * wide] = (
+                    gated * ot[row] * (1.0 - gate)
                 ).astype(BF)
                 yield
-                weight_grad = nn(vn[row], head_block(grad_s[row, part, :], h))
+
+            def heads(row):
+                lanes = slice(row * wide, (row + 1) * wide)
+                for h in range(H):
+                    part = slice(h * HD, (h + 1) * HD)
+                    back_s[2 * width + h * HD : 2 * width + (h + 1) * HD, lanes] = nt(
+                        grad_s[row, part, :], at[row, :, h * wide : (h + 1) * wide]
+                    ).astype(BF)
+                    yield
+                    weight_grad = nn(vn[row], head_block(grad_s[row, part, :], h))
+                    yield
+                    prob = at[row, :, h * wide : (h + 1) * wide].astype(F32)
+                    prod = prob * weight_grad
+                    total = jnp.sum(prod, axis=0, keepdims=True)
+                    yield
+                    prod = prod - prob * total
+                    prod_b = prod.astype(BF)
+                    acc[h] += prod
+                    yield
+                    back_s[h * HD : (h + 1) * HD, lanes] = (nn(kt[row, part, :], prod_b) * inv_root).astype(BF)
+                    back_s[width + h * HD : width + (h + 1) * HD, lanes] = (
+                        nt(qt[row, part, :], prod_b) * inv_root
+                    ).astype(BF)
+                    yield
+
+            both = [heads(row) for row in pair]
+            while both:
+                for row in list(both):
+                    try:
+                        next(row)
+                    except StopIteration:
+                        both.remove(row)
                 yield
-                prob = at[row, :, h * wide : (h + 1) * wide].astype(F32)
-                prod = prob * weight_grad
-                total = jnp.sum(prod, axis=0, keepdims=True)
-                yield
-                prod = prod - prob * total
-                prod_b = prod.astype(BF)
-                acc[h] += prod
-                yield
-                back_s[h * HD : (h + 1) * HD, lanes] = (nn(kt[row, part, :], prod_b) * inv_root).astype(BF)
-                back_s[width + h * HD : width + (h + 1) * HD, lanes] = (
-                    nt(qt[row, part, :], prod_b) * inv_root
-                ).astype(BF)
-                yield
-
-        both = [heads(row) for row in pair]
-        while both:
-            for row in list(both):
-                try:
-                    next(row)
-                except StopIteration:
-                    both.remove(row)
-            yield
-        normed_grad = nn(wall[...], back_s[:, first * wide : (first + 2) * wide])
-        for n, row in enumerate(pair):
-            dzn[row] = normed_grad[:, n * wide : (n + 1) * wide]
-        yield
-
-    interleave([one_pair(row) for row in range(0, rows, 2)], BWD_PACE)
-
-    @pl.when(step == pl.num_programs(0) - 1)
-    def _():
-        for h in range(H):
-            grad = acc[h].T
-            for i in range(grid_side):
-                for j in range(grid_side):
-                    pieces = []
-                    for p in range(groups):
-                        source = ((i * groups + p) * grid_side + j) * group_rows
-                        pieces.append(grad[source : source + group_rows])
-                    order[i * grid_side + j, h * share : (h + 1) * share, :] = jnp.concatenate(
-                        pieces, axis=0
-                    )
-        for k in range(tiles):
-            sends[k][...] = order[mine ^ k].reshape(H, share, wide).astype(BF)
+            normed_grad = nn(wall[...], back_s[:, first * wide : (first + 2) * wide])
+            for n, row in enumerate(pair):
+                dzn[row] = normed_grad[:, n * wide : (n + 1) * wide]
+            yield
+
+        interleave([one_pair(row) for row in range(0, rows, 2)], BWD_PACE)
+
+    loop_blocks(share, one_block)
+
+    for h in range(H):
+        grad = acc[h].T
+        for i in range(grid_side):
+            for j in range(grid_side):
+                pieces = []
+                for p in range(groups):
+                    source = ((i * groups + p) * grid_side + j) * group_rows
+                    pieces.append(grad[source : source + group_rows])
+                order[i * grid_side + j, h * share : (h + 1) * share, :] = jnp.concatenate(
+                    pieces, axis=0
+                )
+    for k in range(tiles):
+        sends[k][...] = order[mine ^ k].reshape(H, share, wide).astype(BF)
 
 
 def finish_kernel(offsets, *refs, tiles):
     rdb = refs[:tiles]
     base, nrm, inv, wgs, out, sums = refs[tiles:]
-    step = pl.program_id(0)
-    rows, chans, wide = base.shape
+    share, chans, wide = base.shape
     states, _, piece, _ = out.shape
     total_rows = rdb[0].shape[1]
     turn = offsets[lax.axis_index("state")] // piece
 
-    @pl.when(step == 0)
-    def _():
-        for h in range(H):
-            total = rdb[0][h].astype(F32)
-            for part in rdb[1:]:
-                total = total + part[h].astype(F32)
-            sums[pl.ds(h * total_rows, total_rows), :] = total
-
-    def one_row(row):
-        local = step * rows + row
-        parts = [sums[pl.ds(h * total_rows + local, 1), :] for h in range(H)]
-        high, low = split(jnp.concatenate(parts, axis=0))
-        high, low = high.astype(F32), low.astype(F32)
-        spread = jnp.concatenate([high, low, high, jnp.zeros((H, wide), F32)], axis=0)
-        yield
-        scaled = nn(wgs[...], spread.astype(BF))
-        yield
-        mean_a = jnp.mean(scaled, axis=0, keepdims=True)
-        mean_b = jnp.mean(scaled * nrm[row], axis=0, keepdims=True)
-        yield
-        total = base[row] + inv[row : row + 1, :] * (scaled - mean_a - nrm[row] * mean_b)
-        yield
-        total = total.T.astype(BF)
-        for c in range(wide // piece):
-            out[lax.rem(turn + c, states), row] = total[c * piece : (c + 1) * piece]
-        yield
-
-    interleave([one_row(row) for row in range(rows)], FIN_PACE)
+    for h in range(H):
+        total = rdb[0][h].astype(F32)
+        for part in rdb[1:]:
+            total = total + part[h].astype(F32)
+        sums[pl.ds(h * total_rows, total_rows), :] = total
+
+    def one_block(step):
+        base_b, nrm_b, inv_b = blocks_of((base, nrm, inv), step)
+
+        def one_row(row):
+            local = step * BLOCK + row
+            parts = [sums[pl.ds(h * total_rows + local, 1), :] for h in range(H)]
+            high, low = split(jnp.concatenate(parts, axis=0))
+            high, low = high.astype(F32), low.astype(F32)
+            spread = jnp.concatenate([high, low, high, jnp.zeros((H, wide), F32)], axis=0)
+            yield
+            scaled = nn(wgs[...], spread.astype(BF))
+            yield
+            mean_a = jnp.mean(scaled, axis=0, keepdims=True)
+            mean_b = jnp.mean(scaled * nrm_b[row], axis=0, keepdims=True)
+            yield
+            total = base_b[row] + inv_b[row : row + 1, :] * (scaled - mean_a - nrm_b[row] * mean_b)
+            yield
+            total = total.T.astype(BF)
+            for c in range(wide // piece):
+                out[lax.rem(turn + c, states), local] = total[c * piece : (c + 1) * piece]
+            yield
+
+        interleave([one_row(row) for row in range(BLOCK)], FIN_PACE)
+
+    loop_blocks(share, one_block)
 
 
 def place_kernel(offsets, rcv, out, *, side):
@@ -599,7 +637,7 @@
         )
     )
 
-    lines = 8
+    lines = per_head
     bias_rows = H * per_head
     target_rows = owner_rows * grid_side
     bias_mine = pl.pallas_call(
@@ -646,15 +684,15 @@
         functools.partial(project_kernel, parts=grid_side),
         grid_spec=pltpu.PrefetchScalarGridSpec(
             num_scalar_prefetch=1,
-            grid=(groups,),
+            grid=(1,),
             in_specs=[
                 pl.BlockSpec(
-                    (None, None, group_rows, side, chans), lambda g, own: (g, own[0], 0, 0, 0)
+                    (groups, None, group_rows, side, chans), lambda g, own: (0, own[0], 0, 0, 0)
                 )
             ]
-            + [by_row(side, chans, rows=group_rows)] * (grid_side - 1)
+            + [by_row(side, chans, rows=share)] * (grid_side - 1)
             + [full((1, chans)), full((1, chans)), full(w4t.shape), full(w2.shape), full(gbc.shape)],
-            out_specs=[by_row(wide, width, rows=group_rows)] * 7,
+            out_specs=[by_row(wide, width, rows=share)] * 7,
             scratch_shapes=[pltpu.VMEM((group_rows * wide, chans), BF)],
         ),
         out_shape=shapes(*([square_b] * 6), ((share, width, wide), F32)),
@@ -666,7 +704,6 @@
     chunks = 2 if groups % 2 == 0 else 1
     chunk_groups = groups // chunks
     count = share // chunks
-    block = group_rows
     layout = dict(grid_side=grid_side, groups=groups, group_rows=group_rows)
     saved_shapes = shapes(
         ((share, wide, H * wide), BF),
@@ -693,16 +730,16 @@
                 extra=len(saved),
                 **layout,
             ),
-            grid=(count // block,),
+            grid=(1,),
             in_specs=[full(gathered[0].shape)] * tiles
-            + [by_row(wide, width, rows=block, base=base)] * 5
+            + [by_row(wide, width, rows=count, base=c)] * 5
             + [full(wod.shape), full(wdt.shape)]
             + [pl.BlockSpec(memory_space=pl.ANY)] * len(saved),
             out_specs=[
-                by_row(wide, H * wide, rows=block, base=base),
-                by_row(width, wide, rows=block, base=base),
-                by_row(NB, wide, rows=block, base=base),
-                by_row(wide, rows=block, base=base),
+                by_row(wide, H * wide, rows=count, base=c),
+                by_row(width, wide, rows=count, base=c),
+                by_row(NB, wide, rows=count, base=c),
+                by_row(wide, rows=count, base=c),
                 full((H, wide, wide)),
             ]
             + [full(packed_shape)] * tiles,
@@ -741,10 +778,10 @@
     )
     nrm, inv, wd3, wall, lgc, cst, wgs = pl.pallas_call(
         middle_kernel,
-        grid=(share // block,),
-        in_specs=[pl.BlockSpec((8, wide), lambda g: (0, 0)), by_row(wide, chans, rows=block)]
+        grid=(1,),
+        in_specs=[pl.BlockSpec((8, wide), lambda g: (0, 0)), by_row(wide, chans, rows=share)]
         + [full(w.shape) for w in late],
-        out_specs=[by_row(chans, wide, rows=block), by_row(wide, rows=block)]
+        out_specs=[by_row(chans, wide, rows=share), by_row(wide, rows=share)]
         + [full(shape) for shape, _ in late_shapes],
         out_shape=shapes(((share, chans, wide), F32), ((share, wide), F32), *late_shapes),
         cost_estimate=cost(20 * share * cell, 3 * share * wide * width * 2),
@@ -754,23 +791,23 @@
 
     results = pl.pallas_call(
         functools.partial(backward_kernel, tiles=tiles, chunks=chunks, **layout),
-        grid=(share // block,),
-        in_specs=[by_row(count // 2, 2 * NB, rows=block)] * (tiles * chunks)
+        grid=(1,),
+        in_specs=[by_row(count // 2, 2 * NB, rows=share)] * (tiles * chunks)
         + [
-            by_row(wide, rows=block),
-            by_row(wide, H * wide, rows=block),
-            by_row(width, wide, rows=block),
-            by_row(NB, wide, rows=block),
+            by_row(wide, rows=share),
+            by_row(wide, H * wide, rows=share),
+            by_row(width, wide, rows=share),
+            by_row(NB, wide, rows=share),
         ]
-        + [by_row(wide, width, rows=block)] * 4
+        + [by_row(wide, width, rows=share)] * 4
         + [full(w.shape) for w in (w_output, wd3, wall, cst)],
-        out_specs=[by_row(chans, wide, rows=block)] * 2 + [full((H, share, wide))] * tiles,
+        out_specs=[by_row(chans, wide, rows=share)] * 2 + [full((H, share, wide))] * tiles,
         out_shape=shapes(*([((share, chans, wide), F32)] * 2), *([((H, share, wide), BF)] * tiles)),
         scratch_shapes=[
             pltpu.VMEM((H, wide, wide), F32),
-            pltpu.VMEM((block, width, wide), BF),
-            pltpu.VMEM((4 * width, block * wide), BF),
-            pltpu.VMEM((block * wide, 2 * NB), F32),
+            pltpu.VMEM((BLOCK, width, wide), BF),
+            pltpu.VMEM((4 * width, BLOCK * wide), BF),
+            pltpu.VMEM((BLOCK * wide, 2 * NB), F32),
             pltpu.VMEM((tiles, H * share, wide), F32),
         ],
         cost_estimate=cost(500 * share * cell, 20 * share * wide * width * 2),
@@ -785,30 +822,29 @@
 
     base = pl.pallas_call(
         main_kernel,
-        grid=(share // block,),
-        in_specs=[by_row(chans, wide, rows=block)] * 3
-        + [by_row(wide, rows=block), full(lgc.shape)],
-        out_specs=by_row(chans, wide, rows=block),
+        grid=(1,),
+        in_specs=[by_row(chans, wide, rows=share)] * 3
+        + [by_row(wide, rows=share), full(lgc.shape)],
+        out_specs=by_row(chans, wide, rows=share),
         out_shape=jax.ShapeDtypeStruct((share, chans, wide), F32),
         cost_estimate=cost(20 * share * cell, 8 * share * wide * width * 2),
         name="main",
         compiler_params=pltpu.CompilerParams(vmem_limit_bytes=VMEM_BYTES),
     )(dpt, dzn, nrm, inv, lgc)
 
-    block = FIN_ROWS if share % FIN_ROWS == 0 else 1
     outgoing = pl.pallas_call(
         functools.partial(finish_kernel, tiles=tiles),
         grid_spec=pltpu.PrefetchScalarGridSpec(
             num_scalar_prefetch=1,
-            grid=(share // block,),
+            grid=(1,),
             in_specs=[
                 *([full(rdb[0].shape)] * tiles),
-                by_row(chans, wide, rows=block),
-                by_row(chans, wide, rows=block),
-                by_row(wide, rows=block),
+                by_row(chans, wide, rows=share),
+                by_row(chans, wide, rows=share),
+                by_row(wide, rows=share),
                 full(wgs.shape),
             ],
-            out_specs=pl.BlockSpec((states, block, piece, chans), lambda g, _: (0, g, 0, 0)),
+            out_specs=pl.BlockSpec((states, share, piece, chans), lambda g, _: (0, g, 0, 0)),
             scratch_shapes=[pltpu.VMEM((H * share, wide), F32)],
         ),
         out_shape=jax.ShapeDtypeStruct((states, share, piece, chans), BF),
@@ -835,7 +871,7 @@
             keepdims=False,
         )
 
-    block = 4 if owner_rows % 4 == 0 else 1
+    block = owner_rows
     out_shape = (2 * grid_side, owner_rows, 2, piece, chans)
     placed = pl.pallas_call(
         functools.partial(place_kernel, side=side),

time: 83 us -> 80.3 us (0.967)
  Pallas kernels: 36.7 us -> 34 us
    pallas_call x1, Pallas kernels: 3.04 us -> 2.07 us  [on_device(): pl.pallas_call(functools.partial(bias_kernel, per_head=per_head), grid=(p...]
    pallas_call x1, Pallas kernels: 12.2 us -> 11.3 us  [on_device(): pl.pallas_call(functools.partial(backward_kernel, tiles=tiles, chunks=chu...]
  transfers between devices with their start and end apart: 13 -> 13, of which waited for: 3 -> 3; matrix products, arithmetic and copies ran while one was open for 0% -> 0% of each run, Pallas kernels for 19% -> 18%
where the time goes in v8:
time: 80.3 us; the launch traced here: 80 us
  Pallas kernels  34 us (42%)
  blocking collectives  31.2 us (39%)
  starting transfers between devices  9.83 us (12%)
  waiting for transfers between devices  3.63 us (5%)
  local copies, waits for them, and re-layouts  1.18 us (1%)
    all_to_all x1, blocking collectives, on_device(): lax.all_to_all(slots, ('state', 'tile'), split_axis=0, concat_axis=0, til...  31.2 us
    pallas_call x1, Pallas kernels, on_device(): pl.pallas_call(functools.partial(backward_kernel, tiles=tiles, chunks=chu...  11.3 us
    ppermute x12, starting transfers between devices, to_partner(): lax.ppermute(value, 'tile', [(t, t ^ k) for t in range(tiles)])  9.26 us
    pallas_call x2, Pallas kernels, on_device(): results = call(*inputs, *saved)  8.51 us
    ppermute x12, waiting for transfers between devices, to_partner(): lax.ppermute(value, 'tile', [(t, t ^ k) for t in range(tiles)])  3.63 us
    pallas_call x1, Pallas kernels, on_device(): pl.pallas_call(functools.partial(project_kernel, parts=grid_side), grid_s...  3.6 us
    pallas_call x1, Pallas kernels, on_device(): pl.pallas_call(middle_kernel, grid=(1,), in_specs=[pl.BlockSpec((8, wide)...  2.6 us
    pallas_call x1, Pallas kernels, on_device(): pl.pallas_call(functools.partial(finish_kernel, tiles=tiles), grid_spec=p...  2.23 us
  transfers between devices with their start and end apart: 13, of which 3 were waited for; matrix products, arithmetic and copies ran while one was open for 0% of the time, Pallas kernels for 18%

profile of v8, /device:TPU:0, one launch (start us, length us, event | category | flops | bytes accessed | tf_op | source)
XLA Modules:
  0.0 80.0 jit_solution(13757300975369586497)
XLA Ops:
  0.0 0.0 copy-start
  0.0 0.0 copy-start.3
  0.0 0.0 copy-start.4
  0.0 1.2 %constant_dynamic-slice_fusion = bf16[4,1,8,64,128]{4,3,2,1,0:T(8,128)(2,1)S(1)} fusion(bf16[4,2,8,64,128]{4,3,2,1,0:T(8,128)(2,1)} %bitcast.19, s32[]{:T(128)S(6)} %select_n.4), kind=kLoop, calls=%fused_computation | loop fusion | bytes 1048580 | tf_op jit(solution)/shard_map/jit(dynamic_index_in_dim)/dynamic_slice | solution.py:600
  1.2 0.6 collective-permute-start.3
  1.8 2.1 %bias.1.refs_0_ = f32[160,128]{1,0:T(8,128)S(1)} custom-call(bf16[2,32,64,128]{3,2,1,0:T(8,128)(2,1)} %bitcast.20, s32[32,128]{1,0:T(8,128)} %bitcast.30, f32[1,128]{1,0:T(1,128)} %bitcast.24, f32[1,128]{1,0:T(1,128)} %bitcast.22, f32[4,128]{1,0:T(4,128)} %bitcast.31), custom_call_target="tpu_custom_call" | custom-call | tf_op jit(solution)/shard_map/bias/pallas_call | solution.py:643
  3.8 2.7 %collective-permute-start.2 = (f32[160,128]{1,0:T(8,128)S(1)}, f32[160,128]{1,0:T(8,128)S(1)}, u32[]{:S(2)}, u32[]{:S(2)}) collective-permute-start(f32[160,128]{1,0:T(8,128)S(1)} %bias.1.refs_0_), channel_id=1, source_target_pairs={{0,3},{1,2},{2,1},{3,0},{4,7},{5,6},{6,5},{7,4},{8,11},{9,10},{10,... | collective-permute-start | bytes 245768 | tf_op jit(solution)/shard_map/ppermute | solution.py:671
  6.5 0.0 collective-permute-start.1
  6.5 0.2 collective-permute-start
  6.7 1.1 %prep.1 = (bf16[512,128]{1,0:T(8,128)(2,1)S(1)}, bf16[128,256]{1,0:T(8,128)(2,1)S(1)}, bf16[128,128]{1,0:T(8,128)(2,1)S(1)}, bf16[128,128]{1,0:T(8,128)(2,1)S(1)}, f32[128,128]{1,0:T(8,128)S(1)}) custom-call(bf16[128,128]{1,0:T(8,128)(2,1)} %wq.3, bf16[128,128]{1,0:T(8,128)(2,1)} %wk.3, bf16[128,128]{1,0:T(8,128)(2,1)} %wv.3, bf16[128,128]{1,0:T(8,128)(2,1)} %wg.3, ...), custom_call_target="tpu_custom_call" | custom-call | tf_op jit(solution)/shard_map/prep/pallas_call | solution.py:620
  7.8 0.0 collective-permute-done.3.refs_1_
  7.8 0.0 copy-done
  7.8 0.0 copy-done.3
  7.8 0.0 copy-done.4
  7.8 3.6 %project.1 = (bf16[32,128,128]{2,1,0:T(8,128)(2,1)S(1)}, bf16[32,128,128]{2,1,0:T(8,128)(2,1)S(1)}, bf16[32,128,128]{2,1,0:T(8,128)(2,1)S(1)}, bf16[32,128,128]{...) custom-call(s32[1]{0:T(128)} %bitcast.5.own_ref, ...), custom_call_target="tpu_custom_call" | custom-call | flops 5368709120 | bytes 12582912 | tf_op jit(solution)/shard_map/project/pallas_call | solution.py:683
  11.4 0.0 collective-permute-done.2.refs_3_
  11.4 0.0 collective-permute-done.1.refs_2_
  11.5 0.0 collective-permute-done.refs_1_
  11.5 4.3 %forward.2 = (bf16[32,128,512]{2,1,0:T(8,128)(2,1)S(1)}, f32[32,128,128]{2,1,0:T(8,128)S(1)}, f32[32,64,128]{2,1,0:T(8,128)S(1)}, f32[32,128]{1,0:T(8,128)S(1)},...) custom-call(f32[160,128]{1,0:T(8,128)S(1)} %bias.1.refs_0_, ...), custom_call_target="tpu_custom_call" | custom-call | flops 5033164800 | bytes 7340032 | tf_op jit(solution)/shard_map/forward/pallas_call | solution.py:756
  15.7 0.3 collective-permute-start.4
  16.0 2.0 %collective-permute-start.5 = (bf16[32,8,128]{2,1,0:T(8,128)(2,1)S(1)}, bf16[32,8,128]{2,1,0:T(8,128)(2,1)S(1)}, u32[]{:S(2)}, u32[]{:S(2)}) collective-permute-start(bf16[32,8,128]{2,1,0:T(8,128)(2,1)S(1)} %get-tuple-element.58), channel_id=1, source_target_pairs={{0,2},{1,3},{2,0},{3,1},{4,6},{5,7},{6,4},{7,5},{8,10},{9,11},{10,... | collective-permute-start | bytes 196616 | tf_op jit(solution)/shard_map/ppermute | solution.py:671
  18.1 0.0 collective-permute-start.6
  18.1 4.3 %forward.3 = (bf16[32,128,512]{2,1,0:T(8,128)(2,1)S(1)}, f32[32,128,128]{2,1,0:T(8,128)S(1)}, f32[32,64,128]{2,1,0:T(8,128)S(1)}, f32[32,128]{1,0:T(8,128)S(1)},...) custom-call(f32[160,128]{1,0:T(8,128)S(1)} %bias.1.refs_0_, ...), custom_call_target="tpu_custom_call", output_to_operand_aliasing={{0}: (11, {}), {1}: (12, {}), {2}: (13, {}), {3}: (14, {})} | custom-call | flops 5033164800 | bytes 7340032 | tf_op jit(solution)/shard_map/forward/pallas_call | solution.py:756
  22.3 0.1 collective-permute-start.7
  22.4 2.0 %collective-permute-start.8 = (bf16[32,8,128]{2,1,0:T(8,128)(2,1)S(1)}, bf16[32,8,128]{2,1,0:T(8,128)(2,1)S(1)}, u32[]{:S(2)}, u32[]{:S(2)}) collective-permute-start(bf16[32,8,128]{2,1,0:T(8,128)(2,1)S(1)} %get-tuple-element.66), channel_id=1, source_target_pairs={{0,2},{1,3},{2,0},{3,1},{4,6},{5,7},{6,4},{7,5},{8,10},{9,11},{10,... | collective-permute-start | bytes 196616 | tf_op jit(solution)/shard_map/ppermute | solution.py:671
  24.5 0.0 collective-permute-done.4.refs_1_
  24.5 0.0 collective-permute-start.9
  24.5 0.0 copy-start.1
  24.5 2.6 %middle.1 = (f32[32,128,128]{2,1,0:T(8,128)S(1)}, f32[32,128]{1,0:T(8,128)S(1)}, bf16[128,192]{1,0:T(8,128)(2,1)S(1)}, bf16[128,512]{1,0:T(8,128)(2,1)S(1)}, f32...) custom-call(f32[32,128]{1,0:T(8,128)S(1)} %get-tuple-element.68.after.refs_8_, ...), custom_call_target="tpu_custom_call" | custom-call | flops 1342177280 | bytes 3145728 | tf_op jit(solution)/shard_map/middle/pallas_call | solution.py:779
  27.1 0.0 collective-permute-done.5.refs_2_
  27.1 0.0 collective-permute-done.6.refs_3_
  27.1 0.0 collective-permute-done.7.refs_5_
  27.1 0.0 collective-permute-done.8.refs_6_
  27.1 1.6 %collective-permute-done.9.refs_7_ = bf16[32,8,128]{2,1,0:T(8,128)(2,1)S(1)} collective-permute-done((bf16[32,8,128]{2,1,0:T(8,128)(2,1)S(1)}, bf16[32,8,128]{2,1,0:T(8,128)(2,1)S(1)}, u32[]{:S(2)}, u32[]{:S(2)}) %collective-permute-start.9) | collective-permute-done | bytes 65568 | tf_op jit(solution)/shard_map/ppermute | solution.py:671
  28.8 0.0 copy-done.1
  28.8 11.3 %backward.1 = (f32[32,128,128]{2,1,0:T(8,128)S(1)}, f32[32,128,128]{2,1,0:T(8,128)S(1)}, bf16[4,32,128]{2,1,0:T(8,128)(2,1)S(1)}, bf16[4,32,128]{2,1,0:T(8,128)(...) custom-call(bf16[32,8,128]{2,1,0:T(8,128)(2,1)S(1)} %get-tuple-element.56.refs_0_, ...), custom_call_target="tpu_custom_call" | custom-call | flops 33554432000 | bytes 20971520 | tf_op jit(solution)/shard_map/backward/pallas_call | solution.py:792
  40.0 0.1 collective-permute-start.10
  40.1 0.9 %collective-permute-start.11 = (bf16[4,32,128]{2,1,0:T(8,128)(2,1)S(1)}, bf16[4,32,128]{2,1,0:T(8,128)(2,1)S(1)}, u32[]{:S(2)}, u32[]{:S(2)}) collective-permute-start(bf16[4,32,128]{2,1,0:T(8,128)(2,1)S(1)} %get-tuple-element.79), channel_id=1, source_target_pairs={{0,2},{1,3},{2,0},{3,1},{4,6},{5,7},{6,4},{7,5},{8,10},{9,11},{10,... | collective-permute-start | bytes 98312 | tf_op jit(solution)/shard_map/ppermute | solution.py:671
  41.1 0.9 %collective-permute-start.12 = (bf16[4,32,128]{2,1,0:T(8,128)(2,1)S(1)}, bf16[4,32,128]{2,1,0:T(8,128)(2,1)S(1)}, u32[]{:S(2)}, u32[]{:S(2)}) collective-permute-start(bf16[4,32,128]{2,1,0:T(8,128)(2,1)S(1)} %get-tuple-element.80), channel_id=1, source_target_pairs={{0,3},{1,2},{2,1},{3,0},{4,7},{5,6},{6,5},{7,4},{8,11},{9,10},{10,... | collective-permute-start | bytes 98312 | tf_op jit(solution)/shard_map/ppermute | solution.py:671
  42.0 0.0 copy-start.2
  42.0 0.8 main.1.refs_4_
  42.8 0.0 collective-permute-done.10.refs_1_
  42.8 1.4 %collective-permute-done.11.refs_2_ = bf16[4,32,128]{2,1,0:T(8,128)(2,1)S(1)} collective-permute-done((bf16[4,32,128]{2,1,0:T(8,128)(2,1)S(1)}, bf16[4,32,128]{2,1,0:T(8,128)(2,1)S(1)}, u32[]{:S(2)}, u32[]{:S(2)}) %collective-permute-start.11) | collective-permute-done | bytes 32800 | tf_op jit(solution)/shard_map/ppermute | solution.py:671
  44.1 0.6 collective-permute-done.12.refs_3_
  44.7 0.0 copy-done.2
  44.7 2.2 %finish.1 = bf16[8,32,16,128]{3,2,1,0:T(8,128)(2,1)S(1)} custom-call(s32[8]{0:T(128)S(1)} %copy-done.2, bf16[4,32,128]{2,1,0:T(8,128)(2,1)S(1)} %get-tuple-element.77.refs_0_, bf16[4,32,128]{2,1,0:T(8,128)(2,1)S(1)} %collective-permute-done.10.refs_1_, bf16[4,32,128]{2,1,0:T(8,128)(2,1)S(1)} %collective-permute-done.11.refs_2_, ...), custom_call_target="tpu_custom_call" | custom-call | tf_op jit(solution)/shard_map/finish/pallas_call | solution.py:835
  47.0 31.2 %all_to_all.5 = bf16[32,8,16,128]{3,2,1,0:T(8,128)(2,1)S(1)} all-to-all(bf16[32,8,16,128]{3,2,1,0:T(8,128)(2,1)S(1)} %bitcast.18), channel_id=1, replica_groups=mesh['state'=8,'tile'=4] {'state','tile'}, dimensions={0} | all-to-all | bytes 2097152 | tf_op jit(solution)/shard_map/all_to_all | solution.py:863
  78.2 1.8 %place.1 = f32[4,16,2,16,128]{4,3,2,1,0:T(8,128)} custom-call(s32[8]{0:T(128)S(1)} %copy-done.2, bf16[8,2,16,16,128]{4,3,2,1,0:T(8,128)(2,1)S(1)} %bitcast.17), custom_call_target="tpu_custom_call" | custom-call | tf_op jit(solution)/shard_map/place/pallas_call | solution.py:876
Async XLA Ops:
  0.0 7.8 %copy-start = (bf16[1,1,64,64,128]{4,3,2,1,0:T(8,128)(2,1)S(1)}, bf16[1,1,64,64,128]{4,3,2,1,0:T(8,128)(2,1)}, u32[]{:S(2)}) copy-start(bf16[1,1,64,64,128]{4,3,2,1,0:T(8,128)(2,1)} %param.15) | copy-start | bytes 3145732
  0.0 7.8 %copy-start.3 = (f32[128]{0:T(128)S(1)}, f32[128]{0:T(128)}, u32[]{:S(2)}) copy-start(f32[128]{0:T(128)} %param.19) | copy-start | bytes 1540
  0.0 7.8 %copy-start.4 = (f32[128]{0:T(128)S(1)}, f32[128]{0:T(128)}, u32[]{:S(2)}) copy-start(f32[128]{0:T(128)} %param.18) | copy-start | bytes 1540
  1.2 6.6 %collective-permute-start.3 = (bf16[32,64,128]{2,1,0:T(8,128)(2,1)S(1)}, bf16[32,64,128]{2,1,0:T(8,128)(2,1)S(1)}, u32[]{:S(2)}, u32[]{:S(2)}) collective-permute-start(bf16[32,64,128]{2,1,0:T(8,128)(2,1)S(1)} %bitcast.27), channel_id=1, source_target_pairs={{0,1},{1,0},{2,3},{3,2},{4,5},{5,4},{6,7},{7,6},{8,9},{9,8},{10,11... | collective-permute-start | bytes 1572872 | tf_op jit(solution)/shard_map/ppermute | solution.py:609
  3.8 7.6 %collective-permute-start.2 = (f32[160,128]{1,0:T(8,128)S(1)}, f32[160,128]{1,0:T(8,128)S(1)}, u32[]{:S(2)}, u32[]{:S(2)}) collective-permute-start(f32[160,128]{1,0:T(8,128)S(1)} %bias.1.refs_0_), channel_id=1, source_target_pairs={{0,3},{1,2},{2,1},{3,0},{4,7},{5,6},{6,5},{7,4},{8,11},{9,10},{10,... | collective-permute-start | bytes 245768 | tf_op jit(solution)/shard_map/ppermute | solution.py:671
  6.5 5.0 %collective-permute-start.1 = (f32[160,128]{1,0:T(8,128)S(1)}, f32[160,128]{1,0:T(8,128)S(1)}, u32[]{:S(2)}, u32[]{:S(2)}) collective-permute-start(f32[160,128]{1,0:T(8,128)S(1)} %bias.1.refs_0_), channel_id=1, source_target_pairs={{0,2},{1,3},{2,0},{3,1},{4,6},{5,7},{6,4},{7,5},{8,10},{9,11},{10,... | collective-permute-start | bytes 245768 | tf_op jit(solution)/shard_map/ppermute | solution.py:671
  6.5 5.0 %collective-permute-start = (f32[160,128]{1,0:T(8,128)S(1)}, f32[160,128]{1,0:T(8,128)S(1)}, u32[]{:S(2)}, u32[]{:S(2)}) collective-permute-start(f32[160,128]{1,0:T(8,128)S(1)} %bias.1.refs_0_), channel_id=1, source_target_pairs={{0,1},{1,0},{2,3},{3,2},{4,5},{5,4},{6,7},{7,6},{8,9},{9,8},{10,11... | collective-permute-start | bytes 245768 | tf_op jit(solution)/shard_map/ppermute | solution.py:671
  15.7 8.7 %collective-permute-start.4 = (bf16[32,8,128]{2,1,0:T(8,128)(2,1)S(1)}, bf16[32,8,128]{2,1,0:T(8,128)(2,1)S(1)}, u32[]{:S(2)}, u32[]{:S(2)}) collective-permute-start(bf16[32,8,128]{2,1,0:T(8,128)(2,1)S(1)} %get-tuple-element.57), channel_id=1, source_target_pairs={{0,1},{1,0},{2,3},{3,2},{4,5},{5,4},{6,7},{7,6},{8,9},{9,8},{10,11... | collective-permute-start | bytes 196616 | tf_op jit(solution)/shard_map/ppermute | solution.py:671
  16.0 11.0 %collective-permute-start.5 = (bf16[32,8,128]{2,1,0:T(8,128)(2,1)S(1)}, bf16[32,8,128]{2,1,0:T(8,128)(2,1)S(1)}, u32[]{:S(2)}, u32[]{:S(2)}) collective-permute-start(bf16[32,8,128]{2,1,0:T(8,128)(2,1)S(1)} %get-tuple-element.58), channel_id=1, source_target_pairs={{0,2},{1,3},{2,0},{3,1},{4,6},{5,7},{6,4},{7,5},{8,10},{9,11},{10,... | collective-permute-start | bytes 196616 | tf_op jit(solution)/shard_map/ppermute | solution.py:671
  18.1 9.0 %collective-permute-start.6 = (bf16[32,8,128]{2,1,0:T(8,128)(2,1)S(1)}, bf16[32,8,128]{2,1,0:T(8,128)(2,1)S(1)}, u32[]{:S(2)}, u32[]{:S(2)}) collective-permute-start(bf16[32,8,128]{2,1,0:T(8,128)(2,1)S(1)} %get-tuple-element.59), channel_id=1, source_target_pairs={{0,3},{1,2},{2,1},{3,0},{4,7},{5,6},{6,5},{7,4},{8,11},{9,10},{10,... | collective-permute-start | bytes 196616 | tf_op jit(solution)/shard_map/ppermute | solution.py:671
  22.3 4.8 %collective-permute-start.7 = (bf16[32,8,128]{2,1,0:T(8,128)(2,1)S(1)}, bf16[32,8,128]{2,1,0:T(8,128)(2,1)S(1)}, u32[]{:S(2)}, u32[]{:S(2)}) collective-permute-start(bf16[32,8,128]{2,1,0:T(8,128)(2,1)S(1)} %get-tuple-element.65), channel_id=1, source_target_pairs={{0,1},{1,0},{2,3},{3,2},{4,5},{5,4},{6,7},{7,6},{8,9},{9,8},{10,11... | collective-permute-start | bytes 196616 | tf_op jit(solution)/shard_map/ppermute | solution.py:671
  22.4 4.7 %collective-permute-start.8 = (bf16[32,8,128]{2,1,0:T(8,128)(2,1)S(1)}, bf16[32,8,128]{2,1,0:T(8,128)(2,1)S(1)}, u32[]{:S(2)}, u32[]{:S(2)}) collective-permute-start(bf16[32,8,128]{2,1,0:T(8,128)(2,1)S(1)} %get-tuple-element.66), channel_id=1, source_target_pairs={{0,2},{1,3},{2,0},{3,1},{4,6},{5,7},{6,4},{7,5},{8,10},{9,11},{10,... | collective-permute-start | bytes 196616 | tf_op jit(solution)/shard_map/ppermute | solution.py:671
  24.5 4.3 %collective-permute-start.9 = (bf16[32,8,128]{2,1,0:T(8,128)(2,1)S(1)}, bf16[32,8,128]{2,1,0:T(8,128)(2,1)S(1)}, u32[]{:S(2)}, u32[]{:S(2)}) collective-permute-start(bf16[32,8,128]{2,1,0:T(8,128)(2,1)S(1)} %get-tuple-element.67), channel_id=1, source_target_pairs={{0,3},{1,2},{2,1},{3,0},{4,7},{5,6},{6,5},{7,4},{8,11},{9,10},{10,... | collective-permute-start | bytes 196616 | tf_op jit(solution)/shard_map/ppermute | solution.py:671
  24.5 4.3 %copy-start.1 = (bf16[128,128]{1,0:T(8,128)(2,1)S(1)}, bf16[128,128]{1,0:T(8,128)(2,1)}, u32[]{:S(2)}) copy-start(bf16[128,128]{1,0:T(8,128)(2,1)} %refs_16_.1) | copy-start | bytes 98308
  40.0 2.7 %collective-permute-start.10 = (bf16[4,32,128]{2,1,0:T(8,128)(2,1)S(1)}, bf16[4,32,128]{2,1,0:T(8,128)(2,1)S(1)}, u32[]{:S(2)}, u32[]{:S(2)}) collective-permute-start(bf16[4,32,128]{2,1,0:T(8,128)(2,1)S(1)} %get-tuple-element.78), channel_id=1, source_target_pairs={{0,1},{1,0},{2,3},{3,2},{4,5},{5,4},{6,7},{7,6},{8,9},{9,8},{10,11... | collective-permute-start | bytes 98312 | tf_op jit(solution)/shard_map/ppermute | solution.py:671
  40.1 4.0 %collective-permute-start.11 = (bf16[4,32,128]{2,1,0:T(8,128)(2,1)S(1)}, bf16[4,32,128]{2,1,0:T(8,128)(2,1)S(1)}, u32[]{:S(2)}, u32[]{:S(2)}) collective-permute-start(bf16[4,32,128]{2,1,0:T(8,128)(2,1)S(1)} %get-tuple-element.79), channel_id=1, source_target_pairs={{0,2},{1,3},{2,0},{3,1},{4,6},{5,7},{6,4},{7,5},{8,10},{9,11},{10,... | collective-permute-start | bytes 98312 | tf_op jit(solution)/shard_map/ppermute | solution.py:671
  41.1 3.7 %collective-permute-start.12 = (bf16[4,32,128]{2,1,0:T(8,128)(2,1)S(1)}, bf16[4,32,128]{2,1,0:T(8,128)(2,1)S(1)}, u32[]{:S(2)}, u32[]{:S(2)}) collective-permute-start(bf16[4,32,128]{2,1,0:T(8,128)(2,1)S(1)} %get-tuple-element.80), channel_id=1, source_target_pairs={{0,3},{1,2},{2,1},{3,0},{4,7},{5,6},{6,5},{7,4},{8,11},{9,10},{10,... | collective-permute-start | bytes 98312 | tf_op jit(solution)/shard_map/ppermute | solution.py:671
  42.0 2.8 %copy-start.2 = (s32[8]{0:T(128)S(1)}, s32[8]{0:T(128)}, u32[]{:S(2)}) copy-start(s32[8]{0:T(128)} %offsets.3) | copy-start | bytes 100

commit v9 on v8

--- a/solution.py
+++ b/solution.py
@@ -152,8 +152,18 @@
     loop_blocks(dzn.shape[0], one_block)
 
 
-def bias_kernel(tile, targets, lng, lnb, wpb, out, *, per_head):
+def bias_kernel(own_ref, tile, targets, lng, lnb, wpb, out, gain, shift, *sends, per_head, groups):
     step = pl.program_id(0)
+    parts = len(sends)
+    runs = per_head // BLOCK
+    gain[...] = lng[...]
+    shift[...] = lnb[...]
+    for k in range(parts):
+        owner = lax.rem(own_ref[0] + k, parts)
+        for p in range(groups):
+            run = p * parts + owner
+            first = pl.multiple_of(lax.rem(run, runs) * BLOCK, BLOCK)
+            sends[k][p * BLOCK : (p + 1) * BLOCK] = tile[run // runs, pl.ds(first, BLOCK)]
     fold, lines, side, chans = tile.shape
     pieces = [tile[f, q] for q in range(lines) for f in range(fold)]
     pair = jnp.concatenate(pieces, axis=0)
@@ -199,7 +209,7 @@
         zr.shape[0],
         lambda step: project_block(
             own,
-            [part_refs[0].at[step]] + blocks_of(part_refs[1:], step),
+            blocks_of(part_refs, step),
             (lng, lnb, w4t, w2, gbc, flat_s),
             blocks_of((zr, qt, kt, vt, kn, vn, gt), step),
         ),
@@ -594,20 +604,7 @@
     def shapes(*pairs):
         return [jax.ShapeDtypeStruct(s, t) for s, t in pairs]
 
-    tile = pair_tiles.reshape(groups, grid_side, group_rows, side, chans)
-
-    def rows_of(j):
-        return lax.dynamic_index_in_dim(tile, j, 1, keepdims=False).reshape(share, side, chans)
-
-    parts = [tile]
-    for k in range(1, grid_side):
-        perm = [
-            (i * grid_side + j, i * grid_side + (j + k) % grid_side)
-            for i in range(grid_side)
-            for j in range(grid_side)
-        ]
-        parts.append(lax.ppermute(rows_of(lax.rem(tile_j + k, grid_side)), "tile", perm))
-
+    own = tile_j.reshape(1)
     gain_row = ln_gain.reshape(1, chans)
     shift_row = ln_bias.reshape(1, chans)
     prep_shapes = shapes(
@@ -637,24 +634,33 @@
         )
     )
 
-    lines = per_head
     bias_rows = H * per_head
     target_rows = owner_rows * grid_side
-    bias_mine = pl.pallas_call(
-        functools.partial(bias_kernel, per_head=per_head),
-        grid=(per_head // lines,),
-        in_specs=[
-            pl.BlockSpec((grid_side, lines, side, chans), lambda g: (0, g, 0, 0)),
-            full((target_rows, wide)),
-            full((1, chans)),
-            full((1, chans)),
-            full((H, chans)),
-        ],
-        out_specs=full((bias_rows + target_rows, wide)),
-        out_shape=jax.ShapeDtypeStruct((bias_rows + target_rows, wide), F32),
+    bias_mine, gain_near, shift_near, *outgoing_rows = pl.pallas_call(
+        functools.partial(bias_kernel, per_head=per_head, groups=groups),
+        grid_spec=pltpu.PrefetchScalarGridSpec(
+            num_scalar_prefetch=1,
+            grid=(1,),
+            in_specs=[
+                full((grid_side, per_head, side, chans)),
+                full((target_rows, wide)),
+                full((1, chans)),
+                full((1, chans)),
+                full((H, chans)),
+            ],
+            out_specs=[full((bias_rows + target_rows, wide))]
+            + [full((1, chans))] * 2
+            + [full((share, side, chans))] * grid_side,
+        ),
+        out_shape=shapes(
+            ((bias_rows + target_rows, wide), F32),
+            *([((1, chans), F32)] * 2),
+            *([((share, side, chans), BF)] * grid_side),
+        ),
         name="bias",
         compiler_params=pltpu.CompilerParams(vmem_limit_bytes=VMEM_BYTES),
     )(
+        own,
         *map(
             stay,
             (
@@ -664,8 +670,16 @@
                 shift_row,
                 w_pairbias.T,
             ),
-        )
+        ),
     )
+    parts = [outgoing_rows[0]]
+    for k in range(1, grid_side):
+        perm = [
+            (i * grid_side + j, i * grid_side + (j + k) % grid_side)
+            for i in range(grid_side)
+            for j in range(grid_side)
+        ]
+        parts.append(lax.ppermute(outgoing_rows[k], "tile", perm))
 
     def to_partner(value, k):
         return lax.ppermute(value, "tile", [(t, t ^ k) for t in range(tiles)]) if k else value
@@ -685,12 +699,7 @@
         grid_spec=pltpu.PrefetchScalarGridSpec(
             num_scalar_prefetch=1,
             grid=(1,),
-            in_specs=[
-                pl.BlockSpec(
-                    (groups, None, group_rows, side, chans), lambda g, own: (0, own[0], 0, 0, 0)
-                )
-            ]
-            + [by_row(side, chans, rows=share)] * (grid_side - 1)
+            in_specs=[by_row(side, chans, rows=share)] * grid_side
             + [full((1, chans)), full((1, chans)), full(w4t.shape), full(w2.shape), full(gbc.shape)],
             out_specs=[by_row(wide, width, rows=share)] * 7,
             scratch_shapes=[pltpu.VMEM((group_rows * wide, chans), BF)],
@@ -699,7 +708,7 @@
         cost_estimate=cost(80 * share * cell, 12 * share * wide * width * 2),
         name="project",
         compiler_params=pltpu.CompilerParams(vmem_limit_bytes=VMEM_BYTES),
-    )(tile_j.reshape(1), *parts, gain_row, shift_row, w4t, w2, gbc)
+    )(own, *parts, gain_near, shift_near, w4t, w2, gbc)
 
     chunks = 2 if groups % 2 == 0 else 1
     chunk_groups = groups // chunks

time: 80.3 us -> 78.9 us (0.983)
  local copies, waits for them, and re-layouts: 1.18 us -> 0.01 us
    dynamic_slice x1 -> x0, local copies, waits for them, and re-layouts: 1.16 us -> none  [rows_of(): lax.dynamic_index_in_dim(tile, j, 1, keepdims=False)]
  transfers between devices with their start and end apart: 13 -> 13, of which waited for: 3 -> 3; matrix products, arithmetic and copies ran while one was open for 0% -> 0% of each run, Pallas kernels for 18% -> 16%
where the time goes in v9:
time: 78.9 us; the launch traced here: 78.6 us
  Pallas kernels  33.9 us (43%)
  blocking collectives  31.2 us (40%)
  starting transfers between devices  9.75 us (12%)
  waiting for transfers between devices  3.62 us (5%)
    all_to_all x1, blocking collectives, on_device(): lax.all_to_all(slots, ('state', 'tile'), split_axis=0, concat_axis=0, til...  31.2 us
    pallas_call x1, Pallas kernels, on_device(): pl.pallas_call(functools.partial(backward_kernel, tiles=tiles, chunks=chu...  11.2 us
    ppermute x12, starting transfers between devices, to_partner(): lax.ppermute(value, 'tile', [(t, t ^ k) for t in range(tiles)])  9.19 us
    pallas_call x2, Pallas kernels, on_device(): results = call(*inputs, *saved)  8.51 us
    ppermute x12, waiting for transfers between devices, to_partner(): lax.ppermute(value, 'tile', [(t, t ^ k) for t in range(tiles)])  3.62 us
    pallas_call x1, Pallas kernels, on_device(): pl.pallas_call(functools.partial(project_kernel, parts=grid_side), grid_s...  3.56 us
    pallas_call x1, Pallas kernels, on_device(): pl.pallas_call(middle_kernel, grid=(1,), in_specs=[pl.BlockSpec((8, wide)...  2.6 us
    pallas_call x1, Pallas kernels, on_device(): pl.pallas_call(functools.partial(finish_kernel, tiles=tiles), grid_spec=p...  2.23 us
  transfers between devices with their start and end apart: 13, of which 3 were waited for; matrix products, arithmetic and copies ran while one was open for 0% of the time, Pallas kernels for 16%

profile of v9, /device:TPU:0, one launch (start us, length us, event | category | flops | bytes accessed | tf_op | source)
XLA Modules:
  0.0 78.6 jit_solution(18017644531151766157)
XLA Ops:
  0.0 2.1 %bias.1 = (f32[160,128]{1,0:T(8,128)S(1)}, f32[1,128]{1,0:T(1,128)S(1)}, f32[1,128]{1,0:T(1,128)S(1)}, bf16[32,64,128]{2,1,0:T(8,128)(2,1)S(1)}, bf16[32,64,128]{2,1,0:T(8,128)(2,1)S(1)}) custom-call(s32[1]{0:T(128)} %bitcast.own_ref, bf16[2,32,64,128]{3,2,1,0:T(8,128)(2,1)} %bitcast.17, s32[32,128]{1,0:T(8,128)} %bitcast.20, f32[1,128]{1,0:T(1,128)} %bitcast.25, ...), custom_call_target="tpu_custom_call" | custom-call | tf_op jit(solution)/shard_map/bias/pallas_call | solution.py:639
  2.1 0.6 collective-permute-start.3
  2.7 2.6 %collective-permute-start.2 = (f32[160,128]{1,0:T(8,128)S(1)}, f32[160,128]{1,0:T(8,128)S(1)}, u32[]{:S(2)}, u32[]{:S(2)}) collective-permute-start(f32[160,128]{1,0:T(8,128)S(1)} %get-tuple-element.51.refs_0_), channel_id=1, source_target_pairs={{0,3},{1,2},{2,1},{3,0},{4,7},{5,6},{6,5},{7,4},{8,11},{9,10},{10,... | collective-permute-start | bytes 245768 | tf_op jit(solution)/shard_map/ppermute | solution.py:685
  5.3 0.0 collective-permute-start.1
  5.3 0.1 collective-permute-start
  5.4 1.1 %prep.1 = (bf16[512,128]{1,0:T(8,128)(2,1)S(1)}, bf16[128,256]{1,0:T(8,128)(2,1)S(1)}, bf16[128,128]{1,0:T(8,128)(2,1)S(1)}, bf16[128,128]{1,0:T(8,128)(2,1)S(1)}, f32[128,128]{1,0:T(8,128)S(1)}) custom-call(bf16[128,128]{1,0:T(8,128)(2,1)} %wq.3, bf16[128,128]{1,0:T(8,128)(2,1)} %wk.3, bf16[128,128]{1,0:T(8,128)(2,1)} %wv.3, bf16[128,128]{1,0:T(8,128)(2,1)} %wg.3, ...), custom_call_target="tpu_custom_call" | custom-call | tf_op jit(solution)/shard_map/prep/pallas_call | solution.py:617
  6.5 0.0 collective-permute-done.3.refs_1_
  6.5 3.6 %project.1 = (bf16[32,128,128]{2,1,0:T(8,128)(2,1)S(1)}, bf16[32,128,128]{2,1,0:T(8,128)(2,1)S(1)}, bf16[32,128,128]{2,1,0:T(8,128)(2,1)S(1)}, bf16[32,128,128]{...) custom-call(s32[1]{0:T(128)} %bitcast.own_ref, ...), custom_call_target="tpu_custom_call" | custom-call | flops 5368709120 | bytes 12582912 | tf_op jit(solution)/shard_map/project/pallas_call | solution.py:697
  10.1 0.0 collective-permute-done.2.refs_3_
  10.1 0.0 collective-permute-done.1.refs_2_
  10.1 0.0 collective-permute-done.refs_1_
  10.1 4.3 %forward.2 = (bf16[32,128,512]{2,1,0:T(8,128)(2,1)S(1)}, f32[32,128,128]{2,1,0:T(8,128)S(1)}, f32[32,64,128]{2,1,0:T(8,128)S(1)}, f32[32,128]{1,0:T(8,128)S(1)},...) custom-call(f32[160,128]{1,0:T(8,128)S(1)} %get-tuple-element.51.ref, ...), custom_call_target="tpu_custom_call" | custom-call | flops 5033164800 | bytes 7340032 | tf_op jit(solution)/shard_map/forward/pallas_call | solution.py:765
  14.4 0.4 collective-permute-start.4
  14.8 2.0 %collective-permute-start.5 = (bf16[32,8,128]{2,1,0:T(8,128)(2,1)S(1)}, bf16[32,8,128]{2,1,0:T(8,128)(2,1)S(1)}, u32[]{:S(2)}, u32[]{:S(2)}) collective-permute-start(bf16[32,8,128]{2,1,0:T(8,128)(2,1)S(1)} %get-tuple-element.68), channel_id=1, source_target_pairs={{0,2},{1,3},{2,0},{3,1},{4,6},{5,7},{6,4},{7,5},{8,10},{9,11},{10,... | collective-permute-start | bytes 196616 | tf_op jit(solution)/shard_map/ppermute | solution.py:685
  16.8 0.0 collective-permute-start.6
  16.8 4.2 %forward.3 = (bf16[32,128,512]{2,1,0:T(8,128)(2,1)S(1)}, f32[32,128,128]{2,1,0:T(8,128)S(1)}, f32[32,64,128]{2,1,0:T(8,128)S(1)}, f32[32,128]{1,0:T(8,128)S(1)},...) custom-call(f32[160,128]{1,0:T(8,128)S(1)} %get-tuple-element.51.ref, ...), custom_call_target="tpu_custom_call", output_to_operand_aliasing={{0}: (11, {}), {1}: (12, {}), {2}: (13, {}), {3}: (14, {})} | custom-call | flops 5033164800 | bytes 7340032 | tf_op jit(solution)/shard_map/forward/pallas_call | solution.py:765
  21.0 0.2 collective-permute-start.7
  21.2 2.0 %collective-permute-start.8 = (bf16[32,8,128]{2,1,0:T(8,128)(2,1)S(1)}, bf16[32,8,128]{2,1,0:T(8,128)(2,1)S(1)}, u32[]{:S(2)}, u32[]{:S(2)}) collective-permute-start(bf16[32,8,128]{2,1,0:T(8,128)(2,1)S(1)} %get-tuple-element.76), channel_id=1, source_target_pairs={{0,2},{1,3},{2,0},{3,1},{4,6},{5,7},{6,4},{7,5},{8,10},{9,11},{10,... | collective-permute-start | bytes 196616 | tf_op jit(solution)/shard_map/ppermute | solution.py:685
  23.2 0.0 collective-permute-done.4.refs_1_
  23.2 0.0 collective-permute-start.9
  23.2 0.0 copy-start
  23.2 2.6 %middle.1 = (f32[32,128,128]{2,1,0:T(8,128)S(1)}, f32[32,128]{1,0:T(8,128)S(1)}, bf16[128,192]{1,0:T(8,128)(2,1)S(1)}, bf16[128,512]{1,0:T(8,128)(2,1)S(1)}, f32...) custom-call(f32[32,128]{1,0:T(8,128)S(1)} %get-tuple-element.78.after.refs_8_, ...), custom_call_target="tpu_custom_call" | custom-call | flops 1342177280 | bytes 3145728 | tf_op jit(solution)/shard_map/middle/pallas_call | solution.py:788
  25.8 0.0 collective-permute-done.5.refs_2_
  25.8 0.0 collective-permute-done.6.refs_3_
  25.8 0.0 collective-permute-done.7.refs_5_
  25.8 0.0 collective-permute-done.8.refs_6_
  25.8 1.6 %collective-permute-done.9.refs_7_ = bf16[32,8,128]{2,1,0:T(8,128)(2,1)S(1)} collective-permute-done((bf16[32,8,128]{2,1,0:T(8,128)(2,1)S(1)}, bf16[32,8,128]{2,1,0:T(8,128)(2,1)S(1)}, u32[]{:S(2)}, u32[]{:S(2)}) %collective-permute-start.9) | collective-permute-done | bytes 65568 | tf_op jit(solution)/shard_map/ppermute | solution.py:685
  27.5 0.0 copy-done
  27.5 11.2 %backward.1 = (f32[32,128,128]{2,1,0:T(8,128)S(1)}, f32[32,128,128]{2,1,0:T(8,128)S(1)}, bf16[4,32,128]{2,1,0:T(8,128)(2,1)S(1)}, bf16[4,32,128]{2,1,0:T(8,128)(...) custom-call(bf16[32,8,128]{2,1,0:T(8,128)(2,1)S(1)} %get-tuple-element.66.refs_0_, ...), custom_call_target="tpu_custom_call" | custom-call | flops 33554432000 | bytes 20971520 | tf_op jit(solution)/shard_map/backward/pallas_call | solution.py:801
  38.7 0.1 collective-permute-start.10
  38.8 0.9 %collective-permute-start.11 = (bf16[4,32,128]{2,1,0:T(8,128)(2,1)S(1)}, bf16[4,32,128]{2,1,0:T(8,128)(2,1)S(1)}, u32[]{:S(2)}, u32[]{:S(2)}) collective-permute-start(bf16[4,32,128]{2,1,0:T(8,128)(2,1)S(1)} %get-tuple-element.89), channel_id=1, source_target_pairs={{0,2},{1,3},{2,0},{3,1},{4,6},{5,7},{6,4},{7,5},{8,10},{9,11},{10,... | collective-permute-start | bytes 98312 | tf_op jit(solution)/shard_map/ppermute | solution.py:685
  39.7 0.9 %collective-permute-start.12 = (bf16[4,32,128]{2,1,0:T(8,128)(2,1)S(1)}, bf16[4,32,128]{2,1,0:T(8,128)(2,1)S(1)}, u32[]{:S(2)}, u32[]{:S(2)}) collective-permute-start(bf16[4,32,128]{2,1,0:T(8,128)(2,1)S(1)} %get-tuple-element.90), channel_id=1, source_target_pairs={{0,3},{1,2},{2,1},{3,0},{4,7},{5,6},{6,5},{7,4},{8,11},{9,10},{10,... | collective-permute-start | bytes 98312 | tf_op jit(solution)/shard_map/ppermute | solution.py:685
  40.6 0.0 copy-start.1
  40.6 0.8 %main.1.refs_4_ = f32[32,128,128]{2,1,0:T(8,128)S(1)} custom-call(f32[32,128,128]{2,1,0:T(8,128)S(1)} %get-tuple-element.91.dpt, f32[32,128,128]{2,1,0:T(8,128)S(1)} %get-tuple-element.92.dzn, f32[32,128,128]{2,1,0:T(8,128)S(1)} %get-tuple-element.93.nrm.refs_5_, f32[32,128]{1,0:T(8,128)S(1)} %get-tuple-element.94.inv.refs_6_, ...), custom_call_target="tpu_custom_call" | custom-call | flops 1342177280 | bytes 8388608 | tf_op jit(solution)/shard_map/main/pallas_call | solution.py:832
  41.4 0.0 collective-permute-done.10.refs_1_
  41.4 1.4 %collective-permute-done.11.refs_2_ = bf16[4,32,128]{2,1,0:T(8,128)(2,1)S(1)} collective-permute-done((bf16[4,32,128]{2,1,0:T(8,128)(2,1)S(1)}, bf16[4,32,128]{2,1,0:T(8,128)(2,1)S(1)}, u32[]{:S(2)}, u32[]{:S(2)}) %collective-permute-start.11) | collective-permute-done | bytes 32800 | tf_op jit(solution)/shard_map/ppermute | solution.py:685
  42.8 0.6 collective-permute-done.12.refs_3_
  43.4 0.0 copy-done.1
  43.4 2.2 %finish.1 = bf16[8,32,16,128]{3,2,1,0:T(8,128)(2,1)S(1)} custom-call(s32[8]{0:T(128)S(1)} %copy-done.1, bf16[4,32,128]{2,1,0:T(8,128)(2,1)S(1)} %get-tuple-element.87.refs_0_, bf16[4,32,128]{2,1,0:T(8,128)(2,1)S(1)} %collective-permute-done.10.refs_1_, bf16[4,32,128]{2,1,0:T(8,128)(2,1)S(1)} %collective-permute-done.11.refs_2_, ...), custom_call_target="tpu_custom_call" | custom-call | tf_op jit(solution)/shard_map/finish/pallas_call | solution.py:844
  45.6 31.2 %all_to_all.5 = bf16[32,8,16,128]{3,2,1,0:T(8,128)(2,1)S(1)} all-to-all(bf16[32,8,16,128]{3,2,1,0:T(8,128)(2,1)S(1)} %bitcast.16), channel_id=1, replica_groups=mesh['state'=8,'tile'=4] {'state','tile'}, dimensions={0} | all-to-all | bytes 2097152 | tf_op jit(solution)/shard_map/all_to_all | solution.py:872
  76.8 1.8 %place.1 = f32[4,16,2,16,128]{4,3,2,1,0:T(8,128)} custom-call(s32[8]{0:T(128)S(1)} %copy-done.1, bf16[8,2,16,16,128]{4,3,2,1,0:T(8,128)(2,1)S(1)} %bitcast.15), custom_call_target="tpu_custom_call" | custom-call | tf_op jit(solution)/shard_map/place/pallas_call | solution.py:885
Async XLA Ops:
  2.1 4.4 %collective-permute-start.3 = (bf16[32,64,128]{2,1,0:T(8,128)(2,1)S(1)}, bf16[32,64,128]{2,1,0:T(8,128)(2,1)S(1)}, u32[]{:S(2)}, u32[]{:S(2)}) collective-permute-start(bf16[32,64,128]{2,1,0:T(8,128)(2,1)S(1)} %get-tuple-element.53), channel_id=1, source_target_pairs={{0,1},{1,0},{2,3},{3,2},{4,5},{5,4},{6,7},{7,6},{8,9},{9,8},{10,11... | collective-permute-start | bytes 1572872 | tf_op jit(solution)/shard_map/ppermute | solution.py:682
  2.7 7.4 %collective-permute-start.2 = (f32[160,128]{1,0:T(8,128)S(1)}, f32[160,128]{1,0:T(8,128)S(1)}, u32[]{:S(2)}, u32[]{:S(2)}) collective-permute-start(f32[160,128]{1,0:T(8,128)S(1)} %get-tuple-element.51.refs_0_), channel_id=1, source_target_pairs={{0,3},{1,2},{2,1},{3,0},{4,7},{5,6},{6,5},{7,4},{8,11},{9,10},{10,... | collective-permute-start | bytes 245768 | tf_op jit(solution)/shard_map/ppermute | solution.py:685
  5.3 4.8 %collective-permute-start.1 = (f32[160,128]{1,0:T(8,128)S(1)}, f32[160,128]{1,0:T(8,128)S(1)}, u32[]{:S(2)}, u32[]{:S(2)}) collective-permute-start(f32[160,128]{1,0:T(8,128)S(1)} %get-tuple-element.51.refs_0_), channel_id=1, source_target_pairs={{0,2},{1,3},{2,0},{3,1},{4,6},{5,7},{6,4},{7,5},{8,10},{9,11},{10,... | collective-permute-start | bytes 245768 | tf_op jit(solution)/shard_map/ppermute | solution.py:685
  5.3 4.8 %collective-permute-start = (f32[160,128]{1,0:T(8,128)S(1)}, f32[160,128]{1,0:T(8,128)S(1)}, u32[]{:S(2)}, u32[]{:S(2)}) collective-permute-start(f32[160,128]{1,0:T(8,128)S(1)} %get-tuple-element.51.refs_0_), channel_id=1, source_target_pairs={{0,1},{1,0},{2,3},{3,2},{4,5},{5,4},{6,7},{7,6},{8,9},{9,8},{10,11... | collective-permute-start | bytes 245768 | tf_op jit(solution)/shard_map/ppermute | solution.py:685
  14.4 8.8 %collective-permute-start.4 = (bf16[32,8,128]{2,1,0:T(8,128)(2,1)S(1)}, bf16[32,8,128]{2,1,0:T(8,128)(2,1)S(1)}, u32[]{:S(2)}, u32[]{:S(2)}) collective-permute-start(bf16[32,8,128]{2,1,0:T(8,128)(2,1)S(1)} %get-tuple-element.67), channel_id=1, source_target_pairs={{0,1},{1,0},{2,3},{3,2},{4,5},{5,4},{6,7},{7,6},{8,9},{9,8},{10,11... | collective-permute-start | bytes 196616 | tf_op jit(solution)/shard_map/ppermute | solution.py:685
  14.8 11.0 %collective-permute-start.5 = (bf16[32,8,128]{2,1,0:T(8,128)(2,1)S(1)}, bf16[32,8,128]{2,1,0:T(8,128)(2,1)S(1)}, u32[]{:S(2)}, u32[]{:S(2)}) collective-permute-start(bf16[32,8,128]{2,1,0:T(8,128)(2,1)S(1)} %get-tuple-element.68), channel_id=1, source_target_pairs={{0,2},{1,3},{2,0},{3,1},{4,6},{5,7},{6,4},{7,5},{8,10},{9,11},{10,... | collective-permute-start | bytes 196616 | tf_op jit(solution)/shard_map/ppermute | solution.py:685
  16.8 9.0 %collective-permute-start.6 = (bf16[32,8,128]{2,1,0:T(8,128)(2,1)S(1)}, bf16[32,8,128]{2,1,0:T(8,128)(2,1)S(1)}, u32[]{:S(2)}, u32[]{:S(2)}) collective-permute-start(bf16[32,8,128]{2,1,0:T(8,128)(2,1)S(1)} %get-tuple-element.69), channel_id=1, source_target_pairs={{0,3},{1,2},{2,1},{3,0},{4,7},{5,6},{6,5},{7,4},{8,11},{9,10},{10,... | collective-permute-start | bytes 196616 | tf_op jit(solution)/shard_map/ppermute | solution.py:685
  21.0 4.8 %collective-permute-start.7 = (bf16[32,8,128]{2,1,0:T(8,128)(2,1)S(1)}, bf16[32,8,128]{2,1,0:T(8,128)(2,1)S(1)}, u32[]{:S(2)}, u32[]{:S(2)}) collective-permute-start(bf16[32,8,128]{2,1,0:T(8,128)(2,1)S(1)} %get-tuple-element.75), channel_id=1, source_target_pairs={{0,1},{1,0},{2,3},{3,2},{4,5},{5,4},{6,7},{7,6},{8,9},{9,8},{10,11... | collective-permute-start | bytes 196616 | tf_op jit(solution)/shard_map/ppermute | solution.py:685
  21.2 4.6 %collective-permute-start.8 = (bf16[32,8,128]{2,1,0:T(8,128)(2,1)S(1)}, bf16[32,8,128]{2,1,0:T(8,128)(2,1)S(1)}, u32[]{:S(2)}, u32[]{:S(2)}) collective-permute-start(bf16[32,8,128]{2,1,0:T(8,128)(2,1)S(1)} %get-tuple-element.76), channel_id=1, source_target_pairs={{0,2},{1,3},{2,0},{3,1},{4,6},{5,7},{6,4},{7,5},{8,10},{9,11},{10,... | collective-permute-start | bytes 196616 | tf_op jit(solution)/shard_map/ppermute | solution.py:685
  23.2 4.3 %collective-permute-start.9 = (bf16[32,8,128]{2,1,0:T(8,128)(2,1)S(1)}, bf16[32,8,128]{2,1,0:T(8,128)(2,1)S(1)}, u32[]{:S(2)}, u32[]{:S(2)}) collective-permute-start(bf16[32,8,128]{2,1,0:T(8,128)(2,1)S(1)} %get-tuple-element.77), channel_id=1, source_target_pairs={{0,3},{1,2},{2,1},{3,0},{4,7},{5,6},{6,5},{7,4},{8,11},{9,10},{10,... | collective-permute-start | bytes 196616 | tf_op jit(solution)/shard_map/ppermute | solution.py:685
  23.2 4.3 %copy-start = (bf16[128,128]{1,0:T(8,128)(2,1)S(1)}, bf16[128,128]{1,0:T(8,128)(2,1)}, u32[]{:S(2)}) copy-start(bf16[128,128]{1,0:T(8,128)(2,1)} %refs_16_.1) | copy-start | bytes 98308
  38.7 2.7 %collective-permute-start.10 = (bf16[4,32,128]{2,1,0:T(8,128)(2,1)S(1)}, bf16[4,32,128]{2,1,0:T(8,128)(2,1)S(1)}, u32[]{:S(2)}, u32[]{:S(2)}) collective-permute-start(bf16[4,32,128]{2,1,0:T(8,128)(2,1)S(1)} %get-tuple-element.88), channel_id=1, source_target_pairs={{0,1},{1,0},{2,3},{3,2},{4,5},{5,4},{6,7},{7,6},{8,9},{9,8},{10,11... | collective-permute-start | bytes 98312 | tf_op jit(solution)/shard_map/ppermute | solution.py:685
  38.8 4.0 %collective-permute-start.11 = (bf16[4,32,128]{2,1,0:T(8,128)(2,1)S(1)}, bf16[4,32,128]{2,1,0:T(8,128)(2,1)S(1)}, u32[]{:S(2)}, u32[]{:S(2)}) collective-permute-start(bf16[4,32,128]{2,1,0:T(8,128)(2,1)S(1)} %get-tuple-element.89), channel_id=1, source_target_pairs={{0,2},{1,3},{2,0},{3,1},{4,6},{5,7},{6,4},{7,5},{8,10},{9,11},{10,... | collective-permute-start | bytes 98312 | tf_op jit(solution)/shard_map/ppermute | solution.py:685
  39.7 3.7 %collective-permute-start.12 = (bf16[4,32,128]{2,1,0:T(8,128)(2,1)S(1)}, bf16[4,32,128]{2,1,0:T(8,128)(2,1)S(1)}, u32[]{:S(2)}, u32[]{:S(2)}) collective-permute-start(bf16[4,32,128]{2,1,0:T(8,128)(2,1)S(1)} %get-tuple-element.90), channel_id=1, source_target_pairs={{0,3},{1,2},{2,1},{3,0},{4,7},{5,6},{6,5},{7,4},{8,11},{9,10},{10,... | collective-permute-start | bytes 98312 | tf_op jit(solution)/shard_map/ppermute | solution.py:685
  40.6 2.8 %copy-start.1 = (s32[8]{0:T(128)S(1)}, s32[8]{0:T(128)}, u32[]{:S(2)}) copy-start(s32[8]{0:T(128)} %offsets.3) | copy-start | bytes 100
